TPU v7x, 768 devices: a whole 4x8x12 slice. The times are simulated.
768 devices in a mesh: cell: 32 (over x, y), band: 24 (over z, core).
Axes of the slice: x: 4, y: 8, z: 12, core: 2. Of those that a mesh axis runs over, the one named last changes fastest.
Arguments:
- waves: float32 [1152, 37856], P('band', 'cell'), may hold values from -6 to 6
- cell_matrix: float32 [128, 343, 343], P('cell')
- node_map: int32 [128, 343], P('cell'), may hold values from 0 to 1182, as said below
- share_list: int32 [32, 2, 169], P('cell'), may hold values from 0 to 1182, as said below
- contacts: int32 [2, 512], P(None, 'cell'), may hold values from 0 to 127, as said below
- proj_values: float32 [512, 8, 343], P('cell'), may hold values from -0.3125 to 0.3125
- coupling: float32 [128, 8], replicated, may hold values from -1 to 1
- proj_count: int32 [128], replicated, may hold values from 1 to 8
- mass: float32 [37856], P('cell'), may hold values from 0.5 to 2
Outputs:
- filtered: float32 [1152, 37856], P('band', 'cell')
- gram: float32 [1152, 1152], P('band')
Inputs may be any that keep to these rules, and one draw needn't show every extreme that they name: `node_map`: row c holds local node numbers of partition c // 4; the nodes of a cell are distinct and every local node belongs to some cell of its partition. `share_list`: row 0 of partition q lists its local nodes that are also nodes of partition q - 1, row 1 those that are also nodes of partition q + 1, cyclically; the k-th node of row 1 of q is the same node as the k-th node of row 0 of q + 1. Within a partition the two rows are disjoint and their entries distinct. `contacts`: column e belongs to partition e // 16: row 0 is a local cell number below 4, row 1 an atom; no pair of cell and atom repeats within a partition. Each partition is home to 4 atoms, and every entry of an atom lies in its home partition or in one of the two beside it, cyclically.
All inputs are finite; a program needn't handle non-finite values.
Results may differ from a plain program's by a relative error of at most 0.0003.
Values may be sent and summed in bfloat16 or wider, within the bound.
No kernel may reach another device: no remote copies, remote signals or barrier semaphores. Data moves between devices by JAX's collectives and lax.ppermute only.
A program may use at most 32 MiB of HBM per device.

v0:
```python
import math

import jax
import jax.numpy as jnp
from jax import lax
from jax.sharding import PartitionSpec as P

PRECISE = lax.Precision.HIGHEST
CENTER = 1.0
HALF_WIDTH = 1.0
LOWEST = -0.5


def extended(block, sides, width):
    for axis, dim in sides:
        count = lax.axis_size(axis)
        forward = [(i, i + 1) for i in range(count - 1)]
        forward.append((count - 1, 0))
        backward = [(target, source) for source, target in forward]
        low = lax.ppermute(
            lax.slice_in_dim(block, block.shape[dim] - width, None, axis=dim), axis, forward
        )
        high = lax.ppermute(lax.slice_in_dim(block, 0, width, axis=dim), axis, backward)
        block = jnp.concatenate([low, block, high], axis=dim)
    return block


def filter_terms():
    sigma_now = HALF_WIDTH / (LOWEST - CENTER)
    gamma_ratio = 2.0 / sigma_now
    first_scale = sigma_now / HALF_WIDTH
    later_terms = []
    for turn_index in range(2):
        sigma_next = 1.0 / (gamma_ratio - sigma_now)
        later_terms.append((2.0 * sigma_next / HALF_WIDTH, sigma_now * sigma_next))
        sigma_now = sigma_next
    return (first_scale, later_terms)


def coeff_rim(stacked):
    return extended(stacked, (("cell", 0),), 1)


def atom_rim(stacked):
    return extended(stacked, (("cell", 0),), 1)


def reach_two(single, rim_fn):
    first = rim_fn(single[None])
    second = rim_fn(jnp.stack([first[2], first[0]]))
    return jnp.concatenate([first, second[0:1], second[3:4]], axis=0)


def operate(
    values,
    cell_matrix,
    node_map,
    share_pair,
    over_cell,
    onehot_atom,
    onehot_cell,
    proj_values,
    scales,
    near_onehot,
):
    cell_vals = values[:, node_map]
    cell_out = jnp.einsum("bcj,cij->bci", cell_vals, cell_matrix, precision=PRECISE)
    entry_vals = cell_vals[:, over_cell, :]
    coeffs = jnp.einsum("bei,epi->bep", entry_vals, proj_values, precision=PRECISE)
    near_coeffs = reach_two(coeffs, coeff_rim)
    table = jnp.einsum("kbep,kea->bap", near_coeffs, near_onehot, precision=PRECISE)
    scaled = table * scales[None]
    returned = jnp.einsum("bap,ea->bep", scaled, onehot_atom, precision=PRECISE)
    added_terms = jnp.einsum("bep,epi->bei", returned, proj_values, precision=PRECISE)
    cell_out = cell_out + jnp.einsum("bei,ec->bci", added_terms, onehot_cell, precision=PRECISE)
    assembled = jnp.zeros_like(values).at[:, node_map].add(cell_out)
    face_vals = jnp.stack([assembled[:, share_pair[0]], assembled[:, share_pair[1]]])
    padded = extended(face_vals, (("cell", 0),), 1)
    return assembled.at[:, share_pair[0]].add(padded[0]).at[:, share_pair[1]].add(padded[3])


def on_device(
    waves, cell_matrix, node_map, share_list, contacts, proj_values, coupling, proj_count, mass
):
    share_pair = share_list[0]
    over_cell = contacts[0]
    atom_count, proj_slots = coupling.shape
    atom_ids = jnp.arange(atom_count, dtype=jnp.int32)
    onehot_atom = (contacts[1][:, None] == atom_ids[None, :]).astype(jnp.float32)
    onehot_cell = (
        over_cell[:, None] == jnp.arange(cell_matrix.shape[0], dtype=jnp.int32)[None, :]
    ).astype(jnp.float32)
    levels = jnp.arange(proj_slots, dtype=jnp.int32)
    scales = coupling * (levels[None, :] < proj_count[:, None]).astype(jnp.float32)
    near_atoms = reach_two(contacts[1], atom_rim)
    near_onehot = (near_atoms[:, :, None] == atom_ids[None, None, :]).astype(jnp.float32)

    def apply_operator(values):
        return operate(
            values,
            cell_matrix,
            node_map,
            share_pair,
            over_cell,
            onehot_atom,
            onehot_cell,
            proj_values,
            scales,
            near_onehot,
        )

    first_scale, later_terms = filter_terms()
    previous = waves
    current = first_scale * (apply_operator(previous) - CENTER * previous)
    for lead_scale, back_scale in later_terms:
        upcoming = lead_scale * (apply_operator(current) - CENTER * current) - back_scale * previous
        previous, current = (current, upcoming)
    node_count = waves.shape[1]
    owned = jnp.ones((node_count,), jnp.float32).at[share_pair[0]].set(0.0)
    zed = (current * (owned * jnp.sqrt(mass))[None, :]).astype(jnp.bfloat16)
    band_rows = zed.shape[0]
    groups = lax.axis_size("band")
    my_group = lax.axis_index("band")
    contract = (((1,), (1,)), ((), ()))
    column_block = lax.dot_general(
        zed,
        lax.all_gather(zed, "band", axis=0, tiled=True),
        contract,
        preferred_element_type=jnp.float32,
    )
    gram = lax.psum(column_block, "cell") / math.sqrt(lax.axis_size("cell") * node_count)
    row_ids = my_group * band_rows + jnp.arange(band_rows, dtype=jnp.int32)
    column_ids = jnp.arange(band_rows * groups, dtype=jnp.int32)
    gram = jnp.where(row_ids[:, None] == column_ids[None, :], 0.0, gram)
    return (current, gram)


def solution(mesh):
    return jax.shard_map(
        on_device,
        mesh=mesh,
        in_specs=(
            P("band", "cell"),
            P("cell", None, None),
            P("cell", None),
            P("cell", None, None),
            P(None, "cell"),
            P("cell", None, None),
            P(),
            P(),
            P("cell"),
        ),
        out_specs=(P("band", "cell"), P("band", None)),
        check_vma=False,
    )
```

profile of v0, /device:TPU:2, one launch (start us, length us, event | category | flops | bytes accessed | tf_op | source)
XLA Modules:
  0.0 501.1 jit_solution(14092032513626581919)
XLA Ops:
  9.3 2.7 gather_fusion
  15.9 2.7 fusion.42
  18.6 3.5 collective-permute-start.4
  22.1 4.5 collective-permute-start.5
  26.6 1.9 collective-permute-start
  28.5 6.0 %collective-permute-start.1 = (s32[1,16]{1,0:T(1,128)S(1)}, s32[1,16]{1,0:T(1,128)S(1)}, u32[]{:S(2)}, u32[]{:S(2)}) collective-permute-start(s32[1,16]{1,0:T(1,128)S(1)} %get-tuple-element.16), channel_id=1, source_target_pairs={{24,0},{48,24},{72,48},{96,72},{120,96},{144,120},{168,144},{192,1... | collective-permute-start | bytes 200 | tf_op jit(solution)/shard_map/ppermute | solution.py:23
  34.7 1.9 collective-permute-start.2
  36.6 6.0 %collective-permute-start.3 = (s32[1,16]{1,0:T(1,128)S(1)}, s32[1,16]{1,0:T(1,128)S(1)}, u32[]{:S(2)}, u32[]{:S(2)}) collective-permute-start(s32[1,16]{1,0:T(1,128)S(1)} %collective-permute-done.1), channel_id=1, source_target_pairs={{24,0},{48,24},{72,48},{96,72},{120,96},{144,120},{168,144},{192,1... | collective-permute-start | bytes 200 | tf_op jit(solution)/shard_map/ppermute | solution.py:23
  44.0 1.9 collective-permute-start.6
  45.9 6.3 %collective-permute-start.7 = (f32[1,48,16,8]{1,3,2,0:T(8,128)S(1)}, f32[1,48,16,8]{1,3,2,0:T(8,128)S(1)}, u32[]{:S(2)}, u32[]{:S(2)}) collective-permute-start(f32[1,48,16,8]{1,3,2,0:T(8,128)S(1)} %collective-permute-done.5), channel_id=1, source_target_pairs={{24,0},{48,24},{72,48},{96,72},{120,96},{144,120},{168,144},{192,1... | collective-permute-start | bytes 73736 | tf_op jit(solution)/shard_map/ppermute | solution.py:23
  57.0 2.0 fusion.21
  60.2 2.0 reshape.296
  62.2 9.3 %scatter_custom_fusion = f32[48,1183]{0,1:T(8,128)S(1)} fusion(s32[1372]{0:T(1024)S(1)} %reshape.248, f32[1372,48]{1,0:T(8,128)} %reshape.296, f32[]{:T(128)} %constant.13.clone.1), kind=kCustom, calls=%fused_computation.75 | custom fusion | flops 65856 | bytes 227648 | tf_op jit(solution)/shard_map/scatter-add | solution.py:76
  74.0 2.9 collective-permute-start.8
  76.9 5.4 %collective-permute-start.9 = (f32[1,48,169]{1,2,0:T(8,128)}, f32[1,48,169]{1,2,0:T(8,128)}, u32[]{:S(2)}, u32[]{:S(2)}) collective-permute-start(f32[1,48,169]{1,2,0:T(8,128)} %bitcast.182), channel_id=1, source_target_pairs={{24,0},{48,24},{72,48},{96,72},{120,96},{144,120},{168,144},{192,1... | collective-permute-start | bytes 97352 | tf_op jit(solution)/shard_map/ppermute | solution.py:23
  83.2 2.0 scatter_custom_fusion.1
  85.2 2.2 scatter_custom_fusion.2
  88.4 4.7 gather_fusion.4
  93.1 2.1 copy.93
  95.2 1.9 reshape.139
  97.1 1.7 copy.169
  98.8 2.7 gather_fusion.5
  101.5 2.6 fusion.45
  104.1 2.4 collective-permute-start.10
  106.5 5.6 %collective-permute-start.11 = (f32[1,48,16,8]{1,3,2,0:T(8,128)S(1)}, f32[1,48,16,8]{1,3,2,0:T(8,128)S(1)}, u32[]{:S(2)}, u32[]{:S(2)}) collective-permute-start(f32[1,48,16,8]{1,3,2,0:T(8,128)S(1)} %fusion.45), channel_id=1, source_target_pairs={{24,0},{48,24},{72,48},{96,72},{120,96},{144,120},{168,144},{192,1... | collective-permute-start | bytes 73736 | tf_op jit(solution)/shard_map/ppermute | solution.py:23
  112.4 1.9 collective-permute-start.12
  114.4 6.0 %collective-permute-start.13 = (f32[1,48,16,8]{1,3,2,0:T(8,128)S(1)}, f32[1,48,16,8]{1,3,2,0:T(8,128)S(1)}, u32[]{:S(2)}, u32[]{:S(2)}) collective-permute-start(f32[1,48,16,8]{1,3,2,0:T(8,128)S(1)} %collective-permute-done.11), channel_id=1, source_target_pairs={{24,0},{48,24},{72,48},{96,72},{120,96},{144,120},{168,144},{192,1... | collective-permute-start | bytes 73736 | tf_op jit(solution)/shard_map/ppermute | solution.py:23
  125.2 2.8 fusion.27
  127.9 2.1 copy.118
  130.0 2.0 reshape.297
  132.0 10.0 %scatter_custom_fusion.3 = f32[48,1183]{0,1:T(8,128)} fusion(s32[1372]{0:T(1024)S(1)} %reshape.248, f32[1372,48]{1,0:T(8,128)} %reshape.297, f32[]{:T(128)} %constant.13.clone.1), kind=kCustom, calls=%fused_computation.73 | custom fusion | flops 65856 | bytes 227648 | tf_op jit(solution)/shard_map/scatter-add | solution.py:76
  142.0 2.3 gather_fusion.7
  144.3 2.3 gather_fusion.6
  146.7 1.9 collective-permute-start.14
  148.6 6.4 %collective-permute-start.15 = (f32[1,48,169]{1,2,0:T(8,128)}, f32[1,48,169]{1,2,0:T(8,128)}, u32[]{:S(2)}, u32[]{:S(2)}) collective-permute-start(f32[1,48,169]{1,2,0:T(8,128)} %bitcast.183), channel_id=1, source_target_pairs={{24,0},{48,24},{72,48},{96,72},{120,96},{144,120},{168,144},{192,1... | collective-permute-start | bytes 97352 | tf_op jit(solution)/shard_map/ppermute | solution.py:23
  155.9 3.6 scatter_custom_fusion.4
  159.5 3.6 scatter_custom_fusion.5
  163.1 2.1 multiply_subtract_fusion.1
  165.2 4.7 gather_fusion.8
  169.9 2.1 copy.103
  171.9 1.9 reshape.171
  173.8 1.7 copy.168
  175.5 2.7 gather_fusion.9
  178.3 3.3 fusion.48
  181.5 1.9 collective-permute-start.16
  185.3 6.0 %collective-permute-start.17 = (f32[1,48,16,8]{1,3,2,0:T(8,128)}, f32[1,48,16,8]{1,3,2,0:T(8,128)S(1)}, u32[]{:S(2)}, u32[]{:S(2)}) collective-permute-start(f32[1,48,16,8]{1,3,2,0:T(8,128)} %fusion.48), channel_id=1, source_target_pairs={{24,0},{48,24},{72,48},{96,72},{120,96},{144,120},{168,144},{192,1... | collective-permute-start | bytes 73736 | tf_op jit(solution)/shard_map/ppermute | solution.py:23
  193.1 1.9 collective-permute-start.18
  195.0 6.0 %collective-permute-start.19 = (f32[1,48,16,8]{1,3,2,0:T(8,128)S(1)}, f32[1,48,16,8]{1,3,2,0:T(8,128)S(1)}, u32[]{:S(2)}, u32[]{:S(2)}) collective-permute-start(f32[1,48,16,8]{1,3,2,0:T(8,128)S(1)} %collective-permute-done.17), channel_id=1, source_target_pairs={{24,0},{48,24},{72,48},{96,72},{120,96},{144,120},{168,144},{192,1... | collective-permute-start | bytes 73736 | tf_op jit(solution)/shard_map/ppermute | solution.py:23
  206.4 2.8 fusion.33
  209.2 2.1 copy.119
  211.3 2.0 reshape.298
  213.3 10.0 %scatter_custom_fusion.6 = f32[48,1183]{0,1:T(8,128)} fusion(s32[1372]{0:T(1024)S(1)} %reshape.248, f32[1372,48]{1,0:T(8,128)} %reshape.298, f32[]{:T(128)} %constant.13.clone.1), kind=kCustom, calls=%fused_computation.71 | custom fusion | flops 65856 | bytes 227648 | tf_op jit(solution)/shard_map/scatter-add | solution.py:76
  223.3 2.3 gather_fusion.11
  225.6 2.3 gather_fusion.10
  228.0 1.9 collective-permute-start.20
  229.9 6.4 %collective-permute-start.21 = (f32[1,48,169]{1,2,0:T(8,128)}, f32[1,48,169]{1,2,0:T(8,128)S(1)}, u32[]{:S(2)}, u32[]{:S(2)}) collective-permute-start(f32[1,48,169]{1,2,0:T(8,128)} %bitcast.181), channel_id=1, source_target_pairs={{24,0},{48,24},{72,48},{96,72},{120,96},{144,120},{168,144},{192,1... | collective-permute-start | bytes 97352 | tf_op jit(solution)/shard_map/ppermute | solution.py:23
  237.0 3.4 scatter_custom_fusion.7
  240.4 3.4 scatter_custom_fusion.8
  243.8 2.5 multiply_convert_fusion
  246.3 1.8 copy.112
  248.1 77.0 %all-gather.2.cloned.1.call-done = bf16[1152,1183]{1,0:T(8,128)(2,1)} async-done(((bf16[48,1183]{1,0:T(8,128)(2,1)}), bf16[1152,1183]{1,0:T(8,128)(2,1)}) %all-gather.2.cloned.1.call-update) | async-done | bytes 2725648 | tf_op jit(solution)/shard_map/all_gather | solution.py:127
  325.1 3.6 fusion.97
  329.7 162.8 %all-reduce.2.cloned.1.call-done = f32[48,1152]{1,0:T(8,128)} async-done(((f32[48,1152]{1,0:T(8,128)}), f32[48,1152]{1,0:T(8,128)}) %all-reduce.2.cloned.1.call-update) | async-done | bytes 221200 | tf_op jit(solution)/shard_map/psum | solution.py:131
  492.5 1.7 multiply_select_fusion
  (107 shorter events, 34.1 us)
Async XLA Ops:
  7.2 49.8 %copy-start = (f32[4,343,343]{2,0,1:T(4,128)S(1)}, f32[4,343,343]{2,0,1:T(4,128)}, u32[]{:S(2)}) copy-start(f32[4,343,343]{2,0,1:T(4,128)} %param.10) | copy-start | bytes 5647156
  7.2 318.0 %all-gather.2.cloned.1.call-start = ((), (), s32[]{:S(2)}) async-start(), calls=%async_computation | async-start | bytes 3072000 | tf_op jit(solution)/shard_map/all_gather | solution.py:127
  12.0 2.2 copy-start.13
  14.2 1.7 copy-start.8
  14.2 1.7 copy-start.1
  15.9 18.6 %copy-start.12 = (s32[1,2,169]{2,1,0:T(2,128)S(1)}, s32[1,2,169]{2,1,0:T(2,128)}, u32[]{:S(2)}) copy-start(s32[1,2,169]{2,1,0:T(2,128)} %param.12) | copy-start | bytes 4060
  15.9 18.7 %copy-start.9 = (f32[128,8]{0,1:T(8,128)S(1)}, f32[128,8]{0,1:T(8,128)}, u32[]{:S(2)}) copy-start(f32[128,8]{0,1:T(8,128)} %param.15) | copy-start | bytes 12292
  15.9 18.7 %copy-start.14 = (s32[128]{0:T(128)S(1)}, s32[128]{0:T(128)}, u32[]{:S(2)}) copy-start(s32[128]{0:T(128)} %param.16) | copy-start | bytes 1540
  18.6 25.3 %collective-permute-start.4 = (f32[1,48,16,8]{1,3,2,0:T(8,128)S(1)}, f32[1,48,16,8]{1,3,2,0:T(8,128)S(1)}, u32[]{:S(2)}, u32[]{:S(2)}) collective-permute-start(f32[1,48,16,8]{1,3,2,0:T(8,128)S(1)} %fusion.42), channel_id=1, source_target_pairs={{0,24},{24,48},{48,72},{72,96},{96,120},{120,144},{144,168},{168,1... | collective-permute-start | bytes 73736 | tf_op jit(solution)/shard_map/ppermute | solution.py:20
  22.1 23.8 %collective-permute-start.5 = (f32[1,48,16,8]{1,3,2,0:T(8,128)S(1)}, f32[1,48,16,8]{1,3,2,0:T(8,128)S(1)}, u32[]{:S(2)}, u32[]{:S(2)}) collective-permute-start(f32[1,48,16,8]{1,3,2,0:T(8,128)S(1)} %fusion.42), channel_id=1, source_target_pairs={{24,0},{48,24},{72,48},{96,72},{120,96},{144,120},{168,144},{192,1... | collective-permute-start | bytes 73736 | tf_op jit(solution)/shard_map/ppermute | solution.py:23
  26.6 29.6 %copy-start.5 = (s32[16]{0:T(128)}, s32[16]{0:T(128)S(1)}, u32[]{:S(2)}) copy-start(s32[16]{0:T(128)S(1)} %get-tuple-element.15) | copy-start | bytes 196
  26.6 8.1 %collective-permute-start = (s32[1,16]{1,0:T(1,128)S(1)}, s32[1,16]{1,0:T(1,128)S(1)}, u32[]{:S(2)}, u32[]{:S(2)}) collective-permute-start(s32[1,16]{1,0:T(1,128)S(1)} %get-tuple-element.16), channel_id=1, source_target_pairs={{0,24},{24,48},{48,72},{72,96},{96,120},{120,144},{144,168},{168,1... | collective-permute-start | bytes 200 | tf_op jit(solution)/shard_map/ppermute | solution.py:20
  28.5 8.1 %collective-permute-start.1 = (s32[1,16]{1,0:T(1,128)S(1)}, s32[1,16]{1,0:T(1,128)S(1)}, u32[]{:S(2)}, u32[]{:S(2)}) collective-permute-start(s32[1,16]{1,0:T(1,128)S(1)} %get-tuple-element.16), channel_id=1, source_target_pairs={{24,0},{48,24},{72,48},{96,72},{120,96},{144,120},{168,144},{192,1... | collective-permute-start | bytes 200 | tf_op jit(solution)/shard_map/ppermute | solution.py:23
  34.6 21.5 %copy-start.10 = (s32[169,1]{0,1:T(1,128)}, s32[169,1]{0,1:T(1,128)S(1)}, u32[]{:S(2)}) copy-start(s32[169,1]{0,1:T(1,128)S(1)} %get-tuple-element.12) | copy-start | bytes 2032
  34.6 21.5 %copy-start.11 = (s32[169,1]{0,1:T(1,128)}, s32[169,1]{0,1:T(1,128)S(1)}, u32[]{:S(2)}) copy-start(s32[169,1]{0,1:T(1,128)S(1)} %get-tuple-element.13) | copy-start | bytes 2032
  34.7 8.0 %collective-permute-start.2 = (s32[1,16]{1,0:T(1,128)S(1)}, s32[1,16]{1,0:T(1,128)S(1)}, u32[]{:S(2)}, u32[]{:S(2)}) collective-permute-start(s32[1,16]{1,0:T(1,128)S(1)} %collective-permute-done), channel_id=1, source_target_pairs={{0,24},{24,48},{48,72},{72,96},{96,120},{120,144},{144,168},{168,1... | collective-permute-start | bytes 200 | tf_op jit(solution)/shard_map/ppermute | solution.py:20
  36.6 7.3 %collective-permute-start.3 = (s32[1,16]{1,0:T(1,128)S(1)}, s32[1,16]{1,0:T(1,128)S(1)}, u32[]{:S(2)}, u32[]{:S(2)}) collective-permute-start(s32[1,16]{1,0:T(1,128)S(1)} %collective-permute-done.1), channel_id=1, source_target_pairs={{24,0},{48,24},{72,48},{96,72},{120,96},{144,120},{168,144},{192,1... | collective-permute-start | bytes 200 | tf_op jit(solution)/shard_map/ppermute | solution.py:23
  44.0 8.5 %collective-permute-start.6 = (f32[1,48,16,8]{1,3,2,0:T(8,128)S(1)}, f32[1,48,16,8]{1,3,2,0:T(8,128)S(1)}, u32[]{:S(2)}, u32[]{:S(2)}) collective-permute-start(f32[1,48,16,8]{1,3,2,0:T(8,128)S(1)} %collective-permute-done.4), channel_id=1, source_target_pairs={{0,24},{24,48},{48,72},{72,96},{96,120},{120,144},{144,168},{168,1... | collective-permute-start | bytes 73736 | tf_op jit(solution)/shard_map/ppermute | solution.py:20
  45.9 8.2 %collective-permute-start.7 = (f32[1,48,16,8]{1,3,2,0:T(8,128)S(1)}, f32[1,48,16,8]{1,3,2,0:T(8,128)S(1)}, u32[]{:S(2)}, u32[]{:S(2)}) collective-permute-start(f32[1,48,16,8]{1,3,2,0:T(8,128)S(1)} %collective-permute-done.5), channel_id=1, source_target_pairs={{24,0},{48,24},{72,48},{96,72},{120,96},{144,120},{168,144},{192,1... | collective-permute-start | bytes 73736 | tf_op jit(solution)/shard_map/ppermute | solution.py:23
  74.0 9.2 %collective-permute-start.8 = (f32[1,48,169]{1,2,0:T(8,128)}, f32[1,48,169]{1,2,0:T(8,128)}, u32[]{:S(2)}, u32[]{:S(2)}) collective-permute-start(f32[1,48,169]{1,2,0:T(8,128)} %bitcast.184), channel_id=1, source_target_pairs={{0,24},{24,48},{48,72},{72,96},{96,120},{120,144},{144,168},{168,1... | collective-permute-start | bytes 97352 | tf_op jit(solution)/shard_map/ppermute | solution.py:20
  76.9 8.3 %collective-permute-start.9 = (f32[1,48,169]{1,2,0:T(8,128)}, f32[1,48,169]{1,2,0:T(8,128)}, u32[]{:S(2)}, u32[]{:S(2)}) collective-permute-start(f32[1,48,169]{1,2,0:T(8,128)} %bitcast.182), channel_id=1, source_target_pairs={{24,0},{48,24},{72,48},{96,72},{120,96},{144,120},{168,144},{192,1... | collective-permute-start | bytes 97352 | tf_op jit(solution)/shard_map/ppermute | solution.py:23
  101.5 21.3 %copy-start.6 = (s32[16]{0:T(128)S(1)}, s32[16]{0:T(128)}, u32[]{:S(2)}) copy-start(s32[16]{0:T(128)} %copy-done.5) | copy-start | bytes 196
  104.1 8.3 %collective-permute-start.10 = (f32[1,48,16,8]{1,3,2,0:T(8,128)S(1)}, f32[1,48,16,8]{1,3,2,0:T(8,128)S(1)}, u32[]{:S(2)}, u32[]{:S(2)}) collective-permute-start(f32[1,48,16,8]{1,3,2,0:T(8,128)S(1)} %fusion.45), channel_id=1, source_target_pairs={{0,24},{24,48},{48,72},{72,96},{96,120},{120,144},{144,168},{168,1... | collective-permute-start | bytes 73736 | tf_op jit(solution)/shard_map/ppermute | solution.py:20
  106.5 7.9 %collective-permute-start.11 = (f32[1,48,16,8]{1,3,2,0:T(8,128)S(1)}, f32[1,48,16,8]{1,3,2,0:T(8,128)S(1)}, u32[]{:S(2)}, u32[]{:S(2)}) collective-permute-start(f32[1,48,16,8]{1,3,2,0:T(8,128)S(1)} %fusion.45), channel_id=1, source_target_pairs={{24,0},{48,24},{72,48},{96,72},{120,96},{144,120},{168,144},{192,1... | collective-permute-start | bytes 73736 | tf_op jit(solution)/shard_map/ppermute | solution.py:23
  112.4 8.3 %collective-permute-start.12 = (f32[1,48,16,8]{1,3,2,0:T(8,128)S(1)}, f32[1,48,16,8]{1,3,2,0:T(8,128)S(1)}, u32[]{:S(2)}, u32[]{:S(2)}) collective-permute-start(f32[1,48,16,8]{1,3,2,0:T(8,128)S(1)} %collective-permute-done.10), channel_id=1, source_target_pairs={{0,24},{24,48},{48,72},{72,96},{96,120},{120,144},{144,168},{168,1... | collective-permute-start | bytes 73736 | tf_op jit(solution)/shard_map/ppermute | solution.py:20
  114.4 7.9 %collective-permute-start.13 = (f32[1,48,16,8]{1,3,2,0:T(8,128)S(1)}, f32[1,48,16,8]{1,3,2,0:T(8,128)S(1)}, u32[]{:S(2)}, u32[]{:S(2)}) collective-permute-start(f32[1,48,16,8]{1,3,2,0:T(8,128)S(1)} %collective-permute-done.11), channel_id=1, source_target_pairs={{24,0},{48,24},{72,48},{96,72},{120,96},{144,120},{168,144},{192,1... | collective-permute-start | bytes 73736 | tf_op jit(solution)/shard_map/ppermute | solution.py:23
  123.2 2.0 copy-start.3
  146.7 9.2 %collective-permute-start.14 = (f32[1,48,169]{1,2,0:T(8,128)}, f32[1,48,169]{1,2,0:T(8,128)}, u32[]{:S(2)}, u32[]{:S(2)}) collective-permute-start(f32[1,48,169]{1,2,0:T(8,128)} %bitcast.185), channel_id=1, source_target_pairs={{0,24},{24,48},{48,72},{72,96},{96,120},{120,144},{144,168},{168,1... | collective-permute-start | bytes 97352 | tf_op jit(solution)/shard_map/ppermute | solution.py:20
  148.6 10.9 %collective-permute-start.15 = (f32[1,48,169]{1,2,0:T(8,128)}, f32[1,48,169]{1,2,0:T(8,128)}, u32[]{:S(2)}, u32[]{:S(2)}) collective-permute-start(f32[1,48,169]{1,2,0:T(8,128)} %bitcast.183), channel_id=1, source_target_pairs={{24,0},{48,24},{72,48},{96,72},{120,96},{144,120},{168,144},{192,1... | collective-permute-start | bytes 97352 | tf_op jit(solution)/shard_map/ppermute | solution.py:23
  181.5 9.8 %collective-permute-start.16 = (f32[1,48,16,8]{1,3,2,0:T(8,128)}, f32[1,48,16,8]{1,3,2,0:T(8,128)}, u32[]{:S(2)}, u32[]{:S(2)}) collective-permute-start(f32[1,48,16,8]{1,3,2,0:T(8,128)} %fusion.48), channel_id=1, source_target_pairs={{0,24},{24,48},{48,72},{72,96},{96,120},{120,144},{144,168},{168,1... | collective-permute-start | bytes 73736 | tf_op jit(solution)/shard_map/ppermute | solution.py:20
  185.3 9.7 %collective-permute-start.17 = (f32[1,48,16,8]{1,3,2,0:T(8,128)}, f32[1,48,16,8]{1,3,2,0:T(8,128)S(1)}, u32[]{:S(2)}, u32[]{:S(2)}) collective-permute-start(f32[1,48,16,8]{1,3,2,0:T(8,128)} %fusion.48), channel_id=1, source_target_pairs={{24,0},{48,24},{72,48},{96,72},{120,96},{144,120},{168,144},{192,1... | collective-permute-start | bytes 73736 | tf_op jit(solution)/shard_map/ppermute | solution.py:23
  193.1 8.5 %collective-permute-start.18 = (f32[1,48,16,8]{1,3,2,0:T(8,128)}, f32[1,48,16,8]{1,3,2,0:T(8,128)S(1)}, u32[]{:S(2)}, u32[]{:S(2)}) collective-permute-start(f32[1,48,16,8]{1,3,2,0:T(8,128)} %collective-permute-done.16), channel_id=1, source_target_pairs={{0,24},{24,48},{48,72},{72,96},{96,120},{120,144},{144,168},{168,1... | collective-permute-start | bytes 73736 | tf_op jit(solution)/shard_map/ppermute | solution.py:20
  195.0 7.9 %collective-permute-start.19 = (f32[1,48,16,8]{1,3,2,0:T(8,128)S(1)}, f32[1,48,16,8]{1,3,2,0:T(8,128)S(1)}, u32[]{:S(2)}, u32[]{:S(2)}) collective-permute-start(f32[1,48,16,8]{1,3,2,0:T(8,128)S(1)} %collective-permute-done.17), channel_id=1, source_target_pairs={{24,0},{48,24},{72,48},{96,72},{120,96},{144,120},{168,144},{192,1... | collective-permute-start | bytes 73736 | tf_op jit(solution)/shard_map/ppermute | solution.py:23
  204.4 2.0 copy-start.2
  211.3 25.0 %copy-start.7 = (f32[1183]{0:T(1024)S(1)}, f32[1183]{0:T(1024)}, u32[]{:S(2)}) copy-start(f32[1183]{0:T(1024)} %param.17) | copy-start | bytes 14200
  228.0 9.1 %collective-permute-start.20 = (f32[1,48,169]{1,2,0:T(8,128)}, f32[1,48,169]{1,2,0:T(8,128)S(1)}, u32[]{:S(2)}, u32[]{:S(2)}) collective-permute-start(f32[1,48,169]{1,2,0:T(8,128)} %bitcast.61), channel_id=1, source_target_pairs={{0,24},{24,48},{48,72},{72,96},{96,120},{120,144},{144,168},{168,1... | collective-permute-start | bytes 97352 | tf_op jit(solution)/shard_map/ppermute | solution.py:20
  229.9 10.5 %collective-permute-start.21 = (f32[1,48,169]{1,2,0:T(8,128)}, f32[1,48,169]{1,2,0:T(8,128)S(1)}, u32[]{:S(2)}, u32[]{:S(2)}) collective-permute-start(f32[1,48,169]{1,2,0:T(8,128)} %bitcast.181), channel_id=1, source_target_pairs={{24,0},{48,24},{72,48},{96,72},{120,96},{144,120},{168,144},{192,1... | collective-permute-start | bytes 97352 | tf_op jit(solution)/shard_map/ppermute | solution.py:23
  248.0 80.8 %copy-start.4 = (f32[48,1183]{0,1:T(8,128)S(1)}, f32[48,1183]{0,1:T(8,128)}, u32[]{:S(2)}) copy-start(f32[48,1183]{0,1:T(8,128)} %get-tuple-element.11) | copy-start | bytes 681412
  248.0 244.5 %all-reduce.2.cloned.1.call-start = ((), (), s32[]{:S(2)}) async-start(), calls=%async_computation.1 | async-start | bytes 442368 | tf_op jit(solution)/shard_map/psum | solution.py:131
Sparse Core Ops, SparseCore 0:
  248.2 76.9 all-gather.1
  329.2 163.2 all-reduce.1
where the time goes:
time: 503 us; the launch traced here: 501 us
  waiting for transfers between devices  250 us (50%)
  starting transfers between devices  88.8 us (18%)
  local copies, waits for them, and re-layouts  63.6 us (13%)
  other arithmetic  55.4 us (11%)
  matrix products  29 us (6%)
  between operations  14.7 us (3%)
    psum x1, waiting for transfers between devices, on_device(): lax.psum(column_block, 'cell')  163 us
    all_gather x1, waiting for transfers between devices, on_device(): lax.all_gather(zed, 'band', axis=0, tiled=True)  77 us
    ppermute x11, starting transfers between devices, extended(): lax.ppermute(lax.slice_in_dim(block, 0, width, axis=dim), axis, backward)  64.6 us
    scatter-add x3, other arithmetic, operate(): assembled = jnp.zeros_like(values).at[:, node_map].add(cell_out)  29.2 us
    gather x12, local copies, waits for them, and re-layouts, operate(): cell_vals = values[:, node_map]  25.5 us
    ppermute x11, starting transfers between devices, extended(): lax.ppermute(lax.slice_in_dim(block, block.shape[dim] - width, None, axis...  24.1 us
    scatter-add x6, other arithmetic, operate(): assembled.at[:, share_pair[0]].add(padded[0]).at[:, share_pair[1]]  18.2 us
    add x6, local copies, waits for them, and re-layouts, operate(): cell_out + jnp.einsum('bei,ec->bci', added_terms, onehot_cell, precision=...  11.3 us
  transfers between devices with their start and end apart: 24, of which 13 were waited for; matrix products, arithmetic and copies ran while one was open for 3% of the time, Pallas kernels for 0%

commit v1 on v0

v1 whole, which is shorter than its diff:
```python
import functools
import math

import jax
import jax.numpy as jnp
from jax import lax
from jax.experimental import pallas as pl
from jax.experimental.pallas import tpu as pltpu
from jax.sharding import PartitionSpec as P

CENTER = 1.0
HALF_WIDTH = 1.0
LOWEST = -0.5
F32 = jnp.float32
BF16 = jnp.bfloat16


def filter_terms():
    sigma_now = HALF_WIDTH / (LOWEST - CENTER)
    gamma_ratio = 2.0 / sigma_now
    first_scale = sigma_now / HALF_WIDTH
    later_terms = []
    for turn_index in range(2):
        sigma_next = 1.0 / (gamma_ratio - sigma_now)
        later_terms.append((2.0 * sigma_next / HALF_WIDTH, sigma_now * sigma_next))
        sigma_now = sigma_next
    return (first_scale, later_terms)


def up(value, step):
    return (value + step - 1) // step * step


def split3(x):
    high = x.astype(BF16)
    rest = x - high.astype(F32)
    mid = rest.astype(BF16)
    low = (rest - mid.astype(F32)).astype(BF16)
    return high, mid, low


def nn(a, b):
    return lax.dot_general(a, b, (((1,), (0,)), ((), ())), preferred_element_type=F32)


def nt(a, b):
    return lax.dot_general(a, b, (((1,), (1,)), ((), ())), preferred_element_type=F32)


def pick(x, table, dot):
    rows = x.shape[0]
    out = dot(jnp.concatenate(split3(x), axis=0), table)
    return out[:rows] + (out[rows : 2 * rows] + out[2 * rows :])


def full(x, parts, dot):
    rows = x.shape[0]
    high, mid, low = split3(x)
    first = dot(jnp.concatenate([high, mid, low], axis=0), parts[0])
    second = dot(jnp.concatenate([high, mid], axis=0), parts[1])
    third = dot(high, parts[2])
    small = (first[2 * rows :] + second[rows:]) + third
    return first[:rows] + ((first[rows : 2 * rows] + second[:rows]) + small)


def column(row, lanes=128):
    return jnp.broadcast_to(row, (lanes, row.shape[1])).T


def hot(mask):
    return jnp.where(mask, 1.0, 0.0).astype(BF16)


def message(coeffs, atoms):
    return jnp.concatenate([coeffs, jnp.broadcast_to(atoms, (8, atoms.shape[1]))], axis=0)


def enter_kernel(waves, node_map, proj, cells, atoms, x_out, msg_out, parts_out, wide, ids, pad):
    bands, nodes = waves.shape
    ncell, cnodes = node_map.shape
    entries = proj.shape[0]
    width = up(cnodes, 128)
    ids[...] = jnp.full(ids.shape, -1.0, F32)
    for c in range(ncell):
        ids[0:1, c * width : c * width + cnodes] = node_map[c : c + 1, :].astype(F32)
    wide[...] = jnp.zeros(wide.shape, F32)
    wide[:, :nodes] = waves[...]
    place = lax.broadcasted_iota(jnp.int32, (wide.shape[1], ids.shape[1]), 0).astype(F32)
    x = pick(wide[...], hot(place == ids[0:1, :]), nn)
    x_out[...] = x
    pad[...] = jnp.zeros(pad.shape, F32)
    pad[:, :cnodes] = proj[...]
    cell_column = column(cells[...])
    block = pad[...]
    spread = []
    for c in range(ncell):
        for t in range(width // 128):
            keep = cell_column == float(c)
            spread.append(jnp.where(keep, block[:, t * 128 : (t + 1) * 128], 0.0))
    parts = split3(jnp.concatenate(spread, axis=1))
    for k in range(3):
        parts_out[k] = parts[k]
    msg_out[...] = message(full(x, parts, nt), atoms[...])


def table_kernel(node_map, share, parity, matrix, w_out, s_out, m_out, weight_out, ids, face, pad):
    ncell, cnodes = node_map.shape
    faces = share.shape[2]
    width = up(cnodes, 128)
    span = up(faces, 128)
    ids[...] = jnp.full(ids.shape, -1.0, F32)
    for c in range(ncell):
        ids[0:1, c * width : c * width + cnodes] = node_map[c : c + 1, :].astype(F32)
    face[...] = jnp.full(face.shape, -2.0, F32)
    low = share[0, 0:1, :].astype(F32)
    high = share[0, 1:2, :].astype(F32)
    even = parity[...] == 0
    face[0:1, 0:faces] = jnp.where(even, high, low)
    face[0:1, span : span + faces] = jnp.where(even, low, high)
    total = ncell * width
    id_row = ids[0:1, :]
    face_row = face[0:1, :]
    id_column = column(id_row)
    face_column = column(face_row)
    count = jnp.zeros((1, total), F32)
    for t in range(total // 128):
        same = id_column == id_row[:, t * 128 : (t + 1) * 128]
        w_out[:, t * 128 : (t + 1) * 128] = hot(same)
    for t in range(2 * span // 128):
        w_out[:, total + t * 128 : total + (t + 1) * 128] = hot(
            id_column == face_row[:, t * 128 : (t + 1) * 128]
        )
    for t in range(total // 128):
        s_out[:, t * 128 : (t + 1) * 128] = hot(
            face_column == id_row[:, t * 128 : (t + 1) * 128]
        )
    count = nn(jnp.ones((16, total), BF16), w_out[:, :total])
    weight_out[...] = 1.0 / jnp.maximum(count[0:8], 1.0)
    for c in range(ncell):
        pad[...] = jnp.zeros(pad.shape, F32)
        pad[:cnodes, :cnodes] = matrix[c]
        parts = split3(pad[...])
        for k in range(3):
            m_out[k, c] = parts[k]


def cell_kernel(x, m, o_out):
    ncell = m.shape[1]
    width = m.shape[2]
    for c in range(ncell):
        o_out[:, c * width : (c + 1) * width] = full(
            x[:, c * width : (c + 1) * width], [m[k, c] for k in range(3)], nt
        )


def gather_kernel(o, own, m1, m2, m3, m4, atoms, scales, parts, w, v_out, a_out, b_out):
    bands = o.shape[0]
    entries = own.shape[1]
    slots = 8
    atom_column = column(atoms[...])
    row = lax.broadcasted_iota(jnp.int32, (entries, entries), 0)
    col = lax.broadcasted_iota(jnp.int32, (entries, entries), 1)
    same_slot = (row & (slots - 1)) == (col & (slots - 1))
    total = jnp.zeros((bands, entries), F32)
    for near in (own, m1, m2, m3, m4):
        table = hot((atom_column == near[bands : bands + 1, :]) & same_slot)
        total = total + pick(near[:bands, :], table, nt)
    atom_of = lax.broadcasted_iota(jnp.int32, scales.shape, 0).astype(F32)
    scale_row = jnp.sum(
        jnp.where(atom_of == atoms[...], scales[...], 0.0), axis=0, keepdims=True
    )
    returned = total * scale_row
    out = o[...] + full(returned, [parts[k] for k in range(3)], nn)
    spread = pick(out, w[...], nn)
    cells = o.shape[1]
    span = (w.shape[1] - cells) // 2
    v_out[...] = spread[:, :cells]
    a_out[...] = spread[:, cells : cells + span]
    b_out[...] = spread[:, cells + span :]


def step_kernel(lead, back, v, from_a, from_b, s, now, before, parts, atoms, x_out, msg_out):
    incoming = jnp.concatenate([from_a[...], from_b[...]], axis=1)
    operated = v[...] + pick(incoming, s[...], nn)
    x = lead * (operated - CENTER * now[...])
    if back:
        x = x - back * before[...]
    x_out[...] = x
    msg_out[...] = message(full(x, [parts[k] for k in range(3)], nt), atoms[...])


def leave_kernel(
    lead, back, v, from_a, from_b, s, now, before, weight, node_map, share, mass, y_out, z_out, ids
):
    ncell, cnodes = node_map.shape
    bands, nodes = y_out.shape
    width = up(cnodes, 128)
    incoming = jnp.concatenate([from_a[...], from_b[...]], axis=1)
    operated = v[...] + pick(incoming, s[...], nn)
    x = lead * (operated - CENTER * now[...]) - back * before[...]
    ids[...] = jnp.full(ids.shape, -1.0, F32)
    for c in range(ncell):
        ids[0:1, c * width : c * width + cnodes] = node_map[c : c + 1, :].astype(F32)
    whole = up(nodes, 128)
    id_column = column(ids[0:1, :])
    tables = []
    for t in range(whole // 128):
        lane = lax.broadcasted_iota(jnp.int32, (ids.shape[1], 128), 1) + t * 128
        tables.append(hot(id_column == lane.astype(F32)))
    y = pick(x * weight[0:1, :], jnp.concatenate(tables, axis=1), nn)[:, :nodes]
    y_out[...] = y
    low_column = column(share[0, 0:1, :].astype(F32))[:, 0:1]
    lane = lax.broadcasted_iota(jnp.int32, (low_column.shape[0], nodes), 1).astype(F32)
    shared = jnp.max(jnp.where(low_column == lane, 1.0, 0.0), axis=0, keepdims=True)
    z_out[...] = (y * ((1.0 - shared) * jnp.sqrt(mass[...]))).astype(BF16)


def gram_kernel(z, everything, out):
    product = nt(z[...], everything[...])
    across = product.shape[1] // 128
    used = 0
    for r in range(product.shape[0] // 8):
        for c in range(across):
            out[used : used + 8, :] = product[8 * r : 8 * r + 8, 128 * c : 128 * c + 128]
            used += 8
    out[used:, :] = jnp.zeros((out.shape[0] - used, 128), F32)


def sum_kernel(groups, x, out):
    rows = x.shape[0] // groups
    total = x[0:rows, :]
    for k in range(1, groups):
        total = total + x[k * rows : (k + 1) * rows, :]
    for k in range(groups):
        out[k * rows : (k + 1) * rows, :] = total


def finish_kernel(scale, x, first_row, out):
    across = out.shape[1] // 128
    used = 0
    start = first_row[0, 0]
    for r in range(out.shape[0] // 8):
        for c in range(across):
            row = lax.broadcasted_iota(jnp.int32, (8, 128), 0) + (8 * r + start)
            col = lax.broadcasted_iota(jnp.int32, (8, 128), 1) + 128 * c
            out[8 * r : 8 * r + 8, 128 * c : 128 * c + 128] = jnp.where(
                row == col, 0.0, x[used : used + 8, :] / scale
            )
            used += 8


def call(body, outs, scratch=(), smem=()):
    def run(*args):
        specs = [
            pl.BlockSpec(memory_space=pltpu.SMEM if k in smem else pltpu.VMEM)
            for k in range(len(args))
        ]
        return pl.pallas_call(
            body,
            out_shape=[jax.ShapeDtypeStruct(shape, kind) for shape, kind in outs],
            in_specs=specs,
            out_specs=[pl.BlockSpec(memory_space=pltpu.VMEM) for _ in outs],
            scratch_shapes=[pltpu.VMEM(shape, kind) for shape, kind in scratch],
        )(*args)

    return run


def swap(x, stride, inner):
    count = lax.axis_size("cell")
    pairs = []
    for q in range(count):
        ahead = (q // stride) % 2 == (0 if inner else 1)
        pairs.append((q, (q + stride if ahead else q - stride) % count))
    return lax.ppermute(x, "cell", pairs)


def on_device(
    waves, cell_matrix, node_map, share_list, contacts, proj_values, coupling, proj_count, mass
):
    bands, nodes = waves.shape
    ncell, cnodes = node_map.shape
    faces = share_list.shape[2]
    entries, slots = proj_values.shape[:2]
    width = up(cnodes, 128)
    total = ncell * width
    whole = up(nodes, 128)
    span = up(faces, 128)
    flat = entries * slots
    parity = jnp.broadcast_to(lax.axis_index("cell") % 2, (1, 1)).astype(jnp.int32)
    contact_rows = jnp.repeat(contacts, slots, axis=1).astype(F32)
    cells = contact_rows[0:1]
    atoms = contact_rows[1:2]
    levels = jnp.arange(slots, dtype=jnp.int32)
    scales = coupling * (levels[None, :] < proj_count[:, None]).astype(F32)
    scales = jnp.tile(scales, (1, entries))
    proj = proj_values.reshape(flat, cnodes)

    x0, msg, parts = call(
        enter_kernel,
        [((bands, total), F32), ((bands + 8, flat), F32), ((3, flat, total), BF16)],
        [((bands, whole), F32), ((8, total), F32), ((flat, width), F32)],
    )(waves, node_map, proj, cells, atoms)
    w, s, m, weight = call(
        table_kernel,
        [
            ((total, total + 2 * span), BF16),
            ((2 * span, total), BF16),
            ((3, ncell, width, width), BF16),
            ((8, total), F32),
        ],
        [((8, total), F32), ((8, 2 * span), F32), ((width, width), F32)],
    )(node_map, share_list, parity, cell_matrix)

    first_scale, later_terms = filter_terms()
    terms = [(first_scale, 0.0)] + later_terms
    before = x0
    now = x0
    for turn, (lead, back) in enumerate(terms):
        near = [swap(msg, 1, True), swap(msg, 2, True), swap(msg, 1, False), swap(msg, 2, False)]
        (o,) = call(cell_kernel, [((bands, total), F32)])(now, m)
        v, to_a, to_b = call(
            gather_kernel,
            [((bands, total), F32), ((bands, span), F32), ((bands, span), F32)],
        )(o, msg, *near, atoms, scales, parts, w)
        from_a = swap(to_a, 1, True)
        from_b = swap(to_b, 1, False)
        if turn < len(terms) - 1:
            x, msg = call(
                functools.partial(step_kernel, lead, back),
                [((bands, total), F32), ((bands + 8, flat), F32)],
            )(v, from_a, from_b, s, now, before, parts, atoms)
            before, now = now, x
    filtered, zed = call(
        functools.partial(leave_kernel, lead, back),
        [((bands, nodes), F32), ((bands, nodes), BF16)],
        [((8, total), F32)],
    )(v, from_a, from_b, s, now, before, weight, node_map, share_list, mass[None, :])

    groups = lax.axis_size("band")
    count = lax.axis_size("cell")
    everything = lax.all_gather(zed, "band", axis=0, tiled=True)
    tiles = bands // 8 * (bands * groups // 128)
    rows = 8 * up(tiles, count)
    (partial,) = call(gram_kernel, [((rows, 128), F32)])(zed, everything)
    pieces = lax.all_to_all(partial, "cell", 0, 0, tiled=True)
    (summed,) = call(functools.partial(sum_kernel, count), [((rows, 128), F32)])(pieces)
    result = lax.all_to_all(summed, "cell", 0, 0, tiled=True)
    first_row = jnp.broadcast_to(lax.axis_index("band") * bands, (1, 1)).astype(jnp.int32)
    (gram,) = call(
        functools.partial(finish_kernel, math.sqrt(count * nodes)),
        [((bands, bands * groups), F32)],
        smem=(1,),
    )(result, first_row)
    return (filtered, gram)


def solution(mesh):
    return jax.shard_map(
        on_device,
        mesh=mesh,
        in_specs=(
            P("band", "cell"),
            P("cell", None, None),
            P("cell", None),
            P("cell", None, None),
            P(None, "cell"),
            P("cell", None, None),
            P(),
            P(),
            P("cell"),
        ),
        out_specs=(P("band", "cell"), P("band", None)),
        check_vma=False,
    )
```

time: 503 us -> 275 us (0.55)
  the two profiles are of different devices: /device:TPU:2 before, /device:TPU:8 now
where the time goes in v1:
time: 275 us; the launch traced here: 274 us
  waiting for transfers between devices  86.4 us (31%)
  starting transfers between devices  77.2 us (28%)
  Pallas kernels  61.3 us (22%)
  blocking collectives  22.6 us (8%)
  between operations  14.4 us (5%)
  local copies, waits for them, and re-layouts  10.7 us (4%)
    ppermute x18, starting transfers between devices, swap(): return lax.ppermute(x, 'cell', pairs)  72.6 us
    all_gather x1, waiting for transfers between devices, on_device(): everything = lax.all_gather(zed, 'band', axis=0, tiled=True)  63.6 us
    pallas_call x14, Pallas kernels, run(): pl.pallas_call(body, out_shape=[jax.ShapeDtypeStruct(shape, kind) for sha...  61.3 us
    all_to_all x1, blocking collectives, on_device(): pieces = lax.all_to_all(partial, 'cell', 0, 0, tiled=True)  22.6 us
    all_to_all x1, waiting for transfers between devices, on_device(): result = lax.all_to_all(summed, 'cell', 0, 0, tiled=True)  12 us
    ppermute x18, waiting for transfers between devices, swap(): return lax.ppermute(x, 'cell', pairs)  10.8 us
    unnamed x41, local copies, waits for them, and re-layouts  7.95 us
  transfers between devices with their start and end apart: 20, of which 10 were waited for; matrix products, arithmetic and copies ran while one was open for 2% of the time, Pallas kernels for 8%

profile of v1, /device:TPU:8, one launch (start us, length us, event | category | flops | bytes accessed | tf_op | source)
XLA Modules:
  0.0 273.9 jit_solution(15816709629232663885)
XLA Ops:
  7.2 0.0 all-gather.2.cloned.1.call-start
  7.2 0.7 convert_element_type.6
  7.9 0.1 broadcast_in_dim.17
  8.0 0.6 slice.23.atoms
  8.6 0.1 broadcast_in_dim.16
  8.7 0.6 slice.20.cells
  9.3 3.9 %shard_map.104 = (f32[48,1536]{1,0:T(8,128)}, f32[56,128]{1,0:T(8,128)}, bf16[3,128,1536]{2,1,0:T(8,128)(2,1)}) custom-call(f32[48,1183]{1,0:T(8,128)} %waves.1, s32[4,343]{1,0:T(4,128)} %node_map.5, f32[128,343]{1,0:T(8,128)} %bitcast.17, f32[1,128]{1,0:T(1,128)} %slice.20.cells, f32[1,128]{1,0:T(1,128)} %slice.23.atoms), custom_call_target="tpu_custom_call" | custom-call | tf_op jit(solution)/shard_map/pallas_call | solution.py:258
  13.1 11.3 %collective-permute-start = (f32[56,128]{1,0:T(8,128)}, f32[56,128]{1,0:T(8,128)S(1)}, u32[]{:S(2)}, u32[]{:S(2)}) collective-permute-start(f32[56,128]{1,0:T(8,128)} %get-tuple-element.26.own), channel_id=1, source_target_pairs={{0,24},{24,0},{48,72},{72,48},{96,120},{120,96},{144,168},{168,144... | collective-permute-start | bytes 86024 | tf_op jit(solution)/shard_map/ppermute | solution.py:275
  24.5 1.9 collective-permute-start.1
  26.4 3.4 %collective-permute-start.2 = (f32[56,128]{1,0:T(8,128)}, f32[56,128]{1,0:T(8,128)S(1)}, u32[]{:S(2)}, u32[]{:S(2)}) collective-permute-start(f32[56,128]{1,0:T(8,128)} %get-tuple-element.26.own), channel_id=1, source_target_pairs={{0,744},{24,48},{48,24},{72,96},{96,72},{120,144},{144,120},{168,1... | collective-permute-start | bytes 86024 | tf_op jit(solution)/shard_map/ppermute | solution.py:275
  29.8 5.2 %collective-permute-start.3 = (f32[56,128]{1,0:T(8,128)}, f32[56,128]{1,0:T(8,128)S(1)}, u32[]{:S(2)}, u32[]{:S(2)}) collective-permute-start(f32[56,128]{1,0:T(8,128)} %get-tuple-element.26.own), channel_id=1, source_target_pairs={{0,720},{24,744},{48,96},{72,120},{96,48},{120,72},{144,192},{168,... | collective-permute-start | bytes 86024 | tf_op jit(solution)/shard_map/ppermute | solution.py:275
  35.0 0.7 fusion
  35.7 3.1 %copy.13.matrix = f32[4,343,343]{2,1,0:T(8,128)} copy(f32[4,343,343]{2,0,1:T(4,128)} %param.10) | data formatting | bytes 3764768 | tf_op args[1]
  38.8 0.7 copy.14.scales
  39.5 8.6 %shard_map.105 = (bf16[1536,2048]{1,0:T(8,128)(2,1)}, bf16[512,1536]{1,0:T(8,128)(2,1)}, bf16[3,4,384,384]{3,2,1,0:T(8,128)(2,1)}, f32[8,1536]{1,0:T(8,128)}) custom-call(s32[4,343]{1,0:T(4,128)} %node_map.5, s32[1,2,169]{2,1,0:T(2,128)} %share.3, s32[1,1]{1,0:T(1,128)} %bitcast.3.parity, f32[4,343,343]{2,1,0:T(8,128)} %copy.13.matrix), custom_call_target="tpu_custom_call" | custom-call | tf_op jit(solution)/shard_map/pallas_call | solution.py:258
  48.1 4.1 %shard_map.106.o = f32[48,1536]{1,0:T(8,128)} custom-call(f32[48,1536]{1,0:T(8,128)} %get-tuple-element.24.x.now.before, bf16[3,4,384,384]{3,2,1,0:T(8,128)(2,1)} %get-tuple-element.25.m), custom_call_target="tpu_custom_call" | custom-call | tf_op jit(solution)/shard_map/pallas_call | solution.py:258
  52.3 0.5 copy-done.7
  52.8 0.0 copy-done.10
  52.9 6.1 %shard_map.107 = (f32[48,1536]{1,0:T(8,128)}, f32[48,256]{1,0:T(8,128)}, f32[48,256]{1,0:T(8,128)}) custom-call(f32[48,1536]{1,0:T(8,128)} %shard_map.106.o, f32[56,128]{1,0:T(8,128)} %get-tuple-element.26.own, f32[56,128]{1,0:T(8,128)} %copy-done.7, f32[56,128]{1,0:T(8,128)} %copy-done.8, f32[56,128]{1,0:T(8,128)} %copy-done.9, f32[56,128]{1,0:T(8,128)} %copy-done.10, ...), custom_call_target="tpu_custom_call" | custom-call | tf_op jit(solution)/shard_map/pallas_call | solution.py:258
  59.0 1.9 collective-permute-start.4
  60.9 3.3 %collective-permute-start.5 = (f32[48,256]{1,0:T(8,128)}, f32[48,256]{1,0:T(8,128)S(1)}, u32[]{:S(2)}, u32[]{:S(2)}) collective-permute-start(f32[48,256]{1,0:T(8,128)} %get-tuple-element.31), channel_id=1, source_target_pairs={{0,744},{24,48},{48,24},{72,96},{96,72},{120,144},{144,120},{168,1... | collective-permute-start | bytes 147464 | tf_op jit(solution)/shard_map/ppermute | solution.py:275
  64.2 1.0 collective-permute-done.4.from_a
  65.2 1.9 collective-permute-done.5.from_b
  67.1 0.6 copy-done.4
  67.7 3.8 %shard_map.108 = (f32[48,1536]{1,0:T(8,128)}, f32[56,128]{1,0:T(8,128)}) custom-call(f32[48,1536]{1,0:T(8,128)} %get-tuple-element.29.v, f32[48,256]{1,0:T(8,128)} %copy-done.2, f32[48,256]{1,0:T(8,128)} %copy-done.4, bf16[512,1536]{1,0:T(8,128)(2,1)} %get-tuple-element.32.s, f32[48,1536]{1,0:T(8,128)} %get-tuple-element.24.x.now.before, ...), custom_call_target="tpu_custom_call" | custom-call | tf_op jit(solution)/shard_map/pallas_call | solution.py:258
  71.5 7.2 %collective-permute-start.6 = (f32[56,128]{1,0:T(8,128)}, f32[56,128]{1,0:T(8,128)S(1)}, u32[]{:S(2)}, u32[]{:S(2)}) collective-permute-start(f32[56,128]{1,0:T(8,128)} %get-tuple-element.34.own), channel_id=1, source_target_pairs={{0,24},{24,0},{48,72},{72,48},{96,120},{120,96},{144,168},{168,144... | collective-permute-start | bytes 86024 | tf_op jit(solution)/shard_map/ppermute | solution.py:275
  78.8 1.9 collective-permute-start.7
  80.7 3.4 %collective-permute-start.8 = (f32[56,128]{1,0:T(8,128)}, f32[56,128]{1,0:T(8,128)S(1)}, u32[]{:S(2)}, u32[]{:S(2)}) collective-permute-start(f32[56,128]{1,0:T(8,128)} %get-tuple-element.34.own), channel_id=1, source_target_pairs={{0,744},{24,48},{48,24},{72,96},{96,72},{120,144},{144,120},{168,1... | collective-permute-start | bytes 86024 | tf_op jit(solution)/shard_map/ppermute | solution.py:275
  84.1 5.9 %collective-permute-start.9 = (f32[56,128]{1,0:T(8,128)}, f32[56,128]{1,0:T(8,128)S(1)}, u32[]{:S(2)}, u32[]{:S(2)}) collective-permute-start(f32[56,128]{1,0:T(8,128)} %get-tuple-element.34.own), channel_id=1, source_target_pairs={{0,720},{24,744},{48,96},{72,120},{96,48},{120,72},{144,192},{168,... | collective-permute-start | bytes 86024 | tf_op jit(solution)/shard_map/ppermute | solution.py:275
  90.0 4.1 %shard_map.109.o = f32[48,1536]{1,0:T(8,128)} custom-call(f32[48,1536]{1,0:T(8,128)} %get-tuple-element.33.x.now.before, bf16[3,4,384,384]{3,2,1,0:T(8,128)(2,1)} %get-tuple-element.25.m), custom_call_target="tpu_custom_call" | custom-call | tf_op jit(solution)/shard_map/pallas_call | solution.py:258
  94.2 0.1 collective-permute-done.9.m4
  94.3 0.5 copy-done.13
  94.8 0.6 copy-done.18
  95.4 6.1 %shard_map.110 = (f32[48,1536]{1,0:T(8,128)}, f32[48,256]{1,0:T(8,128)}, f32[48,256]{1,0:T(8,128)}) custom-call(f32[48,1536]{1,0:T(8,128)} %shard_map.109.o, f32[56,128]{1,0:T(8,128)} %get-tuple-element.34.own, f32[56,128]{1,0:T(8,128)} %copy-done.13, f32[56,128]{1,0:T(8,128)} %copy-done.15, f32[56,128]{1,0:T(8,128)} %copy-done.17, f32[56,128]{1,0:T(8,128)} %copy-done.18, ...), custom_call_target="tpu_custom_call" | custom-call | tf_op jit(solution)/shard_map/pallas_call | solution.py:258
  101.5 1.9 collective-permute-start.10
  103.4 2.7 %collective-permute-start.11 = (f32[48,256]{1,0:T(8,128)}, f32[48,256]{1,0:T(8,128)S(1)}, u32[]{:S(2)}, u32[]{:S(2)}) collective-permute-start(f32[48,256]{1,0:T(8,128)} %get-tuple-element.37), channel_id=1, source_target_pairs={{0,744},{24,48},{48,24},{72,96},{96,72},{120,144},{144,120},{168,1... | collective-permute-start | bytes 147464 | tf_op jit(solution)/shard_map/ppermute | solution.py:275
  106.2 1.5 collective-permute-done.10.from_a
  107.7 1.9 collective-permute-done.11.from_b
  109.6 0.6 copy-done.3
  110.2 3.8 %shard_map.111 = (f32[48,1536]{1,0:T(8,128)}, f32[56,128]{1,0:T(8,128)}) custom-call(f32[48,1536]{1,0:T(8,128)} %get-tuple-element.35.v, f32[48,256]{1,0:T(8,128)} %copy-done.1, f32[48,256]{1,0:T(8,128)} %copy-done.3, bf16[512,1536]{1,0:T(8,128)(2,1)} %get-tuple-element.32.s, f32[48,1536]{1,0:T(8,128)} %get-tuple-element.33.x.now.before, ...), custom_call_target="tpu_custom_call" | custom-call | tf_op jit(solution)/shard_map/pallas_call | solution.py:258
  114.0 7.2 %collective-permute-start.12 = (f32[56,128]{1,0:T(8,128)}, f32[56,128]{1,0:T(8,128)S(1)}, u32[]{:S(2)}, u32[]{:S(2)}) collective-permute-start(f32[56,128]{1,0:T(8,128)} %get-tuple-element.39.own), channel_id=1, source_target_pairs={{0,24},{24,0},{48,72},{72,48},{96,120},{120,96},{144,168},{168,144... | collective-permute-start | bytes 86024 | tf_op jit(solution)/shard_map/ppermute | solution.py:275
  121.3 1.9 collective-permute-start.13
  123.2 3.4 %collective-permute-start.14 = (f32[56,128]{1,0:T(8,128)}, f32[56,128]{1,0:T(8,128)S(1)}, u32[]{:S(2)}, u32[]{:S(2)}) collective-permute-start(f32[56,128]{1,0:T(8,128)} %get-tuple-element.39.own), channel_id=1, source_target_pairs={{0,744},{24,48},{48,24},{72,96},{96,72},{120,144},{144,120},{168,1... | collective-permute-start | bytes 86024 | tf_op jit(solution)/shard_map/ppermute | solution.py:275
  126.6 5.2 %collective-permute-start.15 = (f32[56,128]{1,0:T(8,128)}, f32[56,128]{1,0:T(8,128)S(1)}, u32[]{:S(2)}, u32[]{:S(2)}) collective-permute-start(f32[56,128]{1,0:T(8,128)} %get-tuple-element.39.own), channel_id=1, source_target_pairs={{0,720},{24,744},{48,96},{72,120},{96,48},{120,72},{144,192},{168,... | collective-permute-start | bytes 86024 | tf_op jit(solution)/shard_map/ppermute | solution.py:275
  131.8 4.1 %shard_map.112.o = f32[48,1536]{1,0:T(8,128)} custom-call(f32[48,1536]{1,0:T(8,128)} %get-tuple-element.38.x.now, bf16[3,4,384,384]{3,2,1,0:T(8,128)(2,1)} %get-tuple-element.25.m), custom_call_target="tpu_custom_call" | custom-call | tf_op jit(solution)/shard_map/pallas_call | solution.py:258
  136.0 1.1 collective-permute-done.15.m4
  137.1 0.6 copy-done.16
  137.7 6.1 %shard_map.113 = (f32[48,1536]{1,0:T(8,128)}, f32[48,256]{1,0:T(8,128)}, f32[48,256]{1,0:T(8,128)}) custom-call(f32[48,1536]{1,0:T(8,128)} %shard_map.112.o, f32[56,128]{1,0:T(8,128)} %get-tuple-element.39.own, f32[56,128]{1,0:T(8,128)} %copy-done.11, f32[56,128]{1,0:T(8,128)} %copy-done.12, f32[56,128]{1,0:T(8,128)} %copy-done.14, f32[56,128]{1,0:T(8,128)} %copy-done.16, ...), custom_call_target="tpu_custom_call" | custom-call | tf_op jit(solution)/shard_map/pallas_call | solution.py:258
  143.8 2.3 collective-permute-start.16
  146.1 2.4 collective-permute-start.17
  148.5 0.6 broadcast_in_dim.19.mass
  149.1 0.9 collective-permute-done.16.from_a
  150.0 2.3 collective-permute-done.17.from_b
  152.3 0.6 copy-done.6
  152.9 3.6 %shard_map.114 = (f32[48,1183]{1,0:T(8,128)}, bf16[48,1183]{1,0:T(8,128)(2,1)}) custom-call(f32[48,1536]{1,0:T(8,128)} %get-tuple-element.40.v, f32[48,256]{1,0:T(8,128)} %copy-done.5, f32[48,256]{1,0:T(8,128)} %copy-done.6, bf16[512,1536]{1,0:T(8,128)(2,1)} %get-tuple-element.32.s, f32[48,1536]{1,0:T(8,128)} %get-tuple-element.38.x.now, ...), custom_call_target="tpu_custom_call" | custom-call | tf_op jit(solution)/shard_map/pallas_call | solution.py:258
  156.5 0.0 all-gather.2.cloned.1.call-update
  156.5 63.6 %all-gather.2.cloned.1.call-done.everything = bf16[1152,1183]{1,0:T(8,128)(2,1)} async-done(((bf16[48,1183]{1,0:T(8,128)(2,1)}), bf16[1152,1183]{1,0:T(8,128)(2,1)}) %all-gather.2.cloned.1.call-update) | async-done | bytes 2725648 | tf_op jit(solution)/shard_map/all_gather | solution.py:342
  220.2 3.6 %shard_map.115 = f32[512,128]{1,0:T(8,128)} custom-call(bf16[48,1183]{1,0:T(8,128)(2,1)} %get-tuple-element.45.z, bf16[1152,1183]{1,0:T(8,128)(2,1)} %all-gather.2.cloned.1.call-done.everything), custom_call_target="tpu_custom_call" | custom-call | tf_op jit(solution)/shard_map/pallas_call | solution.py:258
  223.7 22.6 %all_to_all.22 = f32[32,16,128]{2,1,0:T(8,128)} all-to-all(f32[32,16,128]{2,1,0:T(8,128)} %bitcast.13), channel_id=1, replica_groups=mesh['cell'=32,'band'=24] {'cell'}, dimensions={0} | all-to-all | bytes 524288 | tf_op jit(solution)/shard_map/all_to_all | solution.py:346
  246.3 1.7 shard_map.116
  248.0 4.6 %all-to-all-start.1 = ((f32[32,16,128]{2,1,0:T(8,128)}), f32[32,16,128]{2,1,0:T(8,128)S(1)}, u32[]{:S(2)}, u32[]{:S(2)}) async-start(f32[32,16,128]{2,1,0:T(8,128)} %bitcast.15), calls=%async_computation.1 | async-start | bytes 524288 | tf_op jit(solution)/shard_map/all_to_all | solution.py:348
  252.6 12.0 %all-to-all-done.1 = f32[32,16,128]{2,1,0:T(8,128)S(1)} async-done(((f32[32,16,128]{2,1,0:T(8,128)}), f32[32,16,128]{2,1,0:T(8,128)S(1)}, u32[]{:S(2)}, u32[]{:S(2)}) %all-to-all-start.1) | async-done | bytes 262176 | tf_op jit(solution)/shard_map/all_to_all | solution.py:348
  264.7 0.7 copy-done
  265.4 1.7 shard_map.117
  (43 shorter events, 0.1 us)
Async XLA Ops:
  7.2 213.0 %all-gather.2.cloned.1.call-start = ((), (), s32[]{:S(2)}) async-start(), calls=%async_computation.2 | async-start | bytes 3072000 | tf_op jit(solution)/shard_map/all_gather | solution.py:342
  13.1 39.1 %collective-permute-start = (f32[56,128]{1,0:T(8,128)}, f32[56,128]{1,0:T(8,128)S(1)}, u32[]{:S(2)}, u32[]{:S(2)}) collective-permute-start(f32[56,128]{1,0:T(8,128)} %get-tuple-element.26.own), channel_id=1, source_target_pairs={{0,24},{24,0},{48,72},{72,48},{96,120},{120,96},{144,168},{168,144... | collective-permute-start | bytes 86024 | tf_op jit(solution)/shard_map/ppermute | solution.py:275
  24.5 27.8 %collective-permute-start.1 = (f32[56,128]{1,0:T(8,128)}, f32[56,128]{1,0:T(8,128)S(1)}, u32[]{:S(2)}, u32[]{:S(2)}) collective-permute-start(f32[56,128]{1,0:T(8,128)} %get-tuple-element.26.own), channel_id=1, source_target_pairs={{0,48},{24,72},{48,0},{72,24},{96,144},{120,168},{144,96},{168,120... | collective-permute-start | bytes 86024 | tf_op jit(solution)/shard_map/ppermute | solution.py:275
  26.4 25.8 %collective-permute-start.2 = (f32[56,128]{1,0:T(8,128)}, f32[56,128]{1,0:T(8,128)S(1)}, u32[]{:S(2)}, u32[]{:S(2)}) collective-permute-start(f32[56,128]{1,0:T(8,128)} %get-tuple-element.26.own), channel_id=1, source_target_pairs={{0,744},{24,48},{48,24},{72,96},{96,72},{120,144},{144,120},{168,1... | collective-permute-start | bytes 86024 | tf_op jit(solution)/shard_map/ppermute | solution.py:275
  29.8 22.5 %collective-permute-start.3 = (f32[56,128]{1,0:T(8,128)}, f32[56,128]{1,0:T(8,128)S(1)}, u32[]{:S(2)}, u32[]{:S(2)}) collective-permute-start(f32[56,128]{1,0:T(8,128)} %get-tuple-element.26.own), channel_id=1, source_target_pairs={{0,720},{24,744},{48,96},{72,120},{96,48},{120,72},{144,192},{168,... | collective-permute-start | bytes 86024 | tf_op jit(solution)/shard_map/ppermute | solution.py:275
  52.2 0.6 copy-start.7
  52.2 0.6 copy-start.8
  52.2 0.6 copy-start.9
  52.3 0.6 copy-start.10
  59.0 6.2 %collective-permute-start.4 = (f32[48,256]{1,0:T(8,128)}, f32[48,256]{1,0:T(8,128)S(1)}, u32[]{:S(2)}, u32[]{:S(2)}) collective-permute-start(f32[48,256]{1,0:T(8,128)} %get-tuple-element.30), channel_id=1, source_target_pairs={{0,24},{24,0},{48,72},{72,48},{96,120},{120,96},{144,168},{168,144... | collective-permute-start | bytes 147464 | tf_op jit(solution)/shard_map/ppermute | solution.py:275
  60.9 6.2 %collective-permute-start.5 = (f32[48,256]{1,0:T(8,128)}, f32[48,256]{1,0:T(8,128)S(1)}, u32[]{:S(2)}, u32[]{:S(2)}) collective-permute-start(f32[48,256]{1,0:T(8,128)} %get-tuple-element.31), channel_id=1, source_target_pairs={{0,744},{24,48},{48,24},{72,96},{96,72},{120,144},{144,120},{168,1... | collective-permute-start | bytes 147464 | tf_op jit(solution)/shard_map/ppermute | solution.py:275
  65.2 1.9 copy-start.2
  67.1 0.6 copy-start.4
  71.5 22.6 %collective-permute-start.6 = (f32[56,128]{1,0:T(8,128)}, f32[56,128]{1,0:T(8,128)S(1)}, u32[]{:S(2)}, u32[]{:S(2)}) collective-permute-start(f32[56,128]{1,0:T(8,128)} %get-tuple-element.34.own), channel_id=1, source_target_pairs={{0,24},{24,0},{48,72},{72,48},{96,120},{120,96},{144,168},{168,144... | collective-permute-start | bytes 86024 | tf_op jit(solution)/shard_map/ppermute | solution.py:275
  78.8 15.4 %collective-permute-start.7 = (f32[56,128]{1,0:T(8,128)}, f32[56,128]{1,0:T(8,128)S(1)}, u32[]{:S(2)}, u32[]{:S(2)}) collective-permute-start(f32[56,128]{1,0:T(8,128)} %get-tuple-element.34.own), channel_id=1, source_target_pairs={{0,48},{24,72},{48,0},{72,24},{96,144},{120,168},{144,96},{168,120... | collective-permute-start | bytes 86024 | tf_op jit(solution)/shard_map/ppermute | solution.py:275
  80.7 13.5 %collective-permute-start.8 = (f32[56,128]{1,0:T(8,128)}, f32[56,128]{1,0:T(8,128)S(1)}, u32[]{:S(2)}, u32[]{:S(2)}) collective-permute-start(f32[56,128]{1,0:T(8,128)} %get-tuple-element.34.own), channel_id=1, source_target_pairs={{0,744},{24,48},{48,24},{72,96},{96,72},{120,144},{144,120},{168,1... | collective-permute-start | bytes 86024 | tf_op jit(solution)/shard_map/ppermute | solution.py:275
  84.1 10.2 %collective-permute-start.9 = (f32[56,128]{1,0:T(8,128)}, f32[56,128]{1,0:T(8,128)S(1)}, u32[]{:S(2)}, u32[]{:S(2)}) collective-permute-start(f32[56,128]{1,0:T(8,128)} %get-tuple-element.34.own), channel_id=1, source_target_pairs={{0,720},{24,744},{48,96},{72,120},{96,48},{120,72},{144,192},{168,... | collective-permute-start | bytes 86024 | tf_op jit(solution)/shard_map/ppermute | solution.py:275
  94.1 0.6 copy-start.13
  94.1 0.6 copy-start.15
  94.2 0.6 copy-start.17
  94.8 0.6 copy-start.18
  101.5 6.2 %collective-permute-start.10 = (f32[48,256]{1,0:T(8,128)}, f32[48,256]{1,0:T(8,128)S(1)}, u32[]{:S(2)}, u32[]{:S(2)}) collective-permute-start(f32[48,256]{1,0:T(8,128)} %get-tuple-element.36), channel_id=1, source_target_pairs={{0,24},{24,0},{48,72},{72,48},{96,120},{120,96},{144,168},{168,144... | collective-permute-start | bytes 147464 | tf_op jit(solution)/shard_map/ppermute | solution.py:275
  103.4 6.2 %collective-permute-start.11 = (f32[48,256]{1,0:T(8,128)}, f32[48,256]{1,0:T(8,128)S(1)}, u32[]{:S(2)}, u32[]{:S(2)}) collective-permute-start(f32[48,256]{1,0:T(8,128)} %get-tuple-element.37), channel_id=1, source_target_pairs={{0,744},{24,48},{48,24},{72,96},{96,72},{120,144},{144,120},{168,1... | collective-permute-start | bytes 147464 | tf_op jit(solution)/shard_map/ppermute | solution.py:275
  107.7 1.9 copy-start.1
  109.6 0.6 copy-start.3
  114.0 21.9 %collective-permute-start.12 = (f32[56,128]{1,0:T(8,128)}, f32[56,128]{1,0:T(8,128)S(1)}, u32[]{:S(2)}, u32[]{:S(2)}) collective-permute-start(f32[56,128]{1,0:T(8,128)} %get-tuple-element.39.own), channel_id=1, source_target_pairs={{0,24},{24,0},{48,72},{72,48},{96,120},{120,96},{144,168},{168,144... | collective-permute-start | bytes 86024 | tf_op jit(solution)/shard_map/ppermute | solution.py:275
  121.3 14.7 %collective-permute-start.13 = (f32[56,128]{1,0:T(8,128)}, f32[56,128]{1,0:T(8,128)S(1)}, u32[]{:S(2)}, u32[]{:S(2)}) collective-permute-start(f32[56,128]{1,0:T(8,128)} %get-tuple-element.39.own), channel_id=1, source_target_pairs={{0,48},{24,72},{48,0},{72,24},{96,144},{120,168},{144,96},{168,120... | collective-permute-start | bytes 86024 | tf_op jit(solution)/shard_map/ppermute | solution.py:275
  123.2 12.8 %collective-permute-start.14 = (f32[56,128]{1,0:T(8,128)}, f32[56,128]{1,0:T(8,128)S(1)}, u32[]{:S(2)}, u32[]{:S(2)}) collective-permute-start(f32[56,128]{1,0:T(8,128)} %get-tuple-element.39.own), channel_id=1, source_target_pairs={{0,744},{24,48},{48,24},{72,96},{96,72},{120,144},{144,120},{168,1... | collective-permute-start | bytes 86024 | tf_op jit(solution)/shard_map/ppermute | solution.py:275
  126.6 10.5 %collective-permute-start.15 = (f32[56,128]{1,0:T(8,128)}, f32[56,128]{1,0:T(8,128)S(1)}, u32[]{:S(2)}, u32[]{:S(2)}) collective-permute-start(f32[56,128]{1,0:T(8,128)} %get-tuple-element.39.own), channel_id=1, source_target_pairs={{0,720},{24,744},{48,96},{72,120},{96,48},{120,72},{144,192},{168,... | collective-permute-start | bytes 86024 | tf_op jit(solution)/shard_map/ppermute | solution.py:275
  135.9 12.6 %copy-start.19 = (f32[1183]{0:T(1024)S(1)}, f32[1183]{0:T(1024)}, u32[]{:S(2)}) copy-start(f32[1183]{0:T(1024)} %param.17) | copy-start | bytes 14200
  135.9 1.1 copy-start.11
  136.0 1.1 copy-start.12
  136.0 1.1 copy-start.14
  137.1 0.6 copy-start.16
  143.8 6.2 %collective-permute-start.16 = (f32[48,256]{1,0:T(8,128)}, f32[48,256]{1,0:T(8,128)S(1)}, u32[]{:S(2)}, u32[]{:S(2)}) collective-permute-start(f32[48,256]{1,0:T(8,128)} %get-tuple-element.41), channel_id=1, source_target_pairs={{0,24},{24,0},{48,72},{72,48},{96,120},{120,96},{144,168},{168,144... | collective-permute-start | bytes 147464 | tf_op jit(solution)/shard_map/ppermute | solution.py:275
  146.1 6.2 %collective-permute-start.17 = (f32[48,256]{1,0:T(8,128)}, f32[48,256]{1,0:T(8,128)S(1)}, u32[]{:S(2)}, u32[]{:S(2)}) collective-permute-start(f32[48,256]{1,0:T(8,128)} %get-tuple-element.42), channel_id=1, source_target_pairs={{0,744},{24,48},{48,24},{72,96},{96,72},{120,144},{144,120},{168,1... | collective-permute-start | bytes 147464 | tf_op jit(solution)/shard_map/ppermute | solution.py:275
  150.0 2.3 copy-start.5
  152.3 0.6 copy-start.6
  248.0 16.6 %all-to-all-start.1 = ((f32[32,16,128]{2,1,0:T(8,128)}), f32[32,16,128]{2,1,0:T(8,128)S(1)}, u32[]{:S(2)}, u32[]{:S(2)}) async-start(f32[32,16,128]{2,1,0:T(8,128)} %bitcast.15), calls=%async_computation.1 | async-start | bytes 524288 | tf_op jit(solution)/shard_map/all_to_all | solution.py:348
  264.7 0.7 copy-start
Sparse Core Ops, SparseCore 0:
  156.7 63.4 all-gather.1

commit v2 on v1

v2 whole, which is shorter than its diff:
```python
import functools
import math

import jax
import jax.numpy as jnp
from jax import lax
from jax.experimental import pallas as pl
from jax.experimental.pallas import tpu as pltpu
from jax.sharding import PartitionSpec as P


CENTER = 1.0
HALF_WIDTH = 1.0
LOWEST = -0.5
CORES = 2
CUBE = 8
F32 = jnp.float32
BF16 = jnp.bfloat16


def filter_terms():
    sigma_now = HALF_WIDTH / (LOWEST - CENTER)
    gamma_ratio = 2.0 / sigma_now
    first_scale = sigma_now / HALF_WIDTH
    later_terms = []
    for _ in range(2):
        sigma_next = 1.0 / (gamma_ratio - sigma_now)
        later_terms.append((2.0 * sigma_next / HALF_WIDTH, sigma_now * sigma_next))
        sigma_now = sigma_next
    return (first_scale, later_terms)


def up(value, step):
    return (value + step - 1) // step * step


def split(x, count=2):
    parts = []
    for _ in range(count):
        parts.append(x.astype(BF16))
        x = x - parts[-1].astype(F32)
    return parts


def nn(a, b):
    return lax.dot_general(a, b, (((1,), (0,)), ((), ())), preferred_element_type=F32)


def nt(a, b):
    return lax.dot_general(a, b, (((1,), (1,)), ((), ())), preferred_element_type=F32)


def pick(x, table, dot, count=2):
    rows = x.shape[0]
    out = dot(jnp.concatenate(split(x, count), axis=0), table)
    total = out[(count - 1) * rows :]
    for k in range(count - 2, -1, -1):
        total = out[k * rows : (k + 1) * rows] + total
    return total


def full(x, parts, dot):
    rows = x.shape[0]
    pair = split(x)
    first = dot(jnp.concatenate(pair, axis=0), parts[0])
    return first[:rows] + (first[rows:] + dot(pair[0], parts[1]))


def column(row, lanes=128):
    return jnp.broadcast_to(row, (lanes, row.shape[1])).T


def hot(mask):
    return jnp.where(mask, 1.0, 0.0).astype(BF16)


def message(coeffs, atoms):
    return jnp.concatenate([coeffs, jnp.broadcast_to(atoms, (8, atoms.shape[1]))], axis=0)


def node_row(node_map, ids):
    ncell, cnodes = node_map.shape
    width = ids.shape[1] // ncell
    ids[...] = jnp.full(ids.shape, -1.0, F32)
    for c in range(ncell):
        ids[0:1, c * width : c * width + cnodes] = node_map[c : c + 1, :].astype(F32)
    return ids[0:1, :]


def enter_kernel(waves, node_map, proj, contacts, scales, x_out, msg_out, parts_out, aux_out, wide, ids, pad):
    _, nodes = waves.shape
    ncell, cnodes = node_map.shape
    slots, flat = scales.shape[0], proj.shape[0]
    width = ids.shape[1] // ncell
    id_row = node_row(node_map, ids)
    wide[...] = jnp.zeros(wide.shape, F32)
    wide[:, :nodes] = waves[...]
    place = lax.broadcasted_iota(jnp.int32, (wide.shape[1], ids.shape[1]), 0).astype(F32)
    x = pick(wide[...], hot(place == id_row), nn)
    x_out[...] = x
    entries = contacts.shape[1]
    entry_of = lax.broadcasted_iota(jnp.int32, (entries, flat), 1) // slots
    repeat = hot(entry_of == lax.broadcasted_iota(jnp.int32, (entries, flat), 0))
    both = jnp.concatenate(
        [jnp.broadcast_to(contacts[k : k + 1, :].astype(F32), (8, entries)) for k in range(2)],
        axis=0,
    )
    rows = nn(both.astype(BF16), repeat)
    cells, atoms = rows[0:1], rows[8:9]
    count = scales.shape[1]
    atom_of = lax.broadcasted_iota(jnp.int32, (count, flat), 0).astype(F32)
    by_slot = pick(scales[...], hot(atom_of == atoms), nn, 3)
    slot_of = lax.broadcasted_iota(jnp.int32, (slots, flat), 1) % slots
    mine = slot_of == lax.broadcasted_iota(jnp.int32, (slots, flat), 0)
    scale = jnp.sum(jnp.where(mine, by_slot, 0.0), axis=0, keepdims=True)
    aux_out[0:8, :] = jnp.broadcast_to(atoms, (8, flat))
    aux_out[8:16, :] = jnp.broadcast_to(scale, (8, flat))
    pad[...] = jnp.zeros(pad.shape, F32)
    pad[:, :cnodes] = proj[...]
    cell_column = column(cells)
    block = pad[...]
    spread = []
    for c in range(ncell):
        keep = cell_column == float(c)
        for t in range(width // 128):
            spread.append(jnp.where(keep, block[:, t * 128 : (t + 1) * 128], 0.0))
    parts = split(jnp.concatenate(spread, axis=1))
    for k in range(2):
        parts_out[k] = parts[k]
    msg_out[...] = message(full(x, parts, nt), atoms)


def table_kernel(node_map, share, parity, matrix, w_out, s_out, m_out, weight_out, ids, face, pad, here, sem):
    ncell, cnodes = node_map.shape
    faces = share.shape[2]
    span = face.shape[1] // 2
    copy = pltpu.make_async_copy(matrix, here, sem)
    copy.start()
    id_row = node_row(node_map, ids)
    total = ids.shape[1]
    face[...] = jnp.full(face.shape, -2.0, F32)
    low = share[0, 0:1, :].astype(F32)
    high = share[0, 1:2, :].astype(F32)
    even = parity[...] == 0
    face[0:1, 0:faces] = jnp.where(even, high, low)
    face[0:1, span : span + faces] = jnp.where(even, low, high)
    face_row = face[0:1, :]
    id_column = column(id_row)
    face_column = column(face_row)
    for t in range(total // 128):
        w_out[:, t * 128 : (t + 1) * 128] = hot(id_column == id_row[:, t * 128 : (t + 1) * 128])
    for t in range(2 * span // 128):
        w_out[:, total + t * 128 : total + (t + 1) * 128] = hot(
            id_column == face_row[:, t * 128 : (t + 1) * 128]
        )
    for t in range(total // 128):
        s_out[:, t * 128 : (t + 1) * 128] = hot(
            face_column == id_row[:, t * 128 : (t + 1) * 128]
        )
    count = nn(jnp.ones((16, total), BF16), w_out[:, :total])
    weight_out[...] = 1.0 / jnp.maximum(count[0:8], 1.0)
    pad[...] = jnp.zeros(pad.shape, F32)
    copy.wait()
    for c in range(ncell):
        pad[:cnodes, :cnodes] = here[c]
        parts = split(pad[...])
        for k in range(2):
            m_out[k, c] = parts[k]


def cell_kernel(x, m, o_out):
    ncell = m.shape[1]
    width = m.shape[2]
    for c in range(ncell):
        o_out[:, c * width : (c + 1) * width] = full(
            x[:, c * width : (c + 1) * width], [m[k, c] for k in range(2)], nt
        )


def gather_kernel(o, own, m1, m2, m3, m4, aux, parts, w, v_out, a_out, b_out):
    bands = o.shape[0]
    flat = own.shape[1]
    slots = 8
    atom_column = column(aux[0:1, :])
    row = lax.broadcasted_iota(jnp.int32, (flat, flat), 0)
    col = lax.broadcasted_iota(jnp.int32, (flat, flat), 1)
    same_slot = (row & (slots - 1)) == (col & (slots - 1))
    total = jnp.zeros((bands, flat), F32)
    for near in (own, m1, m2, m3, m4):
        table = hot((atom_column == near[bands : bands + 1, :]) & same_slot)
        total = total + pick(near[:bands, :], table, nt)
    scale_row = aux[8:9, :]
    returned = total * scale_row
    out = o[...] + full(returned, [parts[k] for k in range(2)], nn)
    spread = pick(out, w[...], nn)
    cells = o.shape[1]
    span = (w.shape[1] - cells) // 2
    v_out[...] = spread[:, :cells]
    a_out[...] = spread[:, cells : cells + span]
    b_out[...] = spread[:, cells + span :]


def step_kernel(lead, back, v, from_a, from_b, s, now, before, parts, aux, x_out, msg_out):
    incoming = jnp.concatenate([from_a[...], from_b[...]], axis=1)
    operated = v[...] + pick(incoming, s[...], nn)
    x = lead * (operated - CENTER * now[...])
    if back:
        x = x - back * before[...]
    x_out[...] = x
    msg_out[...] = message(full(x, [parts[k] for k in range(2)], nt), aux[0:1, :])


def leave_kernel(
    lead, back, v, from_a, from_b, s, now, before, weight, node_map, share, mass, y_out, z_out, ids
):
    _, nodes = y_out.shape
    incoming = jnp.concatenate([from_a[...], from_b[...]], axis=1)
    operated = v[...] + pick(incoming, s[...], nn)
    x = lead * (operated - CENTER * now[...]) - back * before[...]
    whole = up(nodes, 128)
    id_column = column(node_row(node_map, ids))
    tables = []
    for t in range(whole // 128):
        lane = lax.broadcasted_iota(jnp.int32, (ids.shape[1], 128), 1) + t * 128
        tables.append(hot(id_column == lane.astype(F32)))
    y = pick(x * weight[0:1, :], jnp.concatenate(tables, axis=1), nn, 3)[:, :nodes]
    y_out[...] = y
    low_column = column(share[0, 0:1, :].astype(F32))[:, 0:1]
    lane = lax.broadcasted_iota(jnp.int32, (low_column.shape[0], nodes), 1).astype(F32)
    shared = jnp.max(jnp.where(low_column == lane, 1.0, 0.0), axis=0, keepdims=True)
    z_out[...] = (y * ((1.0 - shared) * jnp.sqrt(mass[...]))).astype(BF16)


def gram_kernel(bands, left, right, out):
    product = nt(left[...], right[...])
    rows, cols = product.shape
    whole = cols // 128
    used = 0
    for r in range(rows // 8):
        for c in range(whole):
            out[used : used + 8, :] = product[8 * r : 8 * r + 8, 128 * c : 128 * c + 128]
            used += 8
    rest = cols - 128 * whole
    owners = rows // bands
    if rest:
        out[used : used + bands, :] = jnp.concatenate(
            [product[k * bands : (k + 1) * bands, 128 * whole :] for k in range(owners)], axis=1
        )
        used += bands
    if used < out.shape[0]:
        out[used:, :] = jnp.zeros((out.shape[0] - used, 128), F32)


def sum_kernel(groups, x, out):
    rows = x.shape[0] // groups
    total = x[0:rows, :]
    for k in range(1, groups):
        total = total + x[k * rows : (k + 1) * rows, :]
    for k in range(groups):
        out[k * rows : (k + 1) * rows, :] = total


def spread_kernel(bands, scale, x, out):
    rows, cols = out.shape
    whole = cols // 128
    rest = cols - 128 * whole
    used = 0
    for r in range(rows // 8):
        for c in range(whole):
            out[8 * r : 8 * r + 8, 128 * c : 128 * c + 128] = x[used : used + 8, :] / scale
            used += 8
    if rest:
        last = x[used : used + bands, :] / scale
        for k in range(rows // bands):
            out[k * bands : (k + 1) * bands, 128 * whole :] = last[:, k * rest : (k + 1) * rest]


def finish_kernel(first_row, x, out):
    bands, cols = out.shape
    groups = cols // bands
    cubes = groups // CUBE
    blocks = []
    for g in range(groups):
        cube, place, core = g // CUBE, g % CUBE // CORES, g % CORES
        at = (core * cubes + cube) * bands
        blocks.append(x[place * bands : (place + 1) * bands, at : at + bands])
    value = jnp.concatenate(blocks, axis=1)
    row = lax.broadcasted_iota(jnp.int32, value.shape, 0) + first_row[0, 0]
    col = lax.broadcasted_iota(jnp.int32, value.shape, 1)
    out[...] = jnp.where(row == col, 0.0, value)


def call(body, outs, scratch=(), smem=(), hbm=()):
    def run(*args):
        spaces = {**{k: pltpu.SMEM for k in smem}, **{k: pl.ANY for k in hbm}}
        specs = [
            pl.BlockSpec(memory_space=spaces.get(k, pltpu.VMEM)) for k in range(len(args))
        ]
        return pl.pallas_call(
            body,
            out_shape=[jax.ShapeDtypeStruct(shape, kind) for shape, kind in outs],
            in_specs=specs,
            out_specs=[pl.BlockSpec(memory_space=pltpu.VMEM) for _ in outs],
            scratch_shapes=[
                one if not isinstance(one, tuple) else pltpu.VMEM(*one) for one in scratch
            ],
        )(*args)

    return run


def swap(x, stride, inner):
    count = lax.axis_size("cell")
    pairs = []
    for q in range(count):
        ahead = (q // stride) % 2 == (0 if inner else 1)
        pairs.append((q, (q + stride if ahead else q - stride) % count))
    return lax.ppermute(x, "cell", pairs)


def filtered_bands(
    waves, cell_matrix, node_map, share_list, contacts, proj_values, coupling, proj_count, mass
):
    bands, nodes = waves.shape
    ncell, cnodes = node_map.shape
    faces = share_list.shape[2]
    entries, slots = proj_values.shape[:2]
    width = up(cnodes, 128)
    total = ncell * width
    whole = up(nodes, 128)
    span = up(faces, 128)
    flat = entries * slots
    parity = jnp.broadcast_to(lax.axis_index("cell") % 2, (1, 1)).astype(jnp.int32)
    levels = jnp.arange(slots, dtype=jnp.int32)
    scales = jnp.where(levels[None, :] < proj_count[:, None], coupling, 0.0).T
    proj = proj_values.reshape(flat, cnodes)

    x0, msg, parts, aux = call(
        enter_kernel,
        [
            ((bands, total), F32),
            ((bands + 8, flat), F32),
            ((2, flat, total), BF16),
            ((16, flat), F32),
        ],
        [((bands, whole), F32), ((8, total), F32), ((flat, width), F32)],
    )(waves, node_map, proj, contacts, scales)
    w, s, m, weight = call(
        table_kernel,
        [
            ((total, total + 2 * span), BF16),
            ((2 * span, total), BF16),
            ((2, ncell, width, width), BF16),
            ((8, total), F32),
        ],
        [
            ((8, total), F32),
            ((8, 2 * span), F32),
            ((width, width), F32),
            ((ncell, cnodes, cnodes), F32),
            pltpu.SemaphoreType.DMA(()),
        ],
        hbm=(3,),
    )(node_map, share_list, parity, cell_matrix)

    first_scale, later_terms = filter_terms()
    terms = [(first_scale, 0.0)] + later_terms
    before = x0
    now = x0
    for turn, (lead, back) in enumerate(terms):
        near = [swap(msg, 1, True), swap(msg, 2, True), swap(msg, 1, False), swap(msg, 2, False)]
        (o,) = call(cell_kernel, [((bands, total), F32)])(now, m)
        v, to_a, to_b = call(
            gather_kernel,
            [((bands, total), F32), ((bands, span), F32), ((bands, span), F32)],
        )(o, msg, *near, aux, parts, w)
        from_b = swap(to_b, 1, False)
        from_a = swap(to_a, 1, True)
        if turn < len(terms) - 1:
            x, msg = call(
                functools.partial(step_kernel, lead, back),
                [((bands, total), F32), ((bands + 8, flat), F32)],
            )(v, from_a, from_b, s, now, before, parts, aux)
            before, now = now, x
    return call(
        functools.partial(leave_kernel, lead, back),
        [((bands, nodes), F32), ((bands, nodes), BF16)],
        [((8, total), F32)],
    )(v, from_a, from_b, s, now, before, weight, node_map, share_list, mass[None, :])


def inner_products(zed):
    bands, nodes = zed.shape
    groups = lax.axis_size("band")
    count = lax.axis_size("cell")
    cubes, quad = groups // CUBE, CUBE // CORES
    quads = [
        [CUBE * m + CORES * i + k for i in range(quad)] for m in range(cubes) for k in range(CORES)
    ]
    across = [
        [CUBE * m + CORES * i + k for m in range(cubes)] for i in range(quad) for k in range(CORES)
    ]
    chips = [[CORES * i + k for k in range(CORES)] for i in range(groups // CORES)]

    def gather(x, members):
        return lax.all_gather(x, "band", axis=0, tiled=True, axis_index_groups=members)

    left = gather(zed, quads)
    right = gather(gather(zed, across), chips)
    height, wide = left.shape[0], right.shape[0]
    tiles = (height * wide + 1023) // 1024
    rows = 8 * up(tiles, count)
    (partial,) = call(functools.partial(gram_kernel, bands), [((rows, 128), F32)])(left, right)
    pieces = lax.all_to_all(partial, "cell", 0, 0, tiled=True)
    (summed,) = call(functools.partial(sum_kernel, count), [((rows, 128), F32)])(pieces)
    result = lax.all_to_all(summed, "cell", 0, 0, tiled=True)
    (block,) = call(
        functools.partial(spread_kernel, bands, math.sqrt(count * nodes)),
        [((height, wide), F32)],
    )(result)
    mine = lax.all_to_all(block, "band", 0, 0, tiled=True, axis_index_groups=quads)
    first_row = jnp.broadcast_to(lax.axis_index("band") * bands, (1, 1)).astype(jnp.int32)
    (gram,) = call(finish_kernel, [((bands, bands * groups), F32)], smem=(0,))(first_row, mine)
    return gram


def on_device(*args):
    filtered, zed = filtered_bands(*args)
    return (filtered, inner_products(zed))


def solution(mesh):
    return jax.shard_map(
        on_device,
        mesh=mesh,
        in_specs=(
            P("band", "cell"),
            P("cell", None, None),
            P("cell", None),
            P("cell", None, None),
            P(None, "cell"),
            P("cell", None, None),
            P(),
            P(),
            P("cell"),
        ),
        out_specs=(P("band", "cell"), P("band", None)),
        check_vma=False,
    )
```

time: 275 us -> 245 us (0.89)
  waiting for transfers between devices: 86.4 us -> 19.8 us
  blocking collectives: 22.6 us -> 80.8 us
  between operations: 14.4 us -> 0.96 us
  Pallas kernels: 61.3 us -> 55.8 us
    all_gather x1 -> x0, waiting for transfers between devices: 63.6 us -> none  [on_device(): everything = lax.all_gather(zed, 'band', axis=0, tiled=True)]
    all_gather x0 -> x3, blocking collectives: none -> 43.2 us  [gather(): lax.all_gather(x, 'band', axis=0, tiled=True, axis_index_groups=members)]
    all_to_all x1 -> x2, blocking collectives: 22.6 us -> 37.6 us  [the longest x1 21.1 us: inner_products(): pieces = lax.all_to_all(partial, 'cell', 0, 0, tiled=True)]
    pallas_call x14 -> x15, Pallas kernels: 61.3 us -> 55.8 us  [run(): pl.pallas_call(body, out_shape=[jax.ShapeDtypeStruct(shape, kind) for sha...]
    all_to_all x1, waiting for transfers between devices: 12 us -> 7.04 us  [inner_products(): lax.all_to_all(block, 'band', 0, 0, tiled=True, axis_index_groups=quads)]
  transfers between devices with their start and end apart: 20 -> 19, of which waited for: 10 -> 9; matrix products, arithmetic and copies ran while one was open for 2% -> 1% of each run, Pallas kernels for 8% -> 7%
where the time goes in v2:
time: 245 us; the launch traced here: 244 us
  blocking collectives  80.8 us (33%)
  starting transfers between devices  76.9 us (31%)
  Pallas kernels  55.8 us (23%)
  waiting for transfers between devices  19.8 us (8%)
  local copies, waits for them, and re-layouts  8.05 us (3%)
    ppermute x18, starting transfers between devices, swap(): return lax.ppermute(x, 'cell', pairs)  72.5 us
    pallas_call x15, Pallas kernels, run(): pl.pallas_call(body, out_shape=[jax.ShapeDtypeStruct(shape, kind) for sha...  55.8 us
    all_gather x3, blocking collectives, gather(): lax.all_gather(x, 'band', axis=0, tiled=True, axis_index_groups=members)  43.2 us
    all_to_all x1, blocking collectives, inner_products(): pieces = lax.all_to_all(partial, 'cell', 0, 0, tiled=True)  21.1 us
    all_to_all x1, blocking collectives, inner_products(): result = lax.all_to_all(summed, 'cell', 0, 0, tiled=True)  16.5 us
    ppermute x18, waiting for transfers between devices, swap(): return lax.ppermute(x, 'cell', pairs)  12.7 us
    unnamed x41, local copies, waits for them, and re-layouts  7.46 us
    all_to_all x1, waiting for transfers between devices, inner_products(): lax.all_to_all(block, 'band', 0, 0, tiled=True, axis_index_groups=quads)  7.04 us
  transfers between devices with their start and end apart: 19, of which 9 were waited for; matrix products, arithmetic and copies ran while one was open for 1% of the time, Pallas kernels for 7%

profile of v2, /device:TPU:8, one launch (start us, length us, event | category | flops | bytes accessed | tf_op | source)
XLA Modules:
  0.0 243.7 jit_solution(12854838238596882862)
XLA Ops:
  0.6 1.3 select_bitcast_fusion.scales
  1.9 3.4 %shard_map.104 = (f32[48,1536]{1,0:T(8,128)}, f32[56,128]{1,0:T(8,128)}, bf16[2,128,1536]{2,1,0:T(8,128)(2,1)}, f32[16,128]{1,0:T(8,128)}) custom-call(f32[48,1183]{1,0:T(8,128)} %waves.1, s32[4,343]{1,0:T(4,128)} %node_map.5, f32[128,343]{1,0:T(8,128)} %bitcast.17, s32[2,16]{1,0:T(2,128)} %contacts.1, f32[8,128]{1,0:T(8,128)} %select_bitcast_fusion.scales), custom_call_target="tpu_custom_call" | custom-call | tf_op jit(solution)/shard_map/pallas_call | solution.py:299
  5.3 11.3 %collective-permute-start = (f32[56,128]{1,0:T(8,128)}, f32[56,128]{1,0:T(8,128)S(1)}, u32[]{:S(2)}, u32[]{:S(2)}) collective-permute-start(f32[56,128]{1,0:T(8,128)} %get-tuple-element.27.own), channel_id=1, source_target_pairs={{0,24},{24,0},{48,72},{72,48},{96,120},{120,96},{144,168},{168,144... | collective-permute-start | bytes 86024 | tf_op jit(solution)/shard_map/ppermute | solution.py:318
  16.6 1.9 collective-permute-start.1
  18.6 3.4 %collective-permute-start.2 = (f32[56,128]{1,0:T(8,128)}, f32[56,128]{1,0:T(8,128)S(1)}, u32[]{:S(2)}, u32[]{:S(2)}) collective-permute-start(f32[56,128]{1,0:T(8,128)} %get-tuple-element.27.own), channel_id=1, source_target_pairs={{0,744},{24,48},{48,24},{72,96},{96,72},{120,144},{144,120},{168,1... | collective-permute-start | bytes 86024 | tf_op jit(solution)/shard_map/ppermute | solution.py:318
  21.9 5.2 %collective-permute-start.3 = (f32[56,128]{1,0:T(8,128)}, f32[56,128]{1,0:T(8,128)S(1)}, u32[]{:S(2)}, u32[]{:S(2)}) collective-permute-start(f32[56,128]{1,0:T(8,128)} %get-tuple-element.27.own), channel_id=1, source_target_pairs={{0,720},{24,744},{48,96},{72,120},{96,48},{120,72},{144,192},{168,... | collective-permute-start | bytes 86024 | tf_op jit(solution)/shard_map/ppermute | solution.py:318
  27.2 3.1 %copy.11.matrix = f32[4,343,343]{2,1,0:T(8,128)} copy(f32[4,343,343]{2,0,1:T(4,128)} %param.10) | data formatting | bytes 3764768 | tf_op args[1]
  30.3 7.6 %shard_map.105 = (bf16[1536,2048]{1,0:T(8,128)(2,1)}, bf16[512,1536]{1,0:T(8,128)(2,1)}, bf16[2,4,384,384]{3,2,1,0:T(8,128)(2,1)}, f32[8,1536]{1,0:T(8,128)}) custom-call(s32[4,343]{1,0:T(4,128)} %node_map.5, s32[1,2,169]{2,1,0:T(2,128)} %share.3, s32[1,1]{1,0:T(1,128)} %bitcast.2.parity, f32[4,343,343]{2,1,0:T(8,128)} %copy.11.matrix), custom_call_target="tpu_custom_call" | custom-call | tf_op jit(solution)/shard_map/pallas_call | solution.py:299
  37.9 3.4 %shard_map.106.o = f32[48,1536]{1,0:T(8,128)} custom-call(f32[48,1536]{1,0:T(8,128)} %get-tuple-element.25.x.now.before, bf16[2,4,384,384]{3,2,1,0:T(8,128)(2,1)} %get-tuple-element.26.m), custom_call_target="tpu_custom_call" | custom-call | tf_op jit(solution)/shard_map/pallas_call | solution.py:299
  41.3 0.0 collective-permute-done.m1
  41.3 0.0 collective-permute-done.1.m2
  41.3 0.0 collective-permute-done.3.m4
  41.3 0.5 copy-done.7
  41.9 0.0 copy-done.8
  41.9 0.0 copy-done.9
  41.9 0.0 copy-done.10
  41.9 5.5 %shard_map.107 = (f32[48,1536]{1,0:T(8,128)}, f32[48,256]{1,0:T(8,128)}, f32[48,256]{1,0:T(8,128)}) custom-call(f32[48,1536]{1,0:T(8,128)} %shard_map.106.o, f32[56,128]{1,0:T(8,128)} %get-tuple-element.27.own, f32[56,128]{1,0:T(8,128)} %copy-done.7, f32[56,128]{1,0:T(8,128)} %copy-done.8, f32[56,128]{1,0:T(8,128)} %copy-done.9, f32[56,128]{1,0:T(8,128)} %copy-done.10, ...), custom_call_target="tpu_custom_call" | custom-call | tf_op jit(solution)/shard_map/pallas_call | solution.py:299
  47.5 1.9 collective-permute-start.4
  49.4 3.3 %collective-permute-start.5 = (f32[48,256]{1,0:T(8,128)}, f32[48,256]{1,0:T(8,128)S(1)}, u32[]{:S(2)}, u32[]{:S(2)}) collective-permute-start(f32[48,256]{1,0:T(8,128)} %get-tuple-element.33), channel_id=1, source_target_pairs={{0,744},{24,48},{48,24},{72,96},{96,72},{120,144},{144,120},{168,1... | collective-permute-start | bytes 147464 | tf_op jit(solution)/shard_map/ppermute | solution.py:318
  52.7 1.0 collective-permute-done.4.from_a
  53.7 1.9 collective-permute-done.5.from_b
  55.6 0.6 copy-done.6
  56.2 3.4 %shard_map.108 = (f32[48,1536]{1,0:T(8,128)}, f32[56,128]{1,0:T(8,128)}) custom-call(f32[48,1536]{1,0:T(8,128)} %get-tuple-element.31.v, f32[48,256]{1,0:T(8,128)} %copy-done.4, f32[48,256]{1,0:T(8,128)} %copy-done.6, bf16[512,1536]{1,0:T(8,128)(2,1)} %get-tuple-element.34.s, f32[48,1536]{1,0:T(8,128)} %get-tuple-element.25.x.now.before, ...), custom_call_target="tpu_custom_call" | custom-call | tf_op jit(solution)/shard_map/pallas_call | solution.py:299
  59.6 7.2 %collective-permute-start.6 = (f32[56,128]{1,0:T(8,128)}, f32[56,128]{1,0:T(8,128)S(1)}, u32[]{:S(2)}, u32[]{:S(2)}) collective-permute-start(f32[56,128]{1,0:T(8,128)} %get-tuple-element.36.own), channel_id=1, source_target_pairs={{0,24},{24,0},{48,72},{72,48},{96,120},{120,96},{144,168},{168,144... | collective-permute-start | bytes 86024 | tf_op jit(solution)/shard_map/ppermute | solution.py:318
  66.8 1.9 collective-permute-start.7
  68.7 3.4 %collective-permute-start.8 = (f32[56,128]{1,0:T(8,128)}, f32[56,128]{1,0:T(8,128)S(1)}, u32[]{:S(2)}, u32[]{:S(2)}) collective-permute-start(f32[56,128]{1,0:T(8,128)} %get-tuple-element.36.own), channel_id=1, source_target_pairs={{0,744},{24,48},{48,24},{72,96},{96,72},{120,144},{144,120},{168,1... | collective-permute-start | bytes 86024 | tf_op jit(solution)/shard_map/ppermute | solution.py:318
  72.1 5.9 %collective-permute-start.9 = (f32[56,128]{1,0:T(8,128)}, f32[56,128]{1,0:T(8,128)S(1)}, u32[]{:S(2)}, u32[]{:S(2)}) collective-permute-start(f32[56,128]{1,0:T(8,128)} %get-tuple-element.36.own), channel_id=1, source_target_pairs={{0,720},{24,744},{48,96},{72,120},{96,48},{120,72},{144,192},{168,... | collective-permute-start | bytes 86024 | tf_op jit(solution)/shard_map/ppermute | solution.py:318
  78.0 3.4 %shard_map.109.o = f32[48,1536]{1,0:T(8,128)} custom-call(f32[48,1536]{1,0:T(8,128)} %get-tuple-element.35.x.now.before, bf16[2,4,384,384]{3,2,1,0:T(8,128)(2,1)} %get-tuple-element.26.m), custom_call_target="tpu_custom_call" | custom-call | tf_op jit(solution)/shard_map/pallas_call | solution.py:299
  81.5 0.8 collective-permute-done.9.m4
  82.3 0.6 copy-done.18
  82.9 5.5 %shard_map.110 = (f32[48,1536]{1,0:T(8,128)}, f32[48,256]{1,0:T(8,128)}, f32[48,256]{1,0:T(8,128)}) custom-call(f32[48,1536]{1,0:T(8,128)} %shard_map.109.o, f32[56,128]{1,0:T(8,128)} %get-tuple-element.36.own, f32[56,128]{1,0:T(8,128)} %copy-done.13, f32[56,128]{1,0:T(8,128)} %copy-done.15, f32[56,128]{1,0:T(8,128)} %copy-done.17, f32[56,128]{1,0:T(8,128)} %copy-done.18, ...), custom_call_target="tpu_custom_call" | custom-call | tf_op jit(solution)/shard_map/pallas_call | solution.py:299
  88.4 1.9 collective-permute-start.10
  90.4 2.3 collective-permute-start.11
  92.7 1.9 collective-permute-done.10.from_a
  94.6 1.9 collective-permute-done.11.from_b
  96.6 0.6 copy-done.5
  97.2 3.3 %shard_map.111 = (f32[48,1536]{1,0:T(8,128)}, f32[56,128]{1,0:T(8,128)}) custom-call(f32[48,1536]{1,0:T(8,128)} %get-tuple-element.37.v, f32[48,256]{1,0:T(8,128)} %copy-done.3, f32[48,256]{1,0:T(8,128)} %copy-done.5, bf16[512,1536]{1,0:T(8,128)(2,1)} %get-tuple-element.34.s, f32[48,1536]{1,0:T(8,128)} %get-tuple-element.35.x.now.before, ...), custom_call_target="tpu_custom_call" | custom-call | tf_op jit(solution)/shard_map/pallas_call | solution.py:299
  100.5 7.2 %collective-permute-start.12 = (f32[56,128]{1,0:T(8,128)}, f32[56,128]{1,0:T(8,128)S(1)}, u32[]{:S(2)}, u32[]{:S(2)}) collective-permute-start(f32[56,128]{1,0:T(8,128)} %get-tuple-element.41.own), channel_id=1, source_target_pairs={{0,24},{24,0},{48,72},{72,48},{96,120},{120,96},{144,168},{168,144... | collective-permute-start | bytes 86024 | tf_op jit(solution)/shard_map/ppermute | solution.py:318
  107.7 1.9 collective-permute-start.13
  109.7 3.4 %collective-permute-start.14 = (f32[56,128]{1,0:T(8,128)}, f32[56,128]{1,0:T(8,128)S(1)}, u32[]{:S(2)}, u32[]{:S(2)}) collective-permute-start(f32[56,128]{1,0:T(8,128)} %get-tuple-element.41.own), channel_id=1, source_target_pairs={{0,744},{24,48},{48,24},{72,96},{96,72},{120,144},{144,120},{168,1... | collective-permute-start | bytes 86024 | tf_op jit(solution)/shard_map/ppermute | solution.py:318
  113.0 5.2 %collective-permute-start.15 = (f32[56,128]{1,0:T(8,128)}, f32[56,128]{1,0:T(8,128)S(1)}, u32[]{:S(2)}, u32[]{:S(2)}) collective-permute-start(f32[56,128]{1,0:T(8,128)} %get-tuple-element.41.own), channel_id=1, source_target_pairs={{0,720},{24,744},{48,96},{72,120},{96,48},{120,72},{144,192},{168,... | collective-permute-start | bytes 86024 | tf_op jit(solution)/shard_map/ppermute | solution.py:318
  118.3 3.4 %shard_map.112.o = f32[48,1536]{1,0:T(8,128)} custom-call(f32[48,1536]{1,0:T(8,128)} %get-tuple-element.40.x.now, bf16[2,4,384,384]{3,2,1,0:T(8,128)(2,1)} %get-tuple-element.26.m), custom_call_target="tpu_custom_call" | custom-call | tf_op jit(solution)/shard_map/pallas_call | solution.py:299
  121.7 1.6 collective-permute-done.15.m4
  123.4 0.6 copy-done.16
  124.0 5.5 %shard_map.113 = (f32[48,1536]{1,0:T(8,128)}, f32[48,256]{1,0:T(8,128)}, f32[48,256]{1,0:T(8,128)}) custom-call(f32[48,1536]{1,0:T(8,128)} %shard_map.112.o, f32[56,128]{1,0:T(8,128)} %get-tuple-element.41.own, f32[56,128]{1,0:T(8,128)} %copy-done.11, f32[56,128]{1,0:T(8,128)} %copy-done.12, f32[56,128]{1,0:T(8,128)} %copy-done.14, f32[56,128]{1,0:T(8,128)} %copy-done.16, ...), custom_call_target="tpu_custom_call" | custom-call | tf_op jit(solution)/shard_map/pallas_call | solution.py:299
  129.5 2.9 %collective-permute-start.16 = (f32[48,256]{1,0:T(8,128)}, f32[48,256]{1,0:T(8,128)S(1)}, u32[]{:S(2)}, u32[]{:S(2)}) collective-permute-start(f32[48,256]{1,0:T(8,128)} %get-tuple-element.43), channel_id=1, source_target_pairs={{0,24},{24,0},{48,72},{72,48},{96,120},{120,96},{144,168},{168,144... | collective-permute-start | bytes 147464 | tf_op jit(solution)/shard_map/ppermute | solution.py:318
  132.4 2.1 collective-permute-start.17
  134.5 0.6 broadcast_in_dim.17.mass
  135.1 0.5 collective-permute-done.16.from_a
  135.7 2.9 %collective-permute-done.17.from_b = f32[48,256]{1,0:T(8,128)S(1)} collective-permute-done((f32[48,256]{1,0:T(8,128)}, f32[48,256]{1,0:T(8,128)S(1)}, u32[]{:S(2)}, u32[]{:S(2)}) %collective-permute-start.17) | collective-permute-done | bytes 49184 | tf_op jit(solution)/shard_map/ppermute | solution.py:318
  138.6 0.6 copy-done.2
  139.2 3.5 %shard_map.114 = (f32[48,1183]{1,0:T(8,128)}, bf16[48,1183]{1,0:T(8,128)(2,1)}) custom-call(f32[48,1536]{1,0:T(8,128)} %get-tuple-element.42.v, f32[48,256]{1,0:T(8,128)} %copy-done.1, f32[48,256]{1,0:T(8,128)} %copy-done.2, bf16[512,1536]{1,0:T(8,128)(2,1)} %get-tuple-element.34.s, f32[48,1536]{1,0:T(8,128)} %get-tuple-element.40.x.now, ...), custom_call_target="tpu_custom_call" | custom-call | tf_op jit(solution)/shard_map/pallas_call | solution.py:299
  142.8 24.2 %all_gather.10 = bf16[144,1183]{1,0:T(8,128)(2,1)S(1)} all-gather(bf16[48,1183]{1,0:T(8,128)(2,1)} %get-tuple-element.47), channel_id=1, replica_groups={{0,8,16},{1,9,17},{2,10,18},{3,11,19},{4,12,20},{5,13,21},{6,14,22},{7,..., dimensions={0}, use_global_device_ids=true | all-gather | bytes 454272 | tf_op jit(solution)/shard_map/all_gather | solution.py:406
  167.0 16.6 %all_gather.9.left = bf16[192,1183]{1,0:T(8,128)(2,1)} all-gather(bf16[48,1183]{1,0:T(8,128)(2,1)} %get-tuple-element.47), channel_id=1, replica_groups={{0,2,4,6},{1,3,5,7},{8,10,12,14},{9,11,13,15},{16,18,20,22},{17,19,21,2..., dimensions={0}, use_global_device_ids=true | all-gather | bytes 567840 | tf_op jit(solution)/shard_map/all_gather | solution.py:406
  183.6 2.5 %all_gather.11.right = bf16[288,1183]{1,0:T(8,128)(2,1)} all-gather(bf16[144,1183]{1,0:T(8,128)(2,1)S(1)} %all_gather.10), channel_id=1, replica_groups={{0,1},{2,3},{4,5},{6,7},{8,9},{10,11},{12,13},{14,15},{16,17},{18,19},{..., dimensions={0}, use_global_device_ids=true | all-gather | bytes 1022112 | tf_op jit(solution)/shard_map/all_gather | solution.py:406
  186.0 2.5 %shard_map.115 = f32[512,128]{1,0:T(8,128)} custom-call(bf16[192,1183]{1,0:T(8,128)(2,1)} %all_gather.9.left, bf16[288,1183]{1,0:T(8,128)(2,1)} %all_gather.11.right), custom_call_target="tpu_custom_call" | custom-call | tf_op jit(solution)/shard_map/pallas_call | solution.py:299
  188.6 21.1 %all_to_all.33 = f32[32,16,128]{2,1,0:T(8,128)} all-to-all(f32[32,16,128]{2,1,0:T(8,128)} %bitcast.16), channel_id=1, replica_groups=mesh['cell'=32,'band'=24] {'cell'}, dimensions={0} | all-to-all | bytes 524288 | tf_op jit(solution)/shard_map/all_to_all | solution.py:414
  209.6 1.7 shard_map.116
  211.4 16.5 %all_to_all.34 = f32[32,16,128]{2,1,0:T(8,128)} all-to-all(f32[32,16,128]{2,1,0:T(8,128)} %bitcast.14), channel_id=1, replica_groups=mesh['cell'=32,'band'=24] {'cell'}, dimensions={0} | all-to-all | bytes 524288 | tf_op jit(solution)/shard_map/all_to_all | solution.py:416
  227.9 1.7 shard_map.117
  229.6 4.4 %all-to-all-start.2 = ((f32[4,48,288]{2,1,0:T(8,128)}), f32[4,48,288]{2,1,0:T(8,128)S(1)}, u32[]{:S(2)}, u32[]{:S(2)}) async-start(f32[4,48,288]{2,1,0:T(8,128)} %bitcast.12), calls=%async_computation.2 | async-start | bytes 589824 | tf_op jit(solution)/shard_map/all_to_all | solution.py:421
  234.1 7.0 %all-to-all-done.2 = f32[4,48,288]{2,1,0:T(8,128)S(1)} async-done(((f32[4,48,288]{2,1,0:T(8,128)}), f32[4,48,288]{2,1,0:T(8,128)S(1)}, u32[]{:S(2)}, u32[]{:S(2)}) %all-to-all-start.2) | async-done | bytes 221216 | tf_op jit(solution)/shard_map/all_to_all | solution.py:421
  241.1 0.7 copy-done
  241.8 1.9 shard_map.118
  (37 shorter events, 0.1 us)
Async XLA Ops:
  5.3 36.0 %collective-permute-start = (f32[56,128]{1,0:T(8,128)}, f32[56,128]{1,0:T(8,128)S(1)}, u32[]{:S(2)}, u32[]{:S(2)}) collective-permute-start(f32[56,128]{1,0:T(8,128)} %get-tuple-element.27.own), channel_id=1, source_target_pairs={{0,24},{24,0},{48,72},{72,48},{96,120},{120,96},{144,168},{168,144... | collective-permute-start | bytes 86024 | tf_op jit(solution)/shard_map/ppermute | solution.py:318
  16.6 24.7 %collective-permute-start.1 = (f32[56,128]{1,0:T(8,128)}, f32[56,128]{1,0:T(8,128)S(1)}, u32[]{:S(2)}, u32[]{:S(2)}) collective-permute-start(f32[56,128]{1,0:T(8,128)} %get-tuple-element.27.own), channel_id=1, source_target_pairs={{0,48},{24,72},{48,0},{72,24},{96,144},{120,168},{144,96},{168,120... | collective-permute-start | bytes 86024 | tf_op jit(solution)/shard_map/ppermute | solution.py:318
  18.6 22.7 %collective-permute-start.2 = (f32[56,128]{1,0:T(8,128)}, f32[56,128]{1,0:T(8,128)S(1)}, u32[]{:S(2)}, u32[]{:S(2)}) collective-permute-start(f32[56,128]{1,0:T(8,128)} %get-tuple-element.27.own), channel_id=1, source_target_pairs={{0,744},{24,48},{48,24},{72,96},{96,72},{120,144},{144,120},{168,1... | collective-permute-start | bytes 86024 | tf_op jit(solution)/shard_map/ppermute | solution.py:318
  21.9 19.4 %collective-permute-start.3 = (f32[56,128]{1,0:T(8,128)}, f32[56,128]{1,0:T(8,128)S(1)}, u32[]{:S(2)}, u32[]{:S(2)}) collective-permute-start(f32[56,128]{1,0:T(8,128)} %get-tuple-element.27.own), channel_id=1, source_target_pairs={{0,720},{24,744},{48,96},{72,120},{96,48},{120,72},{144,192},{168,... | collective-permute-start | bytes 86024 | tf_op jit(solution)/shard_map/ppermute | solution.py:318
  41.3 0.6 copy-start.7
  41.3 0.6 copy-start.8
  41.3 0.6 copy-start.9
  41.3 0.6 copy-start.10
  47.5 6.2 %collective-permute-start.4 = (f32[48,256]{1,0:T(8,128)}, f32[48,256]{1,0:T(8,128)S(1)}, u32[]{:S(2)}, u32[]{:S(2)}) collective-permute-start(f32[48,256]{1,0:T(8,128)} %get-tuple-element.32), channel_id=1, source_target_pairs={{0,24},{24,0},{48,72},{72,48},{96,120},{120,96},{144,168},{168,144... | collective-permute-start | bytes 147464 | tf_op jit(solution)/shard_map/ppermute | solution.py:318
  49.4 6.2 %collective-permute-start.5 = (f32[48,256]{1,0:T(8,128)}, f32[48,256]{1,0:T(8,128)S(1)}, u32[]{:S(2)}, u32[]{:S(2)}) collective-permute-start(f32[48,256]{1,0:T(8,128)} %get-tuple-element.33), channel_id=1, source_target_pairs={{0,744},{24,48},{48,24},{72,96},{96,72},{120,144},{144,120},{168,1... | collective-permute-start | bytes 147464 | tf_op jit(solution)/shard_map/ppermute | solution.py:318
  53.7 1.9 copy-start.4
  55.6 0.6 copy-start.6
  59.6 21.9 %collective-permute-start.6 = (f32[56,128]{1,0:T(8,128)}, f32[56,128]{1,0:T(8,128)S(1)}, u32[]{:S(2)}, u32[]{:S(2)}) collective-permute-start(f32[56,128]{1,0:T(8,128)} %get-tuple-element.36.own), channel_id=1, source_target_pairs={{0,24},{24,0},{48,72},{72,48},{96,120},{120,96},{144,168},{168,144... | collective-permute-start | bytes 86024 | tf_op jit(solution)/shard_map/ppermute | solution.py:318
  66.8 14.6 %collective-permute-start.7 = (f32[56,128]{1,0:T(8,128)}, f32[56,128]{1,0:T(8,128)S(1)}, u32[]{:S(2)}, u32[]{:S(2)}) collective-permute-start(f32[56,128]{1,0:T(8,128)} %get-tuple-element.36.own), channel_id=1, source_target_pairs={{0,48},{24,72},{48,0},{72,24},{96,144},{120,168},{144,96},{168,120... | collective-permute-start | bytes 86024 | tf_op jit(solution)/shard_map/ppermute | solution.py:318
  68.7 12.7 %collective-permute-start.8 = (f32[56,128]{1,0:T(8,128)}, f32[56,128]{1,0:T(8,128)S(1)}, u32[]{:S(2)}, u32[]{:S(2)}) collective-permute-start(f32[56,128]{1,0:T(8,128)} %get-tuple-element.36.own), channel_id=1, source_target_pairs={{0,744},{24,48},{48,24},{72,96},{96,72},{120,144},{144,120},{168,1... | collective-permute-start | bytes 86024 | tf_op jit(solution)/shard_map/ppermute | solution.py:318
  72.1 10.2 %collective-permute-start.9 = (f32[56,128]{1,0:T(8,128)}, f32[56,128]{1,0:T(8,128)S(1)}, u32[]{:S(2)}, u32[]{:S(2)}) collective-permute-start(f32[56,128]{1,0:T(8,128)} %get-tuple-element.36.own), channel_id=1, source_target_pairs={{0,720},{24,744},{48,96},{72,120},{96,48},{120,72},{144,192},{168,... | collective-permute-start | bytes 86024 | tf_op jit(solution)/shard_map/ppermute | solution.py:318
  81.4 0.9 copy-start.13
  81.4 0.9 copy-start.15
  81.4 0.9 copy-start.17
  82.3 0.6 copy-start.18
  88.4 6.2 %collective-permute-start.10 = (f32[48,256]{1,0:T(8,128)}, f32[48,256]{1,0:T(8,128)S(1)}, u32[]{:S(2)}, u32[]{:S(2)}) collective-permute-start(f32[48,256]{1,0:T(8,128)} %get-tuple-element.38), channel_id=1, source_target_pairs={{0,24},{24,0},{48,72},{72,48},{96,120},{120,96},{144,168},{168,144... | collective-permute-start | bytes 147464 | tf_op jit(solution)/shard_map/ppermute | solution.py:318
  90.4 6.2 %collective-permute-start.11 = (f32[48,256]{1,0:T(8,128)}, f32[48,256]{1,0:T(8,128)S(1)}, u32[]{:S(2)}, u32[]{:S(2)}) collective-permute-start(f32[48,256]{1,0:T(8,128)} %get-tuple-element.39), channel_id=1, source_target_pairs={{0,744},{24,48},{48,24},{72,96},{96,72},{120,144},{144,120},{168,1... | collective-permute-start | bytes 147464 | tf_op jit(solution)/shard_map/ppermute | solution.py:318
  94.6 1.9 copy-start.3
  96.5 0.6 copy-start.5
  100.5 21.2 %collective-permute-start.12 = (f32[56,128]{1,0:T(8,128)}, f32[56,128]{1,0:T(8,128)S(1)}, u32[]{:S(2)}, u32[]{:S(2)}) collective-permute-start(f32[56,128]{1,0:T(8,128)} %get-tuple-element.41.own), channel_id=1, source_target_pairs={{0,24},{24,0},{48,72},{72,48},{96,120},{120,96},{144,168},{168,144... | collective-permute-start | bytes 86024 | tf_op jit(solution)/shard_map/ppermute | solution.py:318
  107.7 13.9 %collective-permute-start.13 = (f32[56,128]{1,0:T(8,128)}, f32[56,128]{1,0:T(8,128)S(1)}, u32[]{:S(2)}, u32[]{:S(2)}) collective-permute-start(f32[56,128]{1,0:T(8,128)} %get-tuple-element.41.own), channel_id=1, source_target_pairs={{0,48},{24,72},{48,0},{72,24},{96,144},{120,168},{144,96},{168,120... | collective-permute-start | bytes 86024 | tf_op jit(solution)/shard_map/ppermute | solution.py:318
  109.7 12.0 %collective-permute-start.14 = (f32[56,128]{1,0:T(8,128)}, f32[56,128]{1,0:T(8,128)S(1)}, u32[]{:S(2)}, u32[]{:S(2)}) collective-permute-start(f32[56,128]{1,0:T(8,128)} %get-tuple-element.41.own), channel_id=1, source_target_pairs={{0,744},{24,48},{48,24},{72,96},{96,72},{120,144},{144,120},{168,1... | collective-permute-start | bytes 86024 | tf_op jit(solution)/shard_map/ppermute | solution.py:318
  113.0 10.3 %collective-permute-start.15 = (f32[56,128]{1,0:T(8,128)}, f32[56,128]{1,0:T(8,128)S(1)}, u32[]{:S(2)}, u32[]{:S(2)}) collective-permute-start(f32[56,128]{1,0:T(8,128)} %get-tuple-element.41.own), channel_id=1, source_target_pairs={{0,720},{24,744},{48,96},{72,120},{96,48},{120,72},{144,192},{168,... | collective-permute-start | bytes 86024 | tf_op jit(solution)/shard_map/ppermute | solution.py:318
  121.7 12.9 %copy-start.19 = (f32[1183]{0:T(1024)S(1)}, f32[1183]{0:T(1024)}, u32[]{:S(2)}) copy-start(f32[1183]{0:T(1024)} %param.17) | copy-start | bytes 14200
  121.7 1.7 copy-start.11
  121.7 1.6 copy-start.12
  121.7 1.6 copy-start.14
  123.3 0.6 copy-start.16
  129.5 6.2 %collective-permute-start.16 = (f32[48,256]{1,0:T(8,128)}, f32[48,256]{1,0:T(8,128)S(1)}, u32[]{:S(2)}, u32[]{:S(2)}) collective-permute-start(f32[48,256]{1,0:T(8,128)} %get-tuple-element.43), channel_id=1, source_target_pairs={{0,24},{24,0},{48,72},{72,48},{96,120},{120,96},{144,168},{168,144... | collective-permute-start | bytes 147464 | tf_op jit(solution)/shard_map/ppermute | solution.py:318
  132.4 6.2 %collective-permute-start.17 = (f32[48,256]{1,0:T(8,128)}, f32[48,256]{1,0:T(8,128)S(1)}, u32[]{:S(2)}, u32[]{:S(2)}) collective-permute-start(f32[48,256]{1,0:T(8,128)} %get-tuple-element.44), channel_id=1, source_target_pairs={{0,744},{24,48},{48,24},{72,96},{96,72},{120,144},{144,120},{168,1... | collective-permute-start | bytes 147464 | tf_op jit(solution)/shard_map/ppermute | solution.py:318
  135.7 3.0 %copy-start.1 = (f32[48,256]{1,0:T(8,128)}, f32[48,256]{1,0:T(8,128)S(1)}, u32[]{:S(2)}) copy-start(f32[48,256]{1,0:T(8,128)S(1)} %collective-permute-done.16.from_a) | copy-start | bytes 147460
  138.6 0.6 copy-start.2
  229.6 11.5 %all-to-all-start.2 = ((f32[4,48,288]{2,1,0:T(8,128)}), f32[4,48,288]{2,1,0:T(8,128)S(1)}, u32[]{:S(2)}, u32[]{:S(2)}) async-start(f32[4,48,288]{2,1,0:T(8,128)} %bitcast.12), calls=%async_computation.2 | async-start | bytes 589824 | tf_op jit(solution)/shard_map/all_to_all | solution.py:421
  241.1 0.7 copy-start

commit v3 on v2

--- a/solution.py
+++ b/solution.py
@@ -85,6 +85,18 @@
     for c in range(ncell):
         ids[0:1, c * width : c * width + cnodes] = node_map[c : c + 1, :].astype(F32)
     return ids[0:1, :]
+
+
+def face_row(share, parity, face):
+    faces = share.shape[2]
+    span = face.shape[1] // 2
+    face[...] = jnp.full(face.shape, -2.0, F32)
+    low = share[0, 0:1, :].astype(F32)
+    high = share[0, 1:2, :].astype(F32)
+    even = parity[...] == 0
+    face[0:1, 0:faces] = jnp.where(even, high, low)
+    face[0:1, span : span + faces] = jnp.where(even, low, high)
+    return face[0:1, :]
 
 
 def enter_kernel(waves, node_map, proj, contacts, scales, x_out, msg_out, parts_out, aux_out, wide, ids, pad):
@@ -130,35 +142,36 @@
     msg_out[...] = message(full(x, parts, nt), atoms)
 
 
-def table_kernel(node_map, share, parity, matrix, w_out, s_out, m_out, weight_out, ids, face, pad, here, sem):
+def table_kernel(
+    node_map, share, parity, matrix, bparts,
+    q_out, f_out, s_out, m_out, weight_out, sb_out,
+    ids, face, pad, here, sem,
+):
     ncell, cnodes = node_map.shape
-    faces = share.shape[2]
     span = face.shape[1] // 2
     copy = pltpu.make_async_copy(matrix, here, sem)
     copy.start()
     id_row = node_row(node_map, ids)
     total = ids.shape[1]
-    face[...] = jnp.full(face.shape, -2.0, F32)
-    low = share[0, 0:1, :].astype(F32)
-    high = share[0, 1:2, :].astype(F32)
-    even = parity[...] == 0
-    face[0:1, 0:faces] = jnp.where(even, high, low)
-    face[0:1, span : span + faces] = jnp.where(even, low, high)
-    face_row = face[0:1, :]
+    faces_row = face_row(share, parity, face)
     id_column = column(id_row)
-    face_column = column(face_row)
+    face_column = column(faces_row)
     for t in range(total // 128):
-        w_out[:, t * 128 : (t + 1) * 128] = hot(id_column == id_row[:, t * 128 : (t + 1) * 128])
+        q_out[:, t * 128 : (t + 1) * 128] = hot(id_column == id_row[:, t * 128 : (t + 1) * 128])
     for t in range(2 * span // 128):
-        w_out[:, total + t * 128 : total + (t + 1) * 128] = hot(
-            id_column == face_row[:, t * 128 : (t + 1) * 128]
+        f_out[:, t * 128 : (t + 1) * 128] = hot(
+            id_column == faces_row[:, t * 128 : (t + 1) * 128]
         )
     for t in range(total // 128):
         s_out[:, t * 128 : (t + 1) * 128] = hot(
             face_column == id_row[:, t * 128 : (t + 1) * 128]
         )
-    count = nn(jnp.ones((16, total), BF16), w_out[:, :total])
+    count = nn(jnp.ones((16, total), BF16), q_out[...])
     weight_out[...] = 1.0 / jnp.maximum(count[0:8], 1.0)
+    table = s_out[...]
+    parts = split(nt(table, bparts[0]) + nt(table, bparts[1]))
+    for k in range(2):
+        sb_out[k] = parts[k]
     pad[...] = jnp.zeros(pad.shape, F32)
     copy.wait()
     for c in range(ncell):
@@ -168,16 +181,25 @@
             m_out[k, c] = parts[k]
 
 
-def cell_kernel(x, m, o_out):
-    ncell = m.shape[1]
-    width = m.shape[2]
+def cell_matrices(x, m, o_out):
+    ncell, width = m.shape[1], m.shape[2]
     for c in range(ncell):
         o_out[:, c * width : (c + 1) * width] = full(
             x[:, c * width : (c + 1) * width], [m[k, c] for k in range(2)], nt
         )
 
 
-def gather_kernel(o, own, m1, m2, m3, m4, aux, parts, w, v_out, a_out, b_out):
+def first_kernel(x, m, o_out):
+    cell_matrices(x, m, o_out)
+
+
+def cell_kernel(lead, u, from_a, from_b, s, m, x_out, o_out):
+    incoming = jnp.concatenate([from_a[...], from_b[...]], axis=1)
+    x_out[...] = u[...] + lead * pick(incoming, s[...], nn)
+    cell_matrices(x_out, m, o_out)
+
+
+def gather_kernel(o, own, m1, m2, m3, m4, aux, parts, f, o_out, a_out, b_out):
     bands = o.shape[0]
     flat = own.shape[1]
     slots = 8
@@ -192,43 +214,58 @@
     scale_row = aux[8:9, :]
     returned = total * scale_row
     out = o[...] + full(returned, [parts[k] for k in range(2)], nn)
-    spread = pick(out, w[...], nn)
-    cells = o.shape[1]
-    span = (w.shape[1] - cells) // 2
-    v_out[...] = spread[:, :cells]
-    a_out[...] = spread[:, cells : cells + span]
-    b_out[...] = spread[:, cells + span :]
-
-
-def step_kernel(lead, back, v, from_a, from_b, s, now, before, parts, aux, x_out, msg_out):
+    o_out[...] = out
+    faces = pick(out, f[...], nn)
+    span = a_out.shape[1]
+    a_out[...] = faces[:, :span]
+    b_out[...] = faces[:, span:]
+
+
+def inside_kernel(lead, back, o, q, now, before, parts, u_out, c_out):
+    u = lead * (pick(o[...], q[...], nn) - CENTER * now[...])
+    if back:
+        u = u - back * before[...]
+    u_out[...] = u
+    c_out[...] = full(u, [parts[k] for k in range(2)], nt)
+
+
+def send_kernel(lead, from_a, from_b, sb, c, aux, msg_out):
     incoming = jnp.concatenate([from_a[...], from_b[...]], axis=1)
-    operated = v[...] + pick(incoming, s[...], nn)
-    x = lead * (operated - CENTER * now[...])
-    if back:
-        x = x - back * before[...]
-    x_out[...] = x
-    msg_out[...] = message(full(x, [parts[k] for k in range(2)], nt), aux[0:1, :])
-
-
-def leave_kernel(
-    lead, back, v, from_a, from_b, s, now, before, weight, node_map, share, mass, y_out, z_out, ids
-):
-    _, nodes = y_out.shape
-    incoming = jnp.concatenate([from_a[...], from_b[...]], axis=1)
-    operated = v[...] + pick(incoming, s[...], nn)
-    x = lead * (operated - CENTER * now[...]) - back * before[...]
-    whole = up(nodes, 128)
+    coeffs = c[...] + lead * full(incoming, [sb[k] for k in range(2)], nn)
+    msg_out[...] = message(coeffs, aux[0:1, :])
+
+
+def last_kernel(lead, back, o, now, before, weight, node_map, share, parity, mass, y_out, f_out, z_out, ids, face):
+    nodes = mass.shape[1]
+    whole = y_out.shape[1]
+    span = face.shape[1] // 2
     id_column = column(node_row(node_map, ids))
+    face_column = column(face_row(share, parity, face))
     tables = []
     for t in range(whole // 128):
         lane = lax.broadcasted_iota(jnp.int32, (ids.shape[1], 128), 1) + t * 128
         tables.append(hot(id_column == lane.astype(F32)))
-    y = pick(x * weight[0:1, :], jnp.concatenate(tables, axis=1), nn, 3)[:, :nodes]
-    y_out[...] = y
+        f_out[:, t * 128 : (t + 1) * 128] = hot(
+            face_column == lane[: 2 * span].astype(F32)
+        )
+    past = lead * CENTER * now[...] + back * before[...]
+    u = lead * o[...] - past * weight[0:1, :]
+    y_out[...] = pick(u, jnp.concatenate(tables, axis=1), nn)
     low_column = column(share[0, 0:1, :].astype(F32))[:, 0:1]
     lane = lax.broadcasted_iota(jnp.int32, (low_column.shape[0], nodes), 1).astype(F32)
     shared = jnp.max(jnp.where(low_column == lane, 1.0, 0.0), axis=0, keepdims=True)
-    z_out[...] = (y * ((1.0 - shared) * jnp.sqrt(mass[...]))).astype(BF16)
+    z_out[...] = jnp.broadcast_to((1.0 - shared) * jnp.sqrt(mass[...]), z_out.shape)
+
+
+def leave_kernel(lead, y, from_a, from_b, f, z_scale, y_out, z_out, copies_out):
+    bands, nodes = y_out.shape
+    incoming = jnp.concatenate([from_a[...], from_b[...]], axis=1)
+    result = (y[...] + lead * pick(incoming, f[...], nn))[:, :nodes]
+    y_out[...] = result
+    z = (result * z_scale[0:1, :]).astype(BF16)
+    z_out[...] = z
+    for k in range(copies_out.shape[0] // bands):
+        copies_out[k * bands : (k + 1) * bands, :] = z
 
 
 def gram_kernel(bands, left, right, out):
@@ -345,13 +382,15 @@
         ],
         [((bands, whole), F32), ((8, total), F32), ((flat, width), F32)],
     )(waves, node_map, proj, contacts, scales)
-    w, s, m, weight = call(
+    q, f, s, m, weight, sb = call(
         table_kernel,
         [
-            ((total, total + 2 * span), BF16),
+            ((total, total), BF16),
+            ((total, 2 * span), BF16),
             ((2 * span, total), BF16),
             ((2, ncell, width, width), BF16),
             ((8, total), F32),
+            ((2, 2 * span, flat), BF16),
         ],
         [
             ((8, total), F32),
@@ -361,35 +400,46 @@
             pltpu.SemaphoreType.DMA(()),
         ],
         hbm=(3,),
-    )(node_map, share_list, parity, cell_matrix)
+    )(node_map, share_list, parity, cell_matrix, parts)
 
     first_scale, later_terms = filter_terms()
     terms = [(first_scale, 0.0)] + later_terms
-    before = x0
-    now = x0
+    block = ((bands, total), F32)
+    face_block = ((bands, span), F32)
+    before = now = x0
+    (o,) = call(first_kernel, [block])(x0, m)
     for turn, (lead, back) in enumerate(terms):
         near = [swap(msg, 1, True), swap(msg, 2, True), swap(msg, 1, False), swap(msg, 2, False)]
-        (o,) = call(cell_kernel, [((bands, total), F32)])(now, m)
-        v, to_a, to_b = call(
-            gather_kernel,
-            [((bands, total), F32), ((bands, span), F32), ((bands, span), F32)],
-        )(o, msg, *near, aux, parts, w)
+        if turn:
+            x, o = call(functools.partial(cell_kernel, terms[turn - 1][0]), [block, block])(
+                u, from_a, from_b, s, m
+            )
+            before, now = now, x
+        o, to_a, to_b = call(gather_kernel, [block, face_block, face_block])(
+            o, msg, *near, aux, parts, f
+        )
         from_b = swap(to_b, 1, False)
         from_a = swap(to_a, 1, True)
         if turn < len(terms) - 1:
-            x, msg = call(
-                functools.partial(step_kernel, lead, back),
-                [((bands, total), F32), ((bands + 8, flat), F32)],
-            )(v, from_a, from_b, s, now, before, parts, aux)
-            before, now = now, x
+            u, c = call(
+                functools.partial(inside_kernel, lead, back), [block, ((bands, flat), F32)]
+            )(o, q, now, before, parts)
+            (msg,) = call(functools.partial(send_kernel, lead), [((bands + 8, flat), F32)])(
+                from_a, from_b, sb, c, aux
+            )
+    y, table, z_scale = call(
+        functools.partial(last_kernel, lead, back),
+        [((bands, whole), F32), ((2 * span, whole), BF16), ((8, nodes), F32)],
+        [((8, total), F32), ((8, 2 * span), F32)],
+    )(o, now, before, weight, node_map, share_list, parity, mass[None, :])
+    copies = lax.axis_size("band") // CUBE
     return call(
-        functools.partial(leave_kernel, lead, back),
-        [((bands, nodes), F32), ((bands, nodes), BF16)],
-        [((8, total), F32)],
-    )(v, from_a, from_b, s, now, before, weight, node_map, share_list, mass[None, :])
-
-
-def inner_products(zed):
+        functools.partial(leave_kernel, lead),
+        [((bands, nodes), F32), ((bands, nodes), BF16), ((max(copies, 1) * bands, nodes), BF16)],
+    )(y, from_a, from_b, table, z_scale)
+
+
+def inner_products(zed, copies):
     bands, nodes = zed.shape
     groups = lax.axis_size("band")
     count = lax.axis_size("cell")
@@ -406,7 +456,8 @@
         return lax.all_gather(x, "band", axis=0, tiled=True, axis_index_groups=members)
 
     left = gather(zed, quads)
-    right = gather(gather(zed, across), chips)
+    right = lax.all_to_all(copies, "band", 0, 0, tiled=True, axis_index_groups=across)
+    right = gather(right, chips)
     height, wide = left.shape[0], right.shape[0]
     tiles = (height * wide + 1023) // 1024
     rows = 8 * up(tiles, count)
@@ -425,8 +476,8 @@
 
 
 def on_device(*args):
-    filtered, zed = filtered_bands(*args)
-    return (filtered, inner_products(zed))
+    filtered, zed, copies = filtered_bands(*args)
+    return (filtered, inner_products(zed, copies))
 
 
 def solution(mesh):

time: 245 us -> 229 us (0.935)
  blocking collectives: 80.8 us -> 61.4 us
  waiting for transfers between devices: 19.8 us -> 9.22 us
  starting transfers between devices: 76.9 us -> 86.4 us
  Pallas kernels: 55.8 us -> 60.4 us
    all_gather x3 -> x2, blocking collectives: 43.2 us -> 24.7 us  [gather(): lax.all_gather(x, 'band', axis=0, tiled=True, axis_index_groups=members)]
    ppermute x18, waiting for transfers between devices: 12.7 us -> 1.11 us  [swap(): return lax.ppermute(x, 'cell', pairs)]
    all_to_all x0 -> x1, starting transfers between devices: none -> 10.8 us  [inner_products(): lax.all_to_all(copies, 'band', 0, 0, tiled=True, axis_index_groups=across)]
    pallas_call x15 -> x18, Pallas kernels: 55.8 us -> 60.4 us  [run(): pl.pallas_call(body, out_shape=[jax.ShapeDtypeStruct(shape, kind) for sha...]
  transfers between devices with their start and end apart: 19 -> 20, of which waited for: 9 -> 3; matrix products, arithmetic and copies ran while one was open for 1% -> 2% of each run, Pallas kernels for 7% -> 14%
where the time goes in v3:
time: 229 us; the launch traced here: 228 us
  starting transfers between devices  86.4 us (38%)
  blocking collectives  61.4 us (27%)
  Pallas kernels  60.4 us (26%)
  waiting for transfers between devices  9.22 us (4%)
  local copies, waits for them, and re-layouts  8.1 us (4%)
    ppermute x18, starting transfers between devices, swap(): return lax.ppermute(x, 'cell', pairs)  70.4 us
    pallas_call x18, Pallas kernels, run(): pl.pallas_call(body, out_shape=[jax.ShapeDtypeStruct(shape, kind) for sha...  60.4 us
    all_gather x2, blocking collectives, gather(): lax.all_gather(x, 'band', axis=0, tiled=True, axis_index_groups=members)  24.7 us
    all_to_all x1, blocking collectives, inner_products(): pieces = lax.all_to_all(partial, 'cell', 0, 0, tiled=True)  20 us
    all_to_all x1, blocking collectives, inner_products(): result = lax.all_to_all(summed, 'cell', 0, 0, tiled=True)  16.8 us
    all_to_all x1, starting transfers between devices, inner_products(): lax.all_to_all(copies, 'band', 0, 0, tiled=True, axis_index_groups=across)  10.8 us
    all_to_all x1, waiting for transfers between devices, inner_products(): lax.all_to_all(block, 'band', 0, 0, tiled=True, axis_index_groups=quads)  8.1 us
    unnamed x41, local copies, waits for them, and re-layouts  7.51 us
  transfers between devices with their start and end apart: 20, of which 3 were waited for; matrix products, arithmetic and copies ran while one was open for 2% of the time, Pallas kernels for 14%

profile of v3, /device:TPU:8, one launch (start us, length us, event | category | flops | bytes accessed | tf_op | source)
XLA Modules:
  0.0 227.8 jit_solution(16634174280054137048)
XLA Ops:
  0.6 1.3 select_bitcast_fusion.scales
  1.9 3.4 %shard_map.104 = (f32[48,1536]{1,0:T(8,128)}, f32[56,128]{1,0:T(8,128)}, bf16[2,128,1536]{2,1,0:T(8,128)(2,1)}, f32[16,128]{1,0:T(8,128)}) custom-call(f32[48,1183]{1,0:T(8,128)} %waves.1, s32[4,343]{1,0:T(4,128)} %node_map.5, f32[128,343]{1,0:T(8,128)} %bitcast.21, s32[2,16]{1,0:T(2,128)} %contacts.1, f32[8,128]{1,0:T(8,128)} %select_bitcast_fusion.scales), custom_call_target="tpu_custom_call" | custom-call | tf_op jit(solution)/shard_map/pallas_call | solution.py:336
  5.3 11.3 %collective-permute-start = (f32[56,128]{1,0:T(8,128)}, f32[56,128]{1,0:T(8,128)S(1)}, u32[]{:S(2)}, u32[]{:S(2)}) collective-permute-start(f32[56,128]{1,0:T(8,128)} %get-tuple-element.38.own), channel_id=1, source_target_pairs={{0,24},{24,0},{48,72},{72,48},{96,120},{120,96},{144,168},{168,144... | collective-permute-start | bytes 86024 | tf_op jit(solution)/shard_map/ppermute | solution.py:355
  16.6 1.9 collective-permute-start.1
  18.6 3.4 %collective-permute-start.2 = (f32[56,128]{1,0:T(8,128)}, f32[56,128]{1,0:T(8,128)S(1)}, u32[]{:S(2)}, u32[]{:S(2)}) collective-permute-start(f32[56,128]{1,0:T(8,128)} %get-tuple-element.38.own), channel_id=1, source_target_pairs={{0,744},{24,48},{48,24},{72,96},{96,72},{120,144},{144,120},{168,1... | collective-permute-start | bytes 86024 | tf_op jit(solution)/shard_map/ppermute | solution.py:355
  21.9 5.2 %collective-permute-start.3 = (f32[56,128]{1,0:T(8,128)}, f32[56,128]{1,0:T(8,128)S(1)}, u32[]{:S(2)}, u32[]{:S(2)}) collective-permute-start(f32[56,128]{1,0:T(8,128)} %get-tuple-element.38.own), channel_id=1, source_target_pairs={{0,720},{24,744},{48,96},{72,120},{96,48},{120,72},{144,192},{168,... | collective-permute-start | bytes 86024 | tf_op jit(solution)/shard_map/ppermute | solution.py:355
  27.2 3.1 %copy.11.matrix = f32[4,343,343]{2,1,0:T(8,128)} copy(f32[4,343,343]{2,0,1:T(4,128)} %param.10) | data formatting | bytes 3764768 | tf_op args[1]
  30.3 8.3 %shard_map.105 = (bf16[1536,1536]{1,0:T(8,128)(2,1)}, bf16[1536,512]{1,0:T(8,128)(2,1)}, bf16[512,1536]{1,0:T(8,128)(2,1)}, bf16[2,4,384,384]{3,2,1,0:T(8,128)(2...) custom-call(s32[4,343]{1,0:T(4,128)} %node_map.5, s32[1,2,169]{2,1,0:T(2,128)} %share.3, s32[1,1]{1,0:T(1,128)} %bitcast.2.parity, ...), custom_call_target="tpu_custom_call" | custom-call | tf_op jit(solution)/shard_map/pallas_call | solution.py:336
  38.7 3.4 %shard_map.106.o = f32[48,1536]{1,0:T(8,128)} custom-call(f32[48,1536]{1,0:T(8,128)} %get-tuple-element.35.x.now.before, bf16[2,4,384,384]{3,2,1,0:T(8,128)(2,1)} %get-tuple-element.37.m), custom_call_target="tpu_custom_call" | custom-call | tf_op jit(solution)/shard_map/pallas_call | solution.py:336
  42.2 0.5 copy-done.7
  42.7 0.0 copy-done.8
  42.8 0.0 copy-done.9
  42.8 0.0 copy-done.10
  42.8 3.4 %shard_map.107 = (f32[48,1536]{1,0:T(8,128)}, f32[48,256]{1,0:T(8,128)}, f32[48,256]{1,0:T(8,128)}) custom-call(f32[48,1536]{1,0:T(8,128)} %shard_map.106.o, f32[56,128]{1,0:T(8,128)} %get-tuple-element.38.own, f32[56,128]{1,0:T(8,128)} %copy-done.7, f32[56,128]{1,0:T(8,128)} %copy-done.8, f32[56,128]{1,0:T(8,128)} %copy-done.9, f32[56,128]{1,0:T(8,128)} %copy-done.10, ...), custom_call_target="tpu_custom_call" | custom-call | tf_op jit(solution)/shard_map/pallas_call | solution.py:336
  46.2 1.9 collective-permute-start.4
  48.1 3.3 %collective-permute-start.5 = (f32[48,256]{1,0:T(8,128)}, f32[48,256]{1,0:T(8,128)S(1)}, u32[]{:S(2)}, u32[]{:S(2)}) collective-permute-start(f32[48,256]{1,0:T(8,128)} %get-tuple-element.45), channel_id=1, source_target_pairs={{0,744},{24,48},{48,24},{72,96},{96,72},{120,144},{144,120},{168,1... | collective-permute-start | bytes 147464 | tf_op jit(solution)/shard_map/ppermute | solution.py:355
  51.3 4.8 %shard_map.108 = (f32[48,1536]{1,0:T(8,128)}, f32[48,128]{1,0:T(8,128)}) custom-call(f32[48,1536]{1,0:T(8,128)} %get-tuple-element.41.o, bf16[1536,1536]{1,0:T(8,128)(2,1)} %get-tuple-element.42.q, f32[48,1536]{1,0:T(8,128)} %get-tuple-element.35.x.now.before, f32[48,1536]{1,0:T(8,128)} %get-tuple-element.35.x.now.before, ...), custom_call_target="tpu_custom_call" | custom-call | tf_op jit(solution)/shard_map/pallas_call | solution.py:336
  56.1 0.6 copy-done.3
  56.7 0.0 copy-done.4
  56.7 1.8 shard_map.110.own
  58.5 5.4 %collective-permute-start.6 = (f32[56,128]{1,0:T(8,128)}, f32[56,128]{1,0:T(8,128)S(1)}, u32[]{:S(2)}, u32[]{:S(2)}) collective-permute-start(f32[56,128]{1,0:T(8,128)} %shard_map.110.own), channel_id=1, source_target_pairs={{0,24},{24,0},{48,72},{72,48},{96,120},{120,96},{144,168},{168,144... | collective-permute-start | bytes 86024 | tf_op jit(solution)/shard_map/ppermute | solution.py:355
  63.9 1.9 collective-permute-start.7
  65.9 3.4 %collective-permute-start.8 = (f32[56,128]{1,0:T(8,128)}, f32[56,128]{1,0:T(8,128)S(1)}, u32[]{:S(2)}, u32[]{:S(2)}) collective-permute-start(f32[56,128]{1,0:T(8,128)} %shard_map.110.own), channel_id=1, source_target_pairs={{0,744},{24,48},{48,24},{72,96},{96,72},{120,144},{144,120},{168,1... | collective-permute-start | bytes 86024 | tf_op jit(solution)/shard_map/ppermute | solution.py:355
  69.2 5.9 %collective-permute-start.9 = (f32[56,128]{1,0:T(8,128)}, f32[56,128]{1,0:T(8,128)S(1)}, u32[]{:S(2)}, u32[]{:S(2)}) collective-permute-start(f32[56,128]{1,0:T(8,128)} %shard_map.110.own), channel_id=1, source_target_pairs={{0,720},{24,744},{48,96},{72,120},{96,48},{120,72},{144,192},{168,... | collective-permute-start | bytes 86024 | tf_op jit(solution)/shard_map/ppermute | solution.py:355
  75.2 4.2 %shard_map.109 = (f32[48,1536]{1,0:T(8,128)}, f32[48,1536]{1,0:T(8,128)}) custom-call(f32[48,1536]{1,0:T(8,128)} %get-tuple-element.43.u, f32[48,256]{1,0:T(8,128)} %copy-done.3, f32[48,256]{1,0:T(8,128)} %copy-done.4, bf16[512,1536]{1,0:T(8,128)(2,1)} %get-tuple-element.46.s, bf16[2,4,384,384]{3,2,1,0:T(8,128)(2,1)} %get-tuple-element.37.m), custom_call_target="tpu_custom_call" | custom-call | tf_op jit(solution)/shard_map/pallas_call | solution.py:336
  79.4 0.0 collective-permute-done.9.m4
  79.4 0.5 copy-done.13
  80.0 0.0 copy-done.15
  80.0 0.0 copy-done.17
  80.0 0.0 copy-done.18
  80.0 3.4 %shard_map.111 = (f32[48,1536]{1,0:T(8,128)}, f32[48,256]{1,0:T(8,128)}, f32[48,256]{1,0:T(8,128)}) custom-call(f32[48,1536]{1,0:T(8,128)} %get-tuple-element.47.o, f32[56,128]{1,0:T(8,128)} %shard_map.110.own, f32[56,128]{1,0:T(8,128)} %copy-done.13, f32[56,128]{1,0:T(8,128)} %copy-done.15, f32[56,128]{1,0:T(8,128)} %copy-done.17, f32[56,128]{1,0:T(8,128)} %copy-done.18, ...), custom_call_target="tpu_custom_call" | custom-call | tf_op jit(solution)/shard_map/pallas_call | solution.py:336
  83.4 3.0 %collective-permute-start.10 = (f32[48,256]{1,0:T(8,128)}, f32[48,256]{1,0:T(8,128)S(1)}, u32[]{:S(2)}, u32[]{:S(2)}) collective-permute-start(f32[48,256]{1,0:T(8,128)} %get-tuple-element.53), channel_id=1, source_target_pairs={{0,24},{24,0},{48,72},{72,48},{96,120},{120,96},{144,168},{168,144... | collective-permute-start | bytes 147464 | tf_op jit(solution)/shard_map/ppermute | solution.py:355
  86.4 1.9 collective-permute-start.11
  88.3 4.8 %shard_map.112 = (f32[48,1536]{1,0:T(8,128)}, f32[48,128]{1,0:T(8,128)}) custom-call(f32[48,1536]{1,0:T(8,128)} %get-tuple-element.50.o, bf16[1536,1536]{1,0:T(8,128)(2,1)} %get-tuple-element.42.q, f32[48,1536]{1,0:T(8,128)} %get-tuple-element.51.now.before, f32[48,1536]{1,0:T(8,128)} %get-tuple-element.35.x.now.before, ...), custom_call_target="tpu_custom_call" | custom-call | tf_op jit(solution)/shard_map/pallas_call | solution.py:336
  93.1 0.6 copy-done.1
  93.7 1.8 shard_map.114.own
  95.5 5.7 %collective-permute-start.12 = (f32[56,128]{1,0:T(8,128)}, f32[56,128]{1,0:T(8,128)S(1)}, u32[]{:S(2)}, u32[]{:S(2)}) collective-permute-start(f32[56,128]{1,0:T(8,128)} %shard_map.114.own), channel_id=1, source_target_pairs={{0,24},{24,0},{48,72},{72,48},{96,120},{120,96},{144,168},{168,144... | collective-permute-start | bytes 86024 | tf_op jit(solution)/shard_map/ppermute | solution.py:355
  101.2 1.9 collective-permute-start.13
  103.1 3.4 %collective-permute-start.14 = (f32[56,128]{1,0:T(8,128)}, f32[56,128]{1,0:T(8,128)S(1)}, u32[]{:S(2)}, u32[]{:S(2)}) collective-permute-start(f32[56,128]{1,0:T(8,128)} %shard_map.114.own), channel_id=1, source_target_pairs={{0,744},{24,48},{48,24},{72,96},{96,72},{120,144},{144,120},{168,1... | collective-permute-start | bytes 86024 | tf_op jit(solution)/shard_map/ppermute | solution.py:355
  106.5 5.2 %collective-permute-start.15 = (f32[56,128]{1,0:T(8,128)}, f32[56,128]{1,0:T(8,128)S(1)}, u32[]{:S(2)}, u32[]{:S(2)}) collective-permute-start(f32[56,128]{1,0:T(8,128)} %shard_map.114.own), channel_id=1, source_target_pairs={{0,720},{24,744},{48,96},{72,120},{96,48},{120,72},{144,192},{168,... | collective-permute-start | bytes 86024 | tf_op jit(solution)/shard_map/ppermute | solution.py:355
  111.7 4.2 %shard_map.113 = (f32[48,1536]{1,0:T(8,128)}, f32[48,1536]{1,0:T(8,128)}) custom-call(f32[48,1536]{1,0:T(8,128)} %get-tuple-element.52.u, f32[48,256]{1,0:T(8,128)} %copy-done.1, f32[48,256]{1,0:T(8,128)} %copy-done.2, bf16[512,1536]{1,0:T(8,128)(2,1)} %get-tuple-element.46.s, bf16[2,4,384,384]{3,2,1,0:T(8,128)(2,1)} %get-tuple-element.37.m), custom_call_target="tpu_custom_call" | custom-call | tf_op jit(solution)/shard_map/pallas_call | solution.py:336
  116.0 0.7 collective-permute-done.15.m4
  116.7 0.6 copy-done.16
  117.3 3.4 %shard_map.115 = (f32[48,1536]{1,0:T(8,128)}, f32[48,256]{1,0:T(8,128)}, f32[48,256]{1,0:T(8,128)}) custom-call(f32[48,1536]{1,0:T(8,128)} %get-tuple-element.55.o, f32[56,128]{1,0:T(8,128)} %shard_map.114.own, f32[56,128]{1,0:T(8,128)} %copy-done.11, f32[56,128]{1,0:T(8,128)} %copy-done.12, f32[56,128]{1,0:T(8,128)} %copy-done.14, f32[56,128]{1,0:T(8,128)} %copy-done.16, ...), custom_call_target="tpu_custom_call" | custom-call | tf_op jit(solution)/shard_map/pallas_call | solution.py:336
  120.7 3.7 %collective-permute-start.16 = (f32[48,256]{1,0:T(8,128)}, f32[48,256]{1,0:T(8,128)S(1)}, u32[]{:S(2)}, u32[]{:S(2)}) collective-permute-start(f32[48,256]{1,0:T(8,128)} %get-tuple-element.61), channel_id=1, source_target_pairs={{0,24},{24,0},{48,72},{72,48},{96,120},{120,96},{144,168},{168,144... | collective-permute-start | bytes 147464 | tf_op jit(solution)/shard_map/ppermute | solution.py:355
  124.3 2.1 collective-permute-start.17
  126.4 0.6 broadcast_in_dim.17.mass
  127.0 3.2 %shard_map.116 = (f32[48,1280]{1,0:T(8,128)}, bf16[512,1280]{1,0:T(8,128)(2,1)}, f32[8,1183]{1,0:T(8,128)}) custom-call(f32[48,1536]{1,0:T(8,128)} %get-tuple-element.57.o, f32[48,1536]{1,0:T(8,128)} %get-tuple-element.58.now, f32[48,1536]{1,0:T(8,128)} %get-tuple-element.51.now.before, f32[8,1536]{1,0:T(8,128)} %get-tuple-element.59.weight, ...), custom_call_target="tpu_custom_call" | custom-call | tf_op jit(solution)/shard_map/pallas_call | solution.py:336
  130.2 0.3 collective-permute-done.17.from_b
  130.5 0.3 copy-done.5
  130.8 0.3 copy-done.6
  131.1 2.6 %shard_map.117 = (f32[48,1183]{1,0:T(8,128)}, bf16[48,1183]{1,0:T(8,128)(2,1)}, bf16[144,1183]{1,0:T(8,128)(2,1)}) custom-call(f32[48,1280]{1,0:T(8,128)} %get-tuple-element.60.y, f32[48,256]{1,0:T(8,128)} %copy-done.5, f32[48,256]{1,0:T(8,128)} %copy-done.6, bf16[512,1280]{1,0:T(8,128)(2,1)} %get-tuple-element.63.f, f32[8,1183]{1,0:T(8,128)} %get-tuple-element.64.z_scale), custom_call_target="tpu_custom_call" | custom-call | tf_op jit(solution)/shard_map/pallas_call | solution.py:336
  133.7 10.8 %all-to-all-start = ((bf16[3,48,1183]{2,1,0:T(8,128)(2,1)}), bf16[3,48,1183]{2,1,0:T(8,128)(2,1)S(1)}, u32[]{:S(2)}, u32[]{:S(2)}) async-start(bf16[3,48,1183]{2,1,0:T(8,128)(2,1)} %bitcast.20), calls=%async_computation | async-start | bytes 737280 | tf_op jit(solution)/shard_map/all_to_all | solution.py:459
  144.6 22.2 %all_gather.6.left = bf16[192,1183]{1,0:T(8,128)(2,1)} all-gather(bf16[48,1183]{1,0:T(8,128)(2,1)} %get-tuple-element.66), channel_id=1, replica_groups={{0,2,4,6},{1,3,5,7},{8,10,12,14},{9,11,13,15},{16,18,20,22},{17,19,21,2..., dimensions={0}, use_global_device_ids=true | all-gather | bytes 567840 | tf_op jit(solution)/shard_map/all_gather | solution.py:456
  166.8 2.5 %all_gather.7.right = bf16[288,1183]{1,0:T(8,128)(2,1)} all-gather(bf16[144,1183]{1,0:T(8,128)(2,1)S(1)} %bitcast.13), channel_id=1, replica_groups={{0,1},{2,3},{4,5},{6,7},{8,9},{10,11},{12,13},{14,15},{16,17},{18,19},{..., dimensions={0}, use_global_device_ids=true | all-gather | bytes 1022112 | tf_op jit(solution)/shard_map/all_gather | solution.py:456
  169.2 2.5 %shard_map.118 = f32[512,128]{1,0:T(8,128)} custom-call(bf16[192,1183]{1,0:T(8,128)(2,1)} %all_gather.6.left, bf16[288,1183]{1,0:T(8,128)(2,1)} %all_gather.7.right), custom_call_target="tpu_custom_call" | custom-call | tf_op jit(solution)/shard_map/pallas_call | solution.py:336
  171.8 20.0 %all_to_all.45 = f32[32,16,128]{2,1,0:T(8,128)} all-to-all(f32[32,16,128]{2,1,0:T(8,128)} %bitcast.19), channel_id=1, replica_groups=mesh['cell'=32,'band'=24] {'cell'}, dimensions={0} | all-to-all | bytes 524288 | tf_op jit(solution)/shard_map/all_to_all | solution.py:465
  191.7 1.7 shard_map.119
  193.4 16.8 %all_to_all.46 = f32[32,16,128]{2,1,0:T(8,128)} all-to-all(f32[32,16,128]{2,1,0:T(8,128)} %bitcast.17), channel_id=1, replica_groups=mesh['cell'=32,'band'=24] {'cell'}, dimensions={0} | all-to-all | bytes 524288 | tf_op jit(solution)/shard_map/all_to_all | solution.py:467
  210.2 1.7 shard_map.120
  212.0 5.2 %all-to-all-start.3 = ((f32[4,48,288]{2,1,0:T(8,128)}), f32[4,48,288]{2,1,0:T(8,128)S(1)}, u32[]{:S(2)}, u32[]{:S(2)}) async-start(f32[4,48,288]{2,1,0:T(8,128)} %bitcast.15), calls=%async_computation.3 | async-start | bytes 589824 | tf_op jit(solution)/shard_map/all_to_all | solution.py:472
  217.1 8.1 %all-to-all-done.3 = f32[4,48,288]{2,1,0:T(8,128)S(1)} async-done(((f32[4,48,288]{2,1,0:T(8,128)}), f32[4,48,288]{2,1,0:T(8,128)S(1)}, u32[]{:S(2)}, u32[]{:S(2)}) %all-to-all-start.3) | async-done | bytes 221216 | tf_op jit(solution)/shard_map/all_to_all | solution.py:472
  225.2 0.7 copy-done
  225.9 1.9 shard_map.121
  (41 shorter events, 0.1 us)
Async XLA Ops:
  5.3 36.8 %collective-permute-start = (f32[56,128]{1,0:T(8,128)}, f32[56,128]{1,0:T(8,128)S(1)}, u32[]{:S(2)}, u32[]{:S(2)}) collective-permute-start(f32[56,128]{1,0:T(8,128)} %get-tuple-element.38.own), channel_id=1, source_target_pairs={{0,24},{24,0},{48,72},{72,48},{96,120},{120,96},{144,168},{168,144... | collective-permute-start | bytes 86024 | tf_op jit(solution)/shard_map/ppermute | solution.py:355
  16.6 25.5 %collective-permute-start.1 = (f32[56,128]{1,0:T(8,128)}, f32[56,128]{1,0:T(8,128)S(1)}, u32[]{:S(2)}, u32[]{:S(2)}) collective-permute-start(f32[56,128]{1,0:T(8,128)} %get-tuple-element.38.own), channel_id=1, source_target_pairs={{0,48},{24,72},{48,0},{72,24},{96,144},{120,168},{144,96},{168,120... | collective-permute-start | bytes 86024 | tf_op jit(solution)/shard_map/ppermute | solution.py:355
  18.6 23.6 %collective-permute-start.2 = (f32[56,128]{1,0:T(8,128)}, f32[56,128]{1,0:T(8,128)S(1)}, u32[]{:S(2)}, u32[]{:S(2)}) collective-permute-start(f32[56,128]{1,0:T(8,128)} %get-tuple-element.38.own), channel_id=1, source_target_pairs={{0,744},{24,48},{48,24},{72,96},{96,72},{120,144},{144,120},{168,1... | collective-permute-start | bytes 86024 | tf_op jit(solution)/shard_map/ppermute | solution.py:355
  21.9 20.2 %collective-permute-start.3 = (f32[56,128]{1,0:T(8,128)}, f32[56,128]{1,0:T(8,128)S(1)}, u32[]{:S(2)}, u32[]{:S(2)}) collective-permute-start(f32[56,128]{1,0:T(8,128)} %get-tuple-element.38.own), channel_id=1, source_target_pairs={{0,720},{24,744},{48,96},{72,120},{96,48},{120,72},{144,192},{168,... | collective-permute-start | bytes 86024 | tf_op jit(solution)/shard_map/ppermute | solution.py:355
  42.1 0.6 copy-start.7
  42.1 0.6 copy-start.8
  42.2 0.6 copy-start.9
  42.2 0.6 copy-start.10
  46.2 9.9 %collective-permute-start.4 = (f32[48,256]{1,0:T(8,128)}, f32[48,256]{1,0:T(8,128)S(1)}, u32[]{:S(2)}, u32[]{:S(2)}) collective-permute-start(f32[48,256]{1,0:T(8,128)} %get-tuple-element.44), channel_id=1, source_target_pairs={{0,24},{24,0},{48,72},{72,48},{96,120},{120,96},{144,168},{168,144... | collective-permute-start | bytes 147464 | tf_op jit(solution)/shard_map/ppermute | solution.py:355
  48.1 8.0 %collective-permute-start.5 = (f32[48,256]{1,0:T(8,128)}, f32[48,256]{1,0:T(8,128)S(1)}, u32[]{:S(2)}, u32[]{:S(2)}) collective-permute-start(f32[48,256]{1,0:T(8,128)} %get-tuple-element.45), channel_id=1, source_target_pairs={{0,744},{24,48},{48,24},{72,96},{96,72},{120,144},{144,120},{168,1... | collective-permute-start | bytes 147464 | tf_op jit(solution)/shard_map/ppermute | solution.py:355
  56.1 0.6 copy-start.3
  56.1 0.6 copy-start.4
  58.5 20.8 %collective-permute-start.6 = (f32[56,128]{1,0:T(8,128)}, f32[56,128]{1,0:T(8,128)S(1)}, u32[]{:S(2)}, u32[]{:S(2)}) collective-permute-start(f32[56,128]{1,0:T(8,128)} %shard_map.110.own), channel_id=1, source_target_pairs={{0,24},{24,0},{48,72},{72,48},{96,120},{120,96},{144,168},{168,144... | collective-permute-start | bytes 86024 | tf_op jit(solution)/shard_map/ppermute | solution.py:355
  63.9 15.4 %collective-permute-start.7 = (f32[56,128]{1,0:T(8,128)}, f32[56,128]{1,0:T(8,128)S(1)}, u32[]{:S(2)}, u32[]{:S(2)}) collective-permute-start(f32[56,128]{1,0:T(8,128)} %shard_map.110.own), channel_id=1, source_target_pairs={{0,48},{24,72},{48,0},{72,24},{96,144},{120,168},{144,96},{168,120... | collective-permute-start | bytes 86024 | tf_op jit(solution)/shard_map/ppermute | solution.py:355
  65.9 13.5 %collective-permute-start.8 = (f32[56,128]{1,0:T(8,128)}, f32[56,128]{1,0:T(8,128)S(1)}, u32[]{:S(2)}, u32[]{:S(2)}) collective-permute-start(f32[56,128]{1,0:T(8,128)} %shard_map.110.own), channel_id=1, source_target_pairs={{0,744},{24,48},{48,24},{72,96},{96,72},{120,144},{144,120},{168,1... | collective-permute-start | bytes 86024 | tf_op jit(solution)/shard_map/ppermute | solution.py:355
  69.2 10.2 %collective-permute-start.9 = (f32[56,128]{1,0:T(8,128)}, f32[56,128]{1,0:T(8,128)S(1)}, u32[]{:S(2)}, u32[]{:S(2)}) collective-permute-start(f32[56,128]{1,0:T(8,128)} %shard_map.110.own), channel_id=1, source_target_pairs={{0,720},{24,744},{48,96},{72,120},{96,48},{120,72},{144,192},{168,... | collective-permute-start | bytes 86024 | tf_op jit(solution)/shard_map/ppermute | solution.py:355
  79.4 0.6 copy-start.13
  79.4 0.6 copy-start.15
  79.4 0.6 copy-start.17
  79.4 0.6 copy-start.18
  83.4 9.7 %collective-permute-start.10 = (f32[48,256]{1,0:T(8,128)}, f32[48,256]{1,0:T(8,128)S(1)}, u32[]{:S(2)}, u32[]{:S(2)}) collective-permute-start(f32[48,256]{1,0:T(8,128)} %get-tuple-element.53), channel_id=1, source_target_pairs={{0,24},{24,0},{48,72},{72,48},{96,120},{120,96},{144,168},{168,144... | collective-permute-start | bytes 147464 | tf_op jit(solution)/shard_map/ppermute | solution.py:355
  86.4 6.7 %collective-permute-start.11 = (f32[48,256]{1,0:T(8,128)}, f32[48,256]{1,0:T(8,128)S(1)}, u32[]{:S(2)}, u32[]{:S(2)}) collective-permute-start(f32[48,256]{1,0:T(8,128)} %get-tuple-element.54), channel_id=1, source_target_pairs={{0,744},{24,48},{48,24},{72,96},{96,72},{120,144},{144,120},{168,1... | collective-permute-start | bytes 147464 | tf_op jit(solution)/shard_map/ppermute | solution.py:355
  93.1 0.6 copy-start.1
  93.1 0.6 copy-start.2
  95.5 20.4 %collective-permute-start.12 = (f32[56,128]{1,0:T(8,128)}, f32[56,128]{1,0:T(8,128)S(1)}, u32[]{:S(2)}, u32[]{:S(2)}) collective-permute-start(f32[56,128]{1,0:T(8,128)} %shard_map.114.own), channel_id=1, source_target_pairs={{0,24},{24,0},{48,72},{72,48},{96,120},{120,96},{144,168},{168,144... | collective-permute-start | bytes 86024 | tf_op jit(solution)/shard_map/ppermute | solution.py:355
  101.2 14.7 %collective-permute-start.13 = (f32[56,128]{1,0:T(8,128)}, f32[56,128]{1,0:T(8,128)S(1)}, u32[]{:S(2)}, u32[]{:S(2)}) collective-permute-start(f32[56,128]{1,0:T(8,128)} %shard_map.114.own), channel_id=1, source_target_pairs={{0,48},{24,72},{48,0},{72,24},{96,144},{120,168},{144,96},{168,120... | collective-permute-start | bytes 86024 | tf_op jit(solution)/shard_map/ppermute | solution.py:355
  103.1 12.8 %collective-permute-start.14 = (f32[56,128]{1,0:T(8,128)}, f32[56,128]{1,0:T(8,128)S(1)}, u32[]{:S(2)}, u32[]{:S(2)}) collective-permute-start(f32[56,128]{1,0:T(8,128)} %shard_map.114.own), channel_id=1, source_target_pairs={{0,744},{24,48},{48,24},{72,96},{96,72},{120,144},{144,120},{168,1... | collective-permute-start | bytes 86024 | tf_op jit(solution)/shard_map/ppermute | solution.py:355
  106.5 10.2 %collective-permute-start.15 = (f32[56,128]{1,0:T(8,128)}, f32[56,128]{1,0:T(8,128)S(1)}, u32[]{:S(2)}, u32[]{:S(2)}) collective-permute-start(f32[56,128]{1,0:T(8,128)} %shard_map.114.own), channel_id=1, source_target_pairs={{0,720},{24,744},{48,96},{72,120},{96,48},{120,72},{144,192},{168,... | collective-permute-start | bytes 86024 | tf_op jit(solution)/shard_map/ppermute | solution.py:355
  115.9 10.5 %copy-start.19 = (f32[1183]{0:T(1024)S(1)}, f32[1183]{0:T(1024)}, u32[]{:S(2)}) copy-start(f32[1183]{0:T(1024)} %param.17) | copy-start | bytes 14200
  115.9 0.8 copy-start.11
  115.9 0.8 copy-start.12
  116.0 0.7 copy-start.14
  116.7 0.6 copy-start.16
  120.7 9.5 %collective-permute-start.16 = (f32[48,256]{1,0:T(8,128)}, f32[48,256]{1,0:T(8,128)S(1)}, u32[]{:S(2)}, u32[]{:S(2)}) collective-permute-start(f32[48,256]{1,0:T(8,128)} %get-tuple-element.61), channel_id=1, source_target_pairs={{0,24},{24,0},{48,72},{72,48},{96,120},{120,96},{144,168},{168,144... | collective-permute-start | bytes 147464 | tf_op jit(solution)/shard_map/ppermute | solution.py:355
  124.3 6.2 %collective-permute-start.17 = (f32[48,256]{1,0:T(8,128)}, f32[48,256]{1,0:T(8,128)S(1)}, u32[]{:S(2)}, u32[]{:S(2)}) collective-permute-start(f32[48,256]{1,0:T(8,128)} %get-tuple-element.62), channel_id=1, source_target_pairs={{0,744},{24,48},{48,24},{72,96},{96,72},{120,144},{144,120},{168,1... | collective-permute-start | bytes 147464 | tf_op jit(solution)/shard_map/ppermute | solution.py:355
  130.2 0.6 copy-start.5
  130.5 0.6 copy-start.6
  133.7 33.0 %all-to-all-start = ((bf16[3,48,1183]{2,1,0:T(8,128)(2,1)}), bf16[3,48,1183]{2,1,0:T(8,128)(2,1)S(1)}, u32[]{:S(2)}, u32[]{:S(2)}) async-start(bf16[3,48,1183]{2,1,0:T(8,128)(2,1)} %bitcast.20), calls=%async_computation | async-start | bytes 737280 | tf_op jit(solution)/shard_map/all_to_all | solution.py:459
  212.0 13.3 %all-to-all-start.3 = ((f32[4,48,288]{2,1,0:T(8,128)}), f32[4,48,288]{2,1,0:T(8,128)S(1)}, u32[]{:S(2)}, u32[]{:S(2)}) async-start(f32[4,48,288]{2,1,0:T(8,128)} %bitcast.15), calls=%async_computation.3 | async-start | bytes 589824 | tf_op jit(solution)/shard_map/all_to_all | solution.py:472
  225.2 0.7 copy-start

commit v4 on v3

--- a/solution.py
+++ b/solution.py
@@ -145,12 +145,10 @@
 def table_kernel(
     node_map, share, parity, matrix, bparts,
     q_out, f_out, s_out, m_out, weight_out, sb_out,
-    ids, face, pad, here, sem,
+    ids, face, pad,
 ):
     ncell, cnodes = node_map.shape
     span = face.shape[1] // 2
-    copy = pltpu.make_async_copy(matrix, here, sem)
-    copy.start()
     id_row = node_row(node_map, ids)
     total = ids.shape[1]
     faces_row = face_row(share, parity, face)
@@ -173,9 +171,8 @@
     for k in range(2):
         sb_out[k] = parts[k]
     pad[...] = jnp.zeros(pad.shape, F32)
-    copy.wait()
     for c in range(ncell):
-        pad[:cnodes, :cnodes] = here[c]
+        pad[:cnodes, :cnodes] = matrix[c]
         parts = split(pad[...])
         for k in range(2):
             m_out[k, c] = parts[k]
@@ -327,9 +324,9 @@
     out[...] = jnp.where(row == col, 0.0, value)
 
 
-def call(body, outs, scratch=(), smem=(), hbm=()):
+def call(body, outs, scratch=(), smem=(), grant=16):
     def run(*args):
-        spaces = {**{k: pltpu.SMEM for k in smem}, **{k: pl.ANY for k in hbm}}
+        spaces = {k: pltpu.SMEM for k in smem}
         specs = [
             pl.BlockSpec(memory_space=spaces.get(k, pltpu.VMEM)) for k in range(len(args))
         ]
@@ -341,6 +338,7 @@
             scratch_shapes=[
                 one if not isinstance(one, tuple) else pltpu.VMEM(*one) for one in scratch
             ],
+            compiler_params=pltpu.CompilerParams(vmem_limit_bytes=grant << 20),
         )(*args)
 
     return run
@@ -396,10 +394,7 @@
             ((8, total), F32),
             ((8, 2 * span), F32),
             ((width, width), F32),
-            ((ncell, cnodes, cnodes), F32),
-            pltpu.SemaphoreType.DMA(()),
         ],
-        hbm=(3,),
     )(node_map, share_list, parity, cell_matrix, parts)
 
     first_scale, later_terms = filter_terms()

time: 229 us -> 193 us (0.84)
  the two profiles are of different devices: /device:TPU:8 before, /device:TPU:10 now
where the time goes in v4:
time: 193 us; the launch traced here: 192 us
  starting transfers between devices  85.2 us (44%)
  blocking collectives  63.4 us (33%)
  Pallas kernels  18.7 us (10%)
  waiting for transfers between devices  17.5 us (9%)
  local copies, waits for them, and re-layouts  5.01 us (3%)
    ppermute x18, starting transfers between devices, swap(): return lax.ppermute(x, 'cell', pairs)  72.7 us
    all_to_all x1, blocking collectives, inner_products(): pieces = lax.all_to_all(partial, 'cell', 0, 0, tiled=True)  25.6 us
    all_gather x2, blocking collectives, gather(): lax.all_gather(x, 'band', axis=0, tiled=True, axis_index_groups=members)  21.6 us
    pallas_call x18, Pallas kernels, run(): pl.pallas_call(body, out_shape=[jax.ShapeDtypeStruct(shape, kind) for sha...  18.7 us
    all_to_all x1, blocking collectives, inner_products(): result = lax.all_to_all(summed, 'cell', 0, 0, tiled=True)  16.2 us
    ppermute x18, waiting for transfers between devices, swap(): return lax.ppermute(x, 'cell', pairs)  9.35 us
    all_to_all x1, starting transfers between devices, inner_products(): lax.all_to_all(copies, 'band', 0, 0, tiled=True, axis_index_groups=across)  9.07 us
    all_to_all x1, waiting for transfers between devices, inner_products(): lax.all_to_all(block, 'band', 0, 0, tiled=True, axis_index_groups=quads)  8.13 us
  transfers between devices with their start and end apart: 20, of which 6 were waited for; matrix products, arithmetic and copies ran while one was open for 1% of the time, Pallas kernels for 6%

profile of v4, /device:TPU:10, one launch (start us, length us, event | category | flops | bytes accessed | tf_op | source)
XLA Modules:
  0.0 191.6 jit_solution(6357927178314053662)
XLA Ops:
  0.6 0.7 select_bitcast_fusion.scales
  1.3 0.9 copy-done
  2.3 0.9 copy-done.1
  3.2 0.7 copy-done.2
  3.9 0.7 copy-done.5
  4.6 1.3 shard_map.104
  5.9 2.4 %collective-permute-start = (f32[56,128]{1,0:T(8,128)S(1)}, f32[56,128]{1,0:T(8,128)S(1)}, u32[]{:S(2)}, u32[]{:S(2)}) collective-permute-start(f32[56,128]{1,0:T(8,128)S(1)} %get-tuple-element.38.own), channel_id=1, source_target_pairs={{0,24},{24,0},{48,72},{72,48},{96,120},{120,96},{144,168},{168,144... | collective-permute-start | bytes 86024 | tf_op jit(solution)/shard_map/ppermute | solution.py:353
  8.3 4.5 %collective-permute-start.1 = (f32[56,128]{1,0:T(8,128)S(1)}, f32[56,128]{1,0:T(8,128)S(1)}, u32[]{:S(2)}, u32[]{:S(2)}) collective-permute-start(f32[56,128]{1,0:T(8,128)S(1)} %get-tuple-element.38.own), channel_id=1, source_target_pairs={{0,48},{24,72},{48,0},{72,24},{96,144},{120,168},{144,96},{168,120... | collective-permute-start | bytes 86024 | tf_op jit(solution)/shard_map/ppermute | solution.py:353
  12.8 2.4 %collective-permute-start.2 = (f32[56,128]{1,0:T(8,128)S(1)}, f32[56,128]{1,0:T(8,128)S(1)}, u32[]{:S(2)}, u32[]{:S(2)}) collective-permute-start(f32[56,128]{1,0:T(8,128)S(1)} %get-tuple-element.38.own), channel_id=1, source_target_pairs={{0,744},{24,48},{48,24},{72,96},{96,72},{120,144},{144,120},{168,1... | collective-permute-start | bytes 86024 | tf_op jit(solution)/shard_map/ppermute | solution.py:353
  15.1 6.6 %collective-permute-start.3 = (f32[56,128]{1,0:T(8,128)S(1)}, f32[56,128]{1,0:T(8,128)S(1)}, u32[]{:S(2)}, u32[]{:S(2)}) collective-permute-start(f32[56,128]{1,0:T(8,128)S(1)} %get-tuple-element.38.own), channel_id=1, source_target_pairs={{0,720},{24,744},{48,96},{72,120},{96,48},{120,72},{144,192},{168,... | collective-permute-start | bytes 86024 | tf_op jit(solution)/shard_map/ppermute | solution.py:353
  21.8 0.0 copy-start.3
  21.8 0.0 copy-start.4
  21.8 1.7 copy.11.matrix
  23.6 3.8 %shard_map.105 = (bf16[1536,1536]{1,0:T(8,128)(2,1)S(1)}, bf16[1536,512]{1,0:T(8,128)(2,1)S(1)}, bf16[512,1536]{1,0:T(8,128)(2,1)S(1)}, bf16[2,4,384,384]{3,2,1,...) custom-call(s32[4,343]{1,0:T(4,128)S(1)} %copy-done.3, s32[1,2,169]{2,1,0:T(2,128)S(1)} %copy-done.4, ...), custom_call_target="tpu_custom_call" | custom-call | tf_op jit(solution)/shard_map/pallas_call | solution.py:333
  27.4 0.9 shard_map.106.o
  28.3 0.0 collective-permute-done.1.m2
  28.3 0.0 collective-permute-done.2.m3
  28.3 0.9 shard_map.107
  29.2 1.9 %collective-permute-start.4 = (f32[48,256]{1,0:T(8,128)S(1)}, f32[48,256]{1,0:T(8,128)S(1)}, u32[]{:S(2)}, u32[]{:S(2)}) collective-permute-start(f32[48,256]{1,0:T(8,128)S(1)} %get-tuple-element.44), channel_id=1, source_target_pairs={{0,24},{24,0},{48,72},{72,48},{96,120},{120,96},{144,168},{168,144... | collective-permute-start | bytes 147464 | tf_op jit(solution)/shard_map/ppermute | solution.py:353
  31.1 3.3 %collective-permute-start.5 = (f32[48,256]{1,0:T(8,128)S(1)}, f32[48,256]{1,0:T(8,128)S(1)}, u32[]{:S(2)}, u32[]{:S(2)}) collective-permute-start(f32[48,256]{1,0:T(8,128)S(1)} %get-tuple-element.45), channel_id=1, source_target_pairs={{0,744},{24,48},{48,24},{72,96},{96,72},{120,144},{144,120},{168,1... | collective-permute-start | bytes 147464 | tf_op jit(solution)/shard_map/ppermute | solution.py:353
  34.4 1.3 shard_map.108
  35.7 0.0 collective-permute-done.4.from_a
  35.8 1.3 collective-permute-done.5.from_b
  37.1 0.2 shard_map.110.own
  37.3 6.0 %collective-permute-start.6 = (f32[56,128]{1,0:T(8,128)S(1)}, f32[56,128]{1,0:T(8,128)S(1)}, u32[]{:S(2)}, u32[]{:S(2)}) collective-permute-start(f32[56,128]{1,0:T(8,128)S(1)} %shard_map.110.own), channel_id=1, source_target_pairs={{0,24},{24,0},{48,72},{72,48},{96,120},{120,96},{144,168},{168,144... | collective-permute-start | bytes 86024 | tf_op jit(solution)/shard_map/ppermute | solution.py:353
  43.3 1.9 %collective-permute-start.7 = (f32[56,128]{1,0:T(8,128)S(1)}, f32[56,128]{1,0:T(8,128)S(1)}, u32[]{:S(2)}, u32[]{:S(2)}) collective-permute-start(f32[56,128]{1,0:T(8,128)S(1)} %shard_map.110.own), channel_id=1, source_target_pairs={{0,48},{24,72},{48,0},{72,24},{96,144},{120,168},{144,96},{168,120... | collective-permute-start | bytes 86024 | tf_op jit(solution)/shard_map/ppermute | solution.py:353
  45.3 3.4 %collective-permute-start.8 = (f32[56,128]{1,0:T(8,128)S(1)}, f32[56,128]{1,0:T(8,128)S(1)}, u32[]{:S(2)}, u32[]{:S(2)}) collective-permute-start(f32[56,128]{1,0:T(8,128)S(1)} %shard_map.110.own), channel_id=1, source_target_pairs={{0,744},{24,48},{48,24},{72,96},{96,72},{120,144},{144,120},{168,1... | collective-permute-start | bytes 86024 | tf_op jit(solution)/shard_map/ppermute | solution.py:353
  48.6 7.8 %collective-permute-start.9 = (f32[56,128]{1,0:T(8,128)S(1)}, f32[56,128]{1,0:T(8,128)S(1)}, u32[]{:S(2)}, u32[]{:S(2)}) collective-permute-start(f32[56,128]{1,0:T(8,128)S(1)} %shard_map.110.own), channel_id=1, source_target_pairs={{0,720},{24,744},{48,96},{72,120},{96,48},{120,72},{144,192},{168,... | collective-permute-start | bytes 86024 | tf_op jit(solution)/shard_map/ppermute | solution.py:353
  56.5 1.1 shard_map.109
  57.6 0.0 collective-permute-done.6.m1
  57.7 0.0 collective-permute-done.7.m2
  57.7 0.6 collective-permute-done.9.m4
  58.3 0.9 shard_map.111
  59.2 7.5 %collective-permute-start.10 = (f32[48,256]{1,0:T(8,128)S(1)}, f32[48,256]{1,0:T(8,128)S(1)}, u32[]{:S(2)}, u32[]{:S(2)}) collective-permute-start(f32[48,256]{1,0:T(8,128)S(1)} %get-tuple-element.53), channel_id=1, source_target_pairs={{0,24},{24,0},{48,72},{72,48},{96,120},{120,96},{144,168},{168,144... | collective-permute-start | bytes 147464 | tf_op jit(solution)/shard_map/ppermute | solution.py:353
  66.7 1.9 %collective-permute-start.11 = (f32[48,256]{1,0:T(8,128)S(1)}, f32[48,256]{1,0:T(8,128)S(1)}, u32[]{:S(2)}, u32[]{:S(2)}) collective-permute-start(f32[48,256]{1,0:T(8,128)S(1)} %get-tuple-element.54), channel_id=1, source_target_pairs={{0,744},{24,48},{48,24},{72,96},{96,72},{120,144},{144,120},{168,1... | collective-permute-start | bytes 147464 | tf_op jit(solution)/shard_map/ppermute | solution.py:353
  68.6 1.3 shard_map.112
  70.0 0.0 collective-permute-done.10.from_a
  70.0 2.7 %collective-permute-done.11.from_b = f32[48,256]{1,0:T(8,128)S(1)} collective-permute-done((f32[48,256]{1,0:T(8,128)S(1)}, f32[48,256]{1,0:T(8,128)S(1)}, u32[]{:S(2)}, u32[]{:S(2)}) %collective-permute-start.11) | collective-permute-done | bytes 49184 | tf_op jit(solution)/shard_map/ppermute | solution.py:353
  72.7 0.2 shard_map.114.own
  72.9 4.0 %collective-permute-start.12 = (f32[56,128]{1,0:T(8,128)S(1)}, f32[56,128]{1,0:T(8,128)S(1)}, u32[]{:S(2)}, u32[]{:S(2)}) collective-permute-start(f32[56,128]{1,0:T(8,128)S(1)} %shard_map.114.own), channel_id=1, source_target_pairs={{0,24},{24,0},{48,72},{72,48},{96,120},{120,96},{144,168},{168,144... | collective-permute-start | bytes 86024 | tf_op jit(solution)/shard_map/ppermute | solution.py:353
  76.9 1.9 %collective-permute-start.13 = (f32[56,128]{1,0:T(8,128)S(1)}, f32[56,128]{1,0:T(8,128)S(1)}, u32[]{:S(2)}, u32[]{:S(2)}) collective-permute-start(f32[56,128]{1,0:T(8,128)S(1)} %shard_map.114.own), channel_id=1, source_target_pairs={{0,48},{24,72},{48,0},{72,24},{96,144},{120,168},{144,96},{168,120... | collective-permute-start | bytes 86024 | tf_op jit(solution)/shard_map/ppermute | solution.py:353
  78.8 3.4 %collective-permute-start.14 = (f32[56,128]{1,0:T(8,128)S(1)}, f32[56,128]{1,0:T(8,128)S(1)}, u32[]{:S(2)}, u32[]{:S(2)}) collective-permute-start(f32[56,128]{1,0:T(8,128)S(1)} %shard_map.114.own), channel_id=1, source_target_pairs={{0,744},{24,48},{48,24},{72,96},{96,72},{120,144},{144,120},{168,1... | collective-permute-start | bytes 86024 | tf_op jit(solution)/shard_map/ppermute | solution.py:353
  82.2 5.5 %collective-permute-start.15 = (f32[56,128]{1,0:T(8,128)S(1)}, f32[56,128]{1,0:T(8,128)S(1)}, u32[]{:S(2)}, u32[]{:S(2)}) collective-permute-start(f32[56,128]{1,0:T(8,128)S(1)} %shard_map.114.own), channel_id=1, source_target_pairs={{0,720},{24,744},{48,96},{72,120},{96,48},{120,72},{144,192},{168,... | collective-permute-start | bytes 86024 | tf_op jit(solution)/shard_map/ppermute | solution.py:353
  87.8 1.1 shard_map.113
  88.9 0.0 copy-start.6
  89.0 2.0 %collective-permute-done.15.m4 = f32[56,128]{1,0:T(8,128)S(1)} collective-permute-done((f32[56,128]{1,0:T(8,128)S(1)}, f32[56,128]{1,0:T(8,128)S(1)}, u32[]{:S(2)}, u32[]{:S(2)}) %collective-permute-start.15) | collective-permute-done | bytes 28704 | tf_op jit(solution)/shard_map/ppermute | solution.py:353
  91.0 0.9 shard_map.115
  91.9 6.1 %collective-permute-start.16 = (f32[48,256]{1,0:T(8,128)S(1)}, f32[48,256]{1,0:T(8,128)S(1)}, u32[]{:S(2)}, u32[]{:S(2)}) collective-permute-start(f32[48,256]{1,0:T(8,128)S(1)} %get-tuple-element.61), channel_id=1, source_target_pairs={{0,24},{24,0},{48,72},{72,48},{96,120},{120,96},{144,168},{168,144... | collective-permute-start | bytes 147464 | tf_op jit(solution)/shard_map/ppermute | solution.py:353
  98.0 2.1 %collective-permute-start.17 = (f32[48,256]{1,0:T(8,128)S(1)}, f32[48,256]{1,0:T(8,128)S(1)}, u32[]{:S(2)}, u32[]{:S(2)}) collective-permute-start(f32[48,256]{1,0:T(8,128)S(1)} %get-tuple-element.62), channel_id=1, source_target_pairs={{0,744},{24,48},{48,24},{72,96},{96,72},{120,144},{144,120},{168,1... | collective-permute-start | bytes 147464 | tf_op jit(solution)/shard_map/ppermute | solution.py:353
  100.1 1.2 shard_map.116
  101.4 0.0 collective-permute-done.16.from_a
  101.4 2.6 %collective-permute-done.17.from_b = f32[48,256]{1,0:T(8,128)S(1)} collective-permute-done((f32[48,256]{1,0:T(8,128)S(1)}, f32[48,256]{1,0:T(8,128)S(1)}, u32[]{:S(2)}, u32[]{:S(2)}) %collective-permute-start.17) | collective-permute-done | bytes 49184 | tf_op jit(solution)/shard_map/ppermute | solution.py:353
  104.0 1.2 shard_map.117
  105.2 9.1 %all-to-all-start = ((bf16[3,48,1183]{2,1,0:T(8,128)(2,1)}), bf16[3,48,1183]{2,1,0:T(8,128)(2,1)S(1)}, u32[]{:S(2)}, u32[]{:S(2)}) async-start(bf16[3,48,1183]{2,1,0:T(8,128)(2,1)} %bitcast.4), calls=%async_computation | async-start | bytes 737280 | tf_op jit(solution)/shard_map/all_to_all | solution.py:454
  114.2 19.2 %all_gather.6.left = bf16[192,1183]{1,0:T(8,128)(2,1)S(1)} all-gather(bf16[48,1183]{1,0:T(8,128)(2,1)S(1)} %get-tuple-element.66), channel_id=1, replica_groups={{0,2,4,6},{1,3,5,7},{8,10,12,14},{9,11,13,15},{16,18,20,22},{17,19,21,2..., dimensions={0}, use_global_device_ids=true | all-gather | bytes 567840 | tf_op jit(solution)/shard_map/all_gather | solution.py:451
  133.5 2.3 %all_gather.7.right = bf16[288,1183]{1,0:T(8,128)(2,1)S(1)} all-gather(bf16[144,1183]{1,0:T(8,128)(2,1)S(1)} %bitcast.19), channel_id=1, replica_groups={{0,1},{2,3},{4,5},{6,7},{8,9},{10,11},{12,13},{14,15},{16,17},{18,19},{..., dimensions={0}, use_global_device_ids=true | all-gather | bytes 1022112 | tf_op jit(solution)/shard_map/all_gather | solution.py:451
  135.8 0.6 shard_map.118
  136.3 25.6 %all_to_all.45 = f32[32,16,128]{2,1,0:T(8,128)S(1)} all-to-all(f32[32,16,128]{2,1,0:T(8,128)S(1)} %bitcast.17), channel_id=1, replica_groups=mesh['cell'=32,'band'=24] {'cell'}, dimensions={0} | all-to-all | bytes 524288 | tf_op jit(solution)/shard_map/all_to_all | solution.py:460
  162.0 0.1 shard_map.119
  162.0 16.2 %all_to_all.46 = f32[32,16,128]{2,1,0:T(8,128)S(1)} all-to-all(f32[32,16,128]{2,1,0:T(8,128)S(1)} %bitcast.15), channel_id=1, replica_groups=mesh['cell'=32,'band'=24] {'cell'}, dimensions={0} | all-to-all | bytes 524288 | tf_op jit(solution)/shard_map/all_to_all | solution.py:462
  178.3 0.8 shard_map.120
  179.1 3.5 %all-to-all-start.3 = ((f32[4,48,288]{2,1,0:T(8,128)}), f32[4,48,288]{2,1,0:T(8,128)S(1)}, u32[]{:S(2)}, u32[]{:S(2)}) async-start(f32[4,48,288]{2,1,0:T(8,128)} %bitcast.10), calls=%async_computation.3 | async-start | bytes 589824 | tf_op jit(solution)/shard_map/all_to_all | solution.py:467
  182.5 8.1 %all-to-all-done.3 = f32[4,48,288]{2,1,0:T(8,128)S(1)} async-done(((f32[4,48,288]{2,1,0:T(8,128)}), f32[4,48,288]{2,1,0:T(8,128)S(1)}, u32[]{:S(2)}, u32[]{:S(2)}) %all-to-all-start.3) | async-done | bytes 221216 | tf_op jit(solution)/shard_map/all_to_all | solution.py:467
  190.7 0.9 shard_map.121
  (15 shorter events, 0.0 us)
Async XLA Ops:
  1.3 0.9 copy-start
  2.3 0.9 copy-start.1
  3.2 0.7 copy-start.2
  3.9 0.7 copy-start.5
  5.9 22.4 %collective-permute-start = (f32[56,128]{1,0:T(8,128)S(1)}, f32[56,128]{1,0:T(8,128)S(1)}, u32[]{:S(2)}, u32[]{:S(2)}) collective-permute-start(f32[56,128]{1,0:T(8,128)S(1)} %get-tuple-element.38.own), channel_id=1, source_target_pairs={{0,24},{24,0},{48,72},{72,48},{96,120},{120,96},{144,168},{168,144... | collective-permute-start | bytes 86024 | tf_op jit(solution)/shard_map/ppermute | solution.py:353
  8.3 20.0 %collective-permute-start.1 = (f32[56,128]{1,0:T(8,128)S(1)}, f32[56,128]{1,0:T(8,128)S(1)}, u32[]{:S(2)}, u32[]{:S(2)}) collective-permute-start(f32[56,128]{1,0:T(8,128)S(1)} %get-tuple-element.38.own), channel_id=1, source_target_pairs={{0,48},{24,72},{48,0},{72,24},{96,144},{120,168},{144,96},{168,120... | collective-permute-start | bytes 86024 | tf_op jit(solution)/shard_map/ppermute | solution.py:353
  12.8 15.5 %collective-permute-start.2 = (f32[56,128]{1,0:T(8,128)S(1)}, f32[56,128]{1,0:T(8,128)S(1)}, u32[]{:S(2)}, u32[]{:S(2)}) collective-permute-start(f32[56,128]{1,0:T(8,128)S(1)} %get-tuple-element.38.own), channel_id=1, source_target_pairs={{0,744},{24,48},{48,24},{72,96},{96,72},{120,144},{144,120},{168,1... | collective-permute-start | bytes 86024 | tf_op jit(solution)/shard_map/ppermute | solution.py:353
  15.1 13.1 %collective-permute-start.3 = (f32[56,128]{1,0:T(8,128)S(1)}, f32[56,128]{1,0:T(8,128)S(1)}, u32[]{:S(2)}, u32[]{:S(2)}) collective-permute-start(f32[56,128]{1,0:T(8,128)S(1)} %get-tuple-element.38.own), channel_id=1, source_target_pairs={{0,720},{24,744},{48,96},{72,120},{96,48},{120,72},{144,192},{168,... | collective-permute-start | bytes 86024 | tf_op jit(solution)/shard_map/ppermute | solution.py:353
  21.8 1.8 copy-start.3
  21.8 1.8 copy-start.4
  29.2 6.6 %collective-permute-start.4 = (f32[48,256]{1,0:T(8,128)S(1)}, f32[48,256]{1,0:T(8,128)S(1)}, u32[]{:S(2)}, u32[]{:S(2)}) collective-permute-start(f32[48,256]{1,0:T(8,128)S(1)} %get-tuple-element.44), channel_id=1, source_target_pairs={{0,24},{24,0},{48,72},{72,48},{96,120},{120,96},{144,168},{168,144... | collective-permute-start | bytes 147464 | tf_op jit(solution)/shard_map/ppermute | solution.py:353
  31.1 6.0 %collective-permute-start.5 = (f32[48,256]{1,0:T(8,128)S(1)}, f32[48,256]{1,0:T(8,128)S(1)}, u32[]{:S(2)}, u32[]{:S(2)}) collective-permute-start(f32[48,256]{1,0:T(8,128)S(1)} %get-tuple-element.45), channel_id=1, source_target_pairs={{0,744},{24,48},{48,24},{72,96},{96,72},{120,144},{144,120},{168,1... | collective-permute-start | bytes 147464 | tf_op jit(solution)/shard_map/ppermute | solution.py:353
  37.3 20.4 %collective-permute-start.6 = (f32[56,128]{1,0:T(8,128)S(1)}, f32[56,128]{1,0:T(8,128)S(1)}, u32[]{:S(2)}, u32[]{:S(2)}) collective-permute-start(f32[56,128]{1,0:T(8,128)S(1)} %shard_map.110.own), channel_id=1, source_target_pairs={{0,24},{24,0},{48,72},{72,48},{96,120},{120,96},{144,168},{168,144... | collective-permute-start | bytes 86024 | tf_op jit(solution)/shard_map/ppermute | solution.py:353
  43.3 14.3 %collective-permute-start.7 = (f32[56,128]{1,0:T(8,128)S(1)}, f32[56,128]{1,0:T(8,128)S(1)}, u32[]{:S(2)}, u32[]{:S(2)}) collective-permute-start(f32[56,128]{1,0:T(8,128)S(1)} %shard_map.110.own), channel_id=1, source_target_pairs={{0,48},{24,72},{48,0},{72,24},{96,144},{120,168},{144,96},{168,120... | collective-permute-start | bytes 86024 | tf_op jit(solution)/shard_map/ppermute | solution.py:353
  45.3 12.4 %collective-permute-start.8 = (f32[56,128]{1,0:T(8,128)S(1)}, f32[56,128]{1,0:T(8,128)S(1)}, u32[]{:S(2)}, u32[]{:S(2)}) collective-permute-start(f32[56,128]{1,0:T(8,128)S(1)} %shard_map.110.own), channel_id=1, source_target_pairs={{0,744},{24,48},{48,24},{72,96},{96,72},{120,144},{144,120},{168,1... | collective-permute-start | bytes 86024 | tf_op jit(solution)/shard_map/ppermute | solution.py:353
  48.6 9.7 %collective-permute-start.9 = (f32[56,128]{1,0:T(8,128)S(1)}, f32[56,128]{1,0:T(8,128)S(1)}, u32[]{:S(2)}, u32[]{:S(2)}) collective-permute-start(f32[56,128]{1,0:T(8,128)S(1)} %shard_map.110.own), channel_id=1, source_target_pairs={{0,720},{24,744},{48,96},{72,120},{96,48},{120,72},{144,192},{168,... | collective-permute-start | bytes 86024 | tf_op jit(solution)/shard_map/ppermute | solution.py:353
  59.2 10.8 %collective-permute-start.10 = (f32[48,256]{1,0:T(8,128)S(1)}, f32[48,256]{1,0:T(8,128)S(1)}, u32[]{:S(2)}, u32[]{:S(2)}) collective-permute-start(f32[48,256]{1,0:T(8,128)S(1)} %get-tuple-element.53), channel_id=1, source_target_pairs={{0,24},{24,0},{48,72},{72,48},{96,120},{120,96},{144,168},{168,144... | collective-permute-start | bytes 147464 | tf_op jit(solution)/shard_map/ppermute | solution.py:353
  66.7 6.0 %collective-permute-start.11 = (f32[48,256]{1,0:T(8,128)S(1)}, f32[48,256]{1,0:T(8,128)S(1)}, u32[]{:S(2)}, u32[]{:S(2)}) collective-permute-start(f32[48,256]{1,0:T(8,128)S(1)} %get-tuple-element.54), channel_id=1, source_target_pairs={{0,744},{24,48},{48,24},{72,96},{96,72},{120,144},{144,120},{168,1... | collective-permute-start | bytes 147464 | tf_op jit(solution)/shard_map/ppermute | solution.py:353
  72.9 16.1 %collective-permute-start.12 = (f32[56,128]{1,0:T(8,128)S(1)}, f32[56,128]{1,0:T(8,128)S(1)}, u32[]{:S(2)}, u32[]{:S(2)}) collective-permute-start(f32[56,128]{1,0:T(8,128)S(1)} %shard_map.114.own), channel_id=1, source_target_pairs={{0,24},{24,0},{48,72},{72,48},{96,120},{120,96},{144,168},{168,144... | collective-permute-start | bytes 86024 | tf_op jit(solution)/shard_map/ppermute | solution.py:353
  76.9 12.0 %collective-permute-start.13 = (f32[56,128]{1,0:T(8,128)S(1)}, f32[56,128]{1,0:T(8,128)S(1)}, u32[]{:S(2)}, u32[]{:S(2)}) collective-permute-start(f32[56,128]{1,0:T(8,128)S(1)} %shard_map.114.own), channel_id=1, source_target_pairs={{0,48},{24,72},{48,0},{72,24},{96,144},{120,168},{144,96},{168,120... | collective-permute-start | bytes 86024 | tf_op jit(solution)/shard_map/ppermute | solution.py:353
  78.8 10.1 %collective-permute-start.14 = (f32[56,128]{1,0:T(8,128)S(1)}, f32[56,128]{1,0:T(8,128)S(1)}, u32[]{:S(2)}, u32[]{:S(2)}) collective-permute-start(f32[56,128]{1,0:T(8,128)S(1)} %shard_map.114.own), channel_id=1, source_target_pairs={{0,744},{24,48},{48,24},{72,96},{96,72},{120,144},{144,120},{168,1... | collective-permute-start | bytes 86024 | tf_op jit(solution)/shard_map/ppermute | solution.py:353
  82.2 8.8 %collective-permute-start.15 = (f32[56,128]{1,0:T(8,128)S(1)}, f32[56,128]{1,0:T(8,128)S(1)}, u32[]{:S(2)}, u32[]{:S(2)}) collective-permute-start(f32[56,128]{1,0:T(8,128)S(1)} %shard_map.114.own), channel_id=1, source_target_pairs={{0,720},{24,744},{48,96},{72,120},{96,48},{120,72},{144,192},{168,... | collective-permute-start | bytes 86024 | tf_op jit(solution)/shard_map/ppermute | solution.py:353
  88.9 11.2 %copy-start.6 = (f32[1183]{0:T(1024)S(1)}, f32[1183]{0:T(1024)}, u32[]{:S(2)}) copy-start(f32[1183]{0:T(1024)} %param.17) | copy-start | bytes 14200
  91.9 9.5 %collective-permute-start.16 = (f32[48,256]{1,0:T(8,128)S(1)}, f32[48,256]{1,0:T(8,128)S(1)}, u32[]{:S(2)}, u32[]{:S(2)}) collective-permute-start(f32[48,256]{1,0:T(8,128)S(1)} %get-tuple-element.61), channel_id=1, source_target_pairs={{0,24},{24,0},{48,72},{72,48},{96,120},{120,96},{144,168},{168,144... | collective-permute-start | bytes 147464 | tf_op jit(solution)/shard_map/ppermute | solution.py:353
  98.0 6.0 %collective-permute-start.17 = (f32[48,256]{1,0:T(8,128)S(1)}, f32[48,256]{1,0:T(8,128)S(1)}, u32[]{:S(2)}, u32[]{:S(2)}) collective-permute-start(f32[48,256]{1,0:T(8,128)S(1)} %get-tuple-element.62), channel_id=1, source_target_pairs={{0,744},{24,48},{48,24},{72,96},{96,72},{120,144},{144,120},{168,1... | collective-permute-start | bytes 147464 | tf_op jit(solution)/shard_map/ppermute | solution.py:353
  105.2 28.3 %all-to-all-start = ((bf16[3,48,1183]{2,1,0:T(8,128)(2,1)}), bf16[3,48,1183]{2,1,0:T(8,128)(2,1)S(1)}, u32[]{:S(2)}, u32[]{:S(2)}) async-start(bf16[3,48,1183]{2,1,0:T(8,128)(2,1)} %bitcast.4), calls=%async_computation | async-start | bytes 737280 | tf_op jit(solution)/shard_map/all_to_all | solution.py:454
  179.1 11.6 %all-to-all-start.3 = ((f32[4,48,288]{2,1,0:T(8,128)}), f32[4,48,288]{2,1,0:T(8,128)S(1)}, u32[]{:S(2)}, u32[]{:S(2)}) async-start(f32[4,48,288]{2,1,0:T(8,128)} %bitcast.10), calls=%async_computation.3 | async-start | bytes 589824 | tf_op jit(solution)/shard_map/all_to_all | solution.py:467

commit v5 on v4

--- a/solution.py
+++ b/solution.py
@@ -14,6 +14,7 @@
 LOWEST = -0.5
 CORES = 2
 CUBE = 8
+SWAPS = ((2, False), (1, False), (2, True), (1, True))
 F32 = jnp.float32
 BF16 = jnp.bfloat16
 
@@ -265,24 +266,32 @@
         copies_out[k * bands : (k + 1) * bands, :] = z
 
 
+def chunk_places(bands, cols):
+    whole = cols // 128
+    places = [(4 * r, 128 * t) for r in range(bands // 4) for t in range(whole)]
+    return whole, places
+
+
 def gram_kernel(bands, left, right, out):
     product = nt(left[...], right[...])
     rows, cols = product.shape
-    whole = cols // 128
-    used = 0
-    for r in range(rows // 8):
-        for c in range(whole):
-            out[used : used + 8, :] = product[8 * r : 8 * r + 8, 128 * c : 128 * c + 128]
-            used += 8
+    owners = rows // bands
+    whole, places = chunk_places(bands, cols)
     rest = cols - 128 * whole
-    owners = rows // bands
-    if rest:
-        out[used : used + bands, :] = jnp.concatenate(
-            [product[k * bands : (k + 1) * bands, 128 * whole :] for k in range(owners)], axis=1
-        )
-        used += bands
-    if used < out.shape[0]:
-        out[used:, :] = jnp.zeros((out.shape[0] - used, 128), F32)
+    out[...] = jnp.zeros(out.shape, F32)
+    height = 4 * owners
+    for k in range(owners):
+        mine = product[k * bands : (k + 1) * bands]
+        chunks = [mine[r : r + 4, t : t + 128] for r, t in places]
+        if rest:
+            fold = 128 // rest
+            tall = bands // fold
+            tail = jnp.concatenate(
+                [mine[n * tall : (n + 1) * tall, 128 * whole :] for n in range(fold)], axis=1
+            )
+            chunks += [tail[r : r + 4] for r in range(0, tall, 4)]
+        for q, chunk in enumerate(chunks):
+            out[q * height + 4 * k : q * height + 4 * k + 4, :] = chunk
 
 
 def sum_kernel(groups, x, out):
@@ -290,35 +299,37 @@
     total = x[0:rows, :]
     for k in range(1, groups):
         total = total + x[k * rows : (k + 1) * rows, :]
-    for k in range(groups):
-        out[k * rows : (k + 1) * rows, :] = total
-
-
-def spread_kernel(bands, scale, x, out):
-    rows, cols = out.shape
-    whole = cols // 128
-    rest = cols - 128 * whole
-    used = 0
-    for r in range(rows // 8):
-        for c in range(whole):
-            out[8 * r : 8 * r + 8, 128 * c : 128 * c + 128] = x[used : used + 8, :] / scale
-            used += 8
-    if rest:
-        last = x[used : used + bands, :] / scale
-        for k in range(rows // bands):
-            out[k * bands : (k + 1) * bands, 128 * whole :] = last[:, k * rest : (k + 1) * rest]
-
-
-def finish_kernel(first_row, x, out):
+    out[...] = total
+
+
+def finish_kernel(wide, scale, first_row, x, out, blocks):
     bands, cols = out.shape
     groups = cols // bands
     cubes = groups // CUBE
-    blocks = []
+    quad = CUBE // CORES
+    height = 4 * quad
+    whole, places = chunk_places(bands, wide)
+    rest = wide - 128 * whole
+    for k in range(quad):
+        for q, (r, t) in enumerate(places):
+            at = q * height + 4 * k
+            blocks[k * bands + r : k * bands + r + 4, t : t + 128] = x[at : at + 4, :]
+        if rest:
+            fold = 128 // rest
+            tall = bands // fold
+            for p in range(tall // 4):
+                at = (len(places) + p) * height + 4 * k
+                for n in range(fold):
+                    row = k * bands + n * tall + 4 * p
+                    blocks[row : row + 4, 128 * whole : wide] = x[
+                        at : at + 4, n * rest : (n + 1) * rest
+                    ]
+    pieces = []
     for g in range(groups):
         cube, place, core = g // CUBE, g % CUBE // CORES, g % CORES
         at = (core * cubes + cube) * bands
-        blocks.append(x[place * bands : (place + 1) * bands, at : at + bands])
-    value = jnp.concatenate(blocks, axis=1)
+        pieces.append(blocks[place * bands : (place + 1) * bands, at : at + bands])
+    value = jnp.concatenate(pieces, axis=1) / scale
     row = lax.broadcasted_iota(jnp.int32, value.shape, 0) + first_row[0, 0]
     col = lax.broadcasted_iota(jnp.int32, value.shape, 1)
     out[...] = jnp.where(row == col, 0.0, value)
@@ -404,7 +415,9 @@
     before = now = x0
     (o,) = call(first_kernel, [block])(x0, m)
     for turn, (lead, back) in enumerate(terms):
-        near = [swap(msg, 1, True), swap(msg, 2, True), swap(msg, 1, False), swap(msg, 2, False)]
+        near = []
+        for stride, inner in SWAPS:
+            near.append(swap(msg, stride, inner))
         if turn:
             x, o = call(functools.partial(cell_kernel, terms[turn - 1][0]), [block, block])(
                 u, from_a, from_b, s, m
@@ -454,19 +467,21 @@
     right = lax.all_to_all(copies, "band", 0, 0, tiled=True, axis_index_groups=across)
     right = gather(right, chips)
     height, wide = left.shape[0], right.shape[0]
-    tiles = (height * wide + 1023) // 1024
-    rows = 8 * up(tiles, count)
-    (partial,) = call(functools.partial(gram_kernel, bands), [((rows, 128), F32)])(left, right)
+    rows = 4 * quad
+    (partial,) = call(functools.partial(gram_kernel, bands), [((count * rows, 128), F32)])(
+        left, right
+    )
     pieces = lax.all_to_all(partial, "cell", 0, 0, tiled=True)
     (summed,) = call(functools.partial(sum_kernel, count), [((rows, 128), F32)])(pieces)
-    result = lax.all_to_all(summed, "cell", 0, 0, tiled=True)
-    (block,) = call(
-        functools.partial(spread_kernel, bands, math.sqrt(count * nodes)),
-        [((height, wide), F32)],
-    )(result)
-    mine = lax.all_to_all(block, "band", 0, 0, tiled=True, axis_index_groups=quads)
+    mine = lax.all_to_all(summed, "band", 0, 0, tiled=True, axis_index_groups=quads)
+    result = lax.all_to_all(jnp.tile(mine, (count, 1)), "cell", 0, 0, tiled=True)
     first_row = jnp.broadcast_to(lax.axis_index("band") * bands, (1, 1)).astype(jnp.int32)
-    (gram,) = call(finish_kernel, [((bands, bands * groups), F32)], smem=(0,))(first_row, mine)
+    (gram,) = call(
+        functools.partial(finish_kernel, wide, math.sqrt(count * nodes)),
+        [((bands, bands * groups), F32)],
+        [((height, up(wide, 128)), F32)],
+        smem=(0,),
+    )(first_row, result)
     return gram
 
 

time: 193 us -> 185 us (0.959)
  the two profiles are of different devices: /device:TPU:10 before, /device:TPU:8 now
where the time goes in v5:
time: 185 us; the launch traced here: 184 us
  starting transfers between devices  89.5 us (48%)
  blocking collectives  51.7 us (28%)
  Pallas kernels  17.9 us (10%)
  waiting for transfers between devices  16.9 us (9%)
  local copies, waits for them, and re-layouts  5.72 us (3%)
    ppermute x18, starting transfers between devices, swap(): return lax.ppermute(x, 'cell', pairs)  74.9 us
    all_gather x2, blocking collectives, gather(): lax.all_gather(x, 'band', axis=0, tiled=True, axis_index_groups=members)  21.5 us
    all_to_all x1, blocking collectives, inner_products(): pieces = lax.all_to_all(partial, 'cell', 0, 0, tiled=True)  20.8 us
    pallas_call x17, Pallas kernels, run(): pl.pallas_call(body, out_shape=[jax.ShapeDtypeStruct(shape, kind) for sha...  17.9 us
    all_to_all x1, waiting for transfers between devices, inner_products(): lax.all_to_all(jnp.tile(mine, (count, 1)), 'cell', 0, 0, tiled=True)  11.1 us
    all_to_all x1, starting transfers between devices, inner_products(): lax.all_to_all(copies, 'band', 0, 0, tiled=True, axis_index_groups=across)  10 us
    all_to_all x1, blocking collectives, inner_products(): lax.all_to_all(summed, 'band', 0, 0, tiled=True, axis_index_groups=quads)  9.33 us
    ppermute x18, waiting for transfers between devices, swap(): return lax.ppermute(x, 'cell', pairs)  5.86 us
  transfers between devices with their start and end apart: 20, of which 6 were waited for; matrix products, arithmetic and copies ran while one was open for 1% of the time, Pallas kernels for 6%

profile of v5, /device:TPU:8, one launch (start us, length us, event | category | flops | bytes accessed | tf_op | source)
XLA Modules:
  0.0 183.5 jit_solution(16003556742353842561)
XLA Ops:
  0.6 0.7 select_bitcast_fusion.scales
  1.3 0.9 copy-done
  2.3 0.9 copy-done.1
  3.2 0.7 copy-done.2
  3.9 0.7 copy-done.5
  4.6 1.3 shard_map.104
  5.9 7.5 %collective-permute-start = (f32[56,128]{1,0:T(8,128)S(1)}, f32[56,128]{1,0:T(8,128)S(1)}, u32[]{:S(2)}, u32[]{:S(2)}) collective-permute-start(f32[56,128]{1,0:T(8,128)S(1)} %get-tuple-element.38.own), channel_id=1, source_target_pairs={{0,720},{24,744},{48,96},{72,120},{96,48},{120,72},{144,192},{168,... | collective-permute-start | bytes 86024 | tf_op jit(solution)/shard_map/ppermute | solution.py:364
  13.4 1.9 %collective-permute-start.1 = (f32[56,128]{1,0:T(8,128)S(1)}, f32[56,128]{1,0:T(8,128)S(1)}, u32[]{:S(2)}, u32[]{:S(2)}) collective-permute-start(f32[56,128]{1,0:T(8,128)S(1)} %get-tuple-element.38.own), channel_id=1, source_target_pairs={{0,744},{24,48},{48,24},{72,96},{96,72},{120,144},{144,120},{168,1... | collective-permute-start | bytes 86024 | tf_op jit(solution)/shard_map/ppermute | solution.py:364
  15.3 2.1 %collective-permute-start.2 = (f32[56,128]{1,0:T(8,128)S(1)}, f32[56,128]{1,0:T(8,128)S(1)}, u32[]{:S(2)}, u32[]{:S(2)}) collective-permute-start(f32[56,128]{1,0:T(8,128)S(1)} %get-tuple-element.38.own), channel_id=1, source_target_pairs={{0,48},{24,72},{48,0},{72,24},{96,144},{120,168},{144,96},{168,120... | collective-permute-start | bytes 86024 | tf_op jit(solution)/shard_map/ppermute | solution.py:364
  17.4 5.7 %collective-permute-start.3 = (f32[56,128]{1,0:T(8,128)S(1)}, f32[56,128]{1,0:T(8,128)S(1)}, u32[]{:S(2)}, u32[]{:S(2)}) collective-permute-start(f32[56,128]{1,0:T(8,128)S(1)} %get-tuple-element.38.own), channel_id=1, source_target_pairs={{0,24},{24,0},{48,72},{72,48},{96,120},{120,96},{144,168},{168,144... | collective-permute-start | bytes 86024 | tf_op jit(solution)/shard_map/ppermute | solution.py:364
  23.1 0.0 copy-start.3
  23.1 0.0 copy-start.4
  23.1 1.7 copy.11.matrix
  24.9 3.8 %shard_map.105 = (bf16[1536,1536]{1,0:T(8,128)(2,1)S(1)}, bf16[1536,512]{1,0:T(8,128)(2,1)S(1)}, bf16[512,1536]{1,0:T(8,128)(2,1)S(1)}, bf16[2,4,384,384]{3,2,1,...) custom-call(s32[4,343]{1,0:T(4,128)S(1)} %copy-done.3, s32[1,2,169]{2,1,0:T(2,128)S(1)} %copy-done.4, ...), custom_call_target="tpu_custom_call" | custom-call | tf_op jit(solution)/shard_map/pallas_call | solution.py:344
  28.7 0.9 shard_map.106.o
  29.6 0.0 collective-permute-done.m1
  29.6 0.0 collective-permute-done.1.m2
  29.6 0.0 collective-permute-done.2.m3
  29.6 0.9 shard_map.107
  30.5 1.9 %collective-permute-start.4 = (f32[48,256]{1,0:T(8,128)S(1)}, f32[48,256]{1,0:T(8,128)S(1)}, u32[]{:S(2)}, u32[]{:S(2)}) collective-permute-start(f32[48,256]{1,0:T(8,128)S(1)} %get-tuple-element.44), channel_id=1, source_target_pairs={{0,24},{24,0},{48,72},{72,48},{96,120},{120,96},{144,168},{168,144... | collective-permute-start | bytes 147464 | tf_op jit(solution)/shard_map/ppermute | solution.py:364
  32.4 5.4 %collective-permute-start.5 = (f32[48,256]{1,0:T(8,128)S(1)}, f32[48,256]{1,0:T(8,128)S(1)}, u32[]{:S(2)}, u32[]{:S(2)}) collective-permute-start(f32[48,256]{1,0:T(8,128)S(1)} %get-tuple-element.45), channel_id=1, source_target_pairs={{0,744},{24,48},{48,24},{72,96},{96,72},{120,144},{144,120},{168,1... | collective-permute-start | bytes 147464 | tf_op jit(solution)/shard_map/ppermute | solution.py:364
  37.8 1.3 shard_map.108
  39.1 0.0 collective-permute-done.4.from_a
  39.2 0.7 collective-permute-done.5.from_b
  39.9 0.2 shard_map.110.own
  40.0 13.5 %collective-permute-start.6 = (f32[56,128]{1,0:T(8,128)S(1)}, f32[56,128]{1,0:T(8,128)S(1)}, u32[]{:S(2)}, u32[]{:S(2)}) collective-permute-start(f32[56,128]{1,0:T(8,128)S(1)} %shard_map.110.own), channel_id=1, source_target_pairs={{0,720},{24,744},{48,96},{72,120},{96,48},{120,72},{144,192},{168,... | collective-permute-start | bytes 86024 | tf_op jit(solution)/shard_map/ppermute | solution.py:364
  53.5 1.9 %collective-permute-start.7 = (f32[56,128]{1,0:T(8,128)S(1)}, f32[56,128]{1,0:T(8,128)S(1)}, u32[]{:S(2)}, u32[]{:S(2)}) collective-permute-start(f32[56,128]{1,0:T(8,128)S(1)} %shard_map.110.own), channel_id=1, source_target_pairs={{0,744},{24,48},{48,24},{72,96},{96,72},{120,144},{144,120},{168,1... | collective-permute-start | bytes 86024 | tf_op jit(solution)/shard_map/ppermute | solution.py:364
  55.4 1.9 %collective-permute-start.8 = (f32[56,128]{1,0:T(8,128)S(1)}, f32[56,128]{1,0:T(8,128)S(1)}, u32[]{:S(2)}, u32[]{:S(2)}) collective-permute-start(f32[56,128]{1,0:T(8,128)S(1)} %shard_map.110.own), channel_id=1, source_target_pairs={{0,48},{24,72},{48,0},{72,24},{96,144},{120,168},{144,96},{168,120... | collective-permute-start | bytes 86024 | tf_op jit(solution)/shard_map/ppermute | solution.py:364
  57.4 5.4 %collective-permute-start.9 = (f32[56,128]{1,0:T(8,128)S(1)}, f32[56,128]{1,0:T(8,128)S(1)}, u32[]{:S(2)}, u32[]{:S(2)}) collective-permute-start(f32[56,128]{1,0:T(8,128)S(1)} %shard_map.110.own), channel_id=1, source_target_pairs={{0,24},{24,0},{48,72},{72,48},{96,120},{120,96},{144,168},{168,144... | collective-permute-start | bytes 86024 | tf_op jit(solution)/shard_map/ppermute | solution.py:364
  62.7 1.1 shard_map.109
  63.9 0.0 collective-permute-done.7.m2
  63.9 0.6 collective-permute-done.9.m4
  64.6 0.9 shard_map.111
  65.5 3.9 %collective-permute-start.10 = (f32[48,256]{1,0:T(8,128)S(1)}, f32[48,256]{1,0:T(8,128)S(1)}, u32[]{:S(2)}, u32[]{:S(2)}) collective-permute-start(f32[48,256]{1,0:T(8,128)S(1)} %get-tuple-element.53), channel_id=1, source_target_pairs={{0,24},{24,0},{48,72},{72,48},{96,120},{120,96},{144,168},{168,144... | collective-permute-start | bytes 147464 | tf_op jit(solution)/shard_map/ppermute | solution.py:364
  69.4 1.9 %collective-permute-start.11 = (f32[48,256]{1,0:T(8,128)S(1)}, f32[48,256]{1,0:T(8,128)S(1)}, u32[]{:S(2)}, u32[]{:S(2)}) collective-permute-start(f32[48,256]{1,0:T(8,128)S(1)} %get-tuple-element.54), channel_id=1, source_target_pairs={{0,744},{24,48},{48,24},{72,96},{96,72},{120,144},{144,120},{168,1... | collective-permute-start | bytes 147464 | tf_op jit(solution)/shard_map/ppermute | solution.py:364
  71.3 1.3 shard_map.112
  72.7 0.0 collective-permute-done.10.from_a
  72.7 2.7 %collective-permute-done.11.from_b = f32[48,256]{1,0:T(8,128)S(1)} collective-permute-done((f32[48,256]{1,0:T(8,128)S(1)}, f32[48,256]{1,0:T(8,128)S(1)}, u32[]{:S(2)}, u32[]{:S(2)}) %collective-permute-start.11) | collective-permute-done | bytes 49184 | tf_op jit(solution)/shard_map/ppermute | solution.py:364
  75.4 0.2 shard_map.114.own
  75.6 5.0 %collective-permute-start.12 = (f32[56,128]{1,0:T(8,128)S(1)}, f32[56,128]{1,0:T(8,128)S(1)}, u32[]{:S(2)}, u32[]{:S(2)}) collective-permute-start(f32[56,128]{1,0:T(8,128)S(1)} %shard_map.114.own), channel_id=1, source_target_pairs={{0,720},{24,744},{48,96},{72,120},{96,48},{120,72},{144,192},{168,... | collective-permute-start | bytes 86024 | tf_op jit(solution)/shard_map/ppermute | solution.py:364
  80.6 1.9 %collective-permute-start.13 = (f32[56,128]{1,0:T(8,128)S(1)}, f32[56,128]{1,0:T(8,128)S(1)}, u32[]{:S(2)}, u32[]{:S(2)}) collective-permute-start(f32[56,128]{1,0:T(8,128)S(1)} %shard_map.114.own), channel_id=1, source_target_pairs={{0,744},{24,48},{48,24},{72,96},{96,72},{120,144},{144,120},{168,1... | collective-permute-start | bytes 86024 | tf_op jit(solution)/shard_map/ppermute | solution.py:364
  82.5 3.0 %collective-permute-start.14 = (f32[56,128]{1,0:T(8,128)S(1)}, f32[56,128]{1,0:T(8,128)S(1)}, u32[]{:S(2)}, u32[]{:S(2)}) collective-permute-start(f32[56,128]{1,0:T(8,128)S(1)} %shard_map.114.own), channel_id=1, source_target_pairs={{0,48},{24,72},{48,0},{72,24},{96,144},{120,168},{144,96},{168,120... | collective-permute-start | bytes 86024 | tf_op jit(solution)/shard_map/ppermute | solution.py:364
  85.5 4.6 %collective-permute-start.15 = (f32[56,128]{1,0:T(8,128)S(1)}, f32[56,128]{1,0:T(8,128)S(1)}, u32[]{:S(2)}, u32[]{:S(2)}) collective-permute-start(f32[56,128]{1,0:T(8,128)S(1)} %shard_map.114.own), channel_id=1, source_target_pairs={{0,24},{24,0},{48,72},{72,48},{96,120},{120,96},{144,168},{168,144... | collective-permute-start | bytes 86024 | tf_op jit(solution)/shard_map/ppermute | solution.py:364
  90.1 1.1 shard_map.113
  91.2 0.0 copy-start.6
  91.2 0.0 collective-permute-done.14.m3
  91.3 0.6 collective-permute-done.15.m4
  91.9 0.9 shard_map.115
  92.8 3.9 %collective-permute-start.16 = (f32[48,256]{1,0:T(8,128)S(1)}, f32[48,256]{1,0:T(8,128)S(1)}, u32[]{:S(2)}, u32[]{:S(2)}) collective-permute-start(f32[48,256]{1,0:T(8,128)S(1)} %get-tuple-element.61), channel_id=1, source_target_pairs={{0,24},{24,0},{48,72},{72,48},{96,120},{120,96},{144,168},{168,144... | collective-permute-start | bytes 147464 | tf_op jit(solution)/shard_map/ppermute | solution.py:364
  96.7 3.5 %collective-permute-start.17 = (f32[48,256]{1,0:T(8,128)S(1)}, f32[48,256]{1,0:T(8,128)S(1)}, u32[]{:S(2)}, u32[]{:S(2)}) collective-permute-start(f32[48,256]{1,0:T(8,128)S(1)} %get-tuple-element.62), channel_id=1, source_target_pairs={{0,744},{24,48},{48,24},{72,96},{96,72},{120,144},{144,120},{168,1... | collective-permute-start | bytes 147464 | tf_op jit(solution)/shard_map/ppermute | solution.py:364
  100.3 1.2 shard_map.116
  101.6 0.0 collective-permute-done.16.from_a
  101.6 1.1 collective-permute-done.17.from_b
  102.7 1.2 shard_map.117
  103.9 10.0 %all-to-all-start = ((bf16[3,48,1183]{2,1,0:T(8,128)(2,1)}), bf16[3,48,1183]{2,1,0:T(8,128)(2,1)S(1)}, u32[]{:S(2)}, u32[]{:S(2)}) async-start(bf16[3,48,1183]{2,1,0:T(8,128)(2,1)} %bitcast.4), calls=%async_computation | async-start | bytes 737280 | tf_op jit(solution)/shard_map/all_to_all | solution.py:467
  113.9 19.2 %all_gather.6.left = bf16[192,1183]{1,0:T(8,128)(2,1)S(1)} all-gather(bf16[48,1183]{1,0:T(8,128)(2,1)S(1)} %get-tuple-element.66), channel_id=1, replica_groups={{0,2,4,6},{1,3,5,7},{8,10,12,14},{9,11,13,15},{16,18,20,22},{17,19,21,2..., dimensions={0}, use_global_device_ids=true | all-gather | bytes 567840 | tf_op jit(solution)/shard_map/all_gather | solution.py:464
  133.1 2.3 %all_gather.7.right = bf16[288,1183]{1,0:T(8,128)(2,1)S(1)} all-gather(bf16[144,1183]{1,0:T(8,128)(2,1)S(1)} %bitcast.17), channel_id=1, replica_groups={{0,1},{2,3},{4,5},{6,7},{8,9},{10,11},{12,13},{14,15},{16,17},{18,19},{..., dimensions={0}, use_global_device_ids=true | all-gather | bytes 1022112 | tf_op jit(solution)/shard_map/all_gather | solution.py:464
  135.5 0.6 shard_map.118
  136.0 20.8 %all_to_all.40 = f32[32,16,128]{2,1,0:T(8,128)S(1)} all-to-all(f32[32,16,128]{2,1,0:T(8,128)S(1)} %bitcast.14), channel_id=1, replica_groups=mesh['cell'=32,'band'=24] {'cell'}, dimensions={0} | all-to-all | bytes 524288 | tf_op jit(solution)/shard_map/all_to_all | solution.py:474
  156.9 9.3 %all_to_all.41 = f32[4,4,128]{2,1,0:T(4,128)S(1)} all-to-all(f32[4,4,128]{2,1,0:T(4,128)S(1)} %bitcast.16), channel_id=1, replica_groups={{0,2,4,6},{1,3,5,7},{8,10,12,14},{9,11,13,15},{16,18,20,22},{17,19,21,2..., dimensions={0} | all-to-all | bytes 16384 | tf_op jit(solution)/shard_map/all_to_all | solution.py:476
  166.2 0.7 tile.10
  166.9 4.6 %all-to-all-start.3 = ((f32[32,16,128]{2,1,0:T(8,128)}), f32[32,16,128]{2,1,0:T(8,128)S(1)}, u32[]{:S(2)}, u32[]{:S(2)}) async-start(f32[32,16,128]{2,1,0:T(8,128)} %tile.10), calls=%async_computation.3 | async-start | bytes 524288 | tf_op jit(solution)/shard_map/all_to_all | solution.py:477
  171.5 11.1 %all-to-all-done.3 = f32[32,16,128]{2,1,0:T(8,128)S(1)} async-done(((f32[32,16,128]{2,1,0:T(8,128)}), f32[32,16,128]{2,1,0:T(8,128)S(1)}, u32[]{:S(2)}, u32[]{:S(2)}) %all-to-all-start.3) | async-done | bytes 262176 | tf_op jit(solution)/shard_map/all_to_all | solution.py:477
  182.6 1.0 shard_map.120
  (15 shorter events, 0.1 us)
Async XLA Ops:
  1.3 0.9 copy-start
  2.3 0.9 copy-start.1
  3.2 0.7 copy-start.2
  3.9 0.7 copy-start.5
  5.9 23.7 %collective-permute-start = (f32[56,128]{1,0:T(8,128)S(1)}, f32[56,128]{1,0:T(8,128)S(1)}, u32[]{:S(2)}, u32[]{:S(2)}) collective-permute-start(f32[56,128]{1,0:T(8,128)S(1)} %get-tuple-element.38.own), channel_id=1, source_target_pairs={{0,720},{24,744},{48,96},{72,120},{96,48},{120,72},{144,192},{168,... | collective-permute-start | bytes 86024 | tf_op jit(solution)/shard_map/ppermute | solution.py:364
  13.4 16.2 %collective-permute-start.1 = (f32[56,128]{1,0:T(8,128)S(1)}, f32[56,128]{1,0:T(8,128)S(1)}, u32[]{:S(2)}, u32[]{:S(2)}) collective-permute-start(f32[56,128]{1,0:T(8,128)S(1)} %get-tuple-element.38.own), channel_id=1, source_target_pairs={{0,744},{24,48},{48,24},{72,96},{96,72},{120,144},{144,120},{168,1... | collective-permute-start | bytes 86024 | tf_op jit(solution)/shard_map/ppermute | solution.py:364
  15.3 14.3 %collective-permute-start.2 = (f32[56,128]{1,0:T(8,128)S(1)}, f32[56,128]{1,0:T(8,128)S(1)}, u32[]{:S(2)}, u32[]{:S(2)}) collective-permute-start(f32[56,128]{1,0:T(8,128)S(1)} %get-tuple-element.38.own), channel_id=1, source_target_pairs={{0,48},{24,72},{48,0},{72,24},{96,144},{120,168},{144,96},{168,120... | collective-permute-start | bytes 86024 | tf_op jit(solution)/shard_map/ppermute | solution.py:364
  17.4 12.2 %collective-permute-start.3 = (f32[56,128]{1,0:T(8,128)S(1)}, f32[56,128]{1,0:T(8,128)S(1)}, u32[]{:S(2)}, u32[]{:S(2)}) collective-permute-start(f32[56,128]{1,0:T(8,128)S(1)} %get-tuple-element.38.own), channel_id=1, source_target_pairs={{0,24},{24,0},{48,72},{72,48},{96,120},{120,96},{144,168},{168,144... | collective-permute-start | bytes 86024 | tf_op jit(solution)/shard_map/ppermute | solution.py:364
  23.1 1.8 copy-start.3
  23.1 1.8 copy-start.4
  30.5 8.7 %collective-permute-start.4 = (f32[48,256]{1,0:T(8,128)S(1)}, f32[48,256]{1,0:T(8,128)S(1)}, u32[]{:S(2)}, u32[]{:S(2)}) collective-permute-start(f32[48,256]{1,0:T(8,128)S(1)} %get-tuple-element.44), channel_id=1, source_target_pairs={{0,24},{24,0},{48,72},{72,48},{96,120},{120,96},{144,168},{168,144... | collective-permute-start | bytes 147464 | tf_op jit(solution)/shard_map/ppermute | solution.py:364
  32.4 7.4 %collective-permute-start.5 = (f32[48,256]{1,0:T(8,128)S(1)}, f32[48,256]{1,0:T(8,128)S(1)}, u32[]{:S(2)}, u32[]{:S(2)}) collective-permute-start(f32[48,256]{1,0:T(8,128)S(1)} %get-tuple-element.45), channel_id=1, source_target_pairs={{0,744},{24,48},{48,24},{72,96},{96,72},{120,144},{144,120},{168,1... | collective-permute-start | bytes 147464 | tf_op jit(solution)/shard_map/ppermute | solution.py:364
  40.0 23.9 %collective-permute-start.6 = (f32[56,128]{1,0:T(8,128)S(1)}, f32[56,128]{1,0:T(8,128)S(1)}, u32[]{:S(2)}, u32[]{:S(2)}) collective-permute-start(f32[56,128]{1,0:T(8,128)S(1)} %shard_map.110.own), channel_id=1, source_target_pairs={{0,720},{24,744},{48,96},{72,120},{96,48},{120,72},{144,192},{168,... | collective-permute-start | bytes 86024 | tf_op jit(solution)/shard_map/ppermute | solution.py:364
  53.5 10.4 %collective-permute-start.7 = (f32[56,128]{1,0:T(8,128)S(1)}, f32[56,128]{1,0:T(8,128)S(1)}, u32[]{:S(2)}, u32[]{:S(2)}) collective-permute-start(f32[56,128]{1,0:T(8,128)S(1)} %shard_map.110.own), channel_id=1, source_target_pairs={{0,744},{24,48},{48,24},{72,96},{96,72},{120,144},{144,120},{168,1... | collective-permute-start | bytes 86024 | tf_op jit(solution)/shard_map/ppermute | solution.py:364
  55.4 8.5 %collective-permute-start.8 = (f32[56,128]{1,0:T(8,128)S(1)}, f32[56,128]{1,0:T(8,128)S(1)}, u32[]{:S(2)}, u32[]{:S(2)}) collective-permute-start(f32[56,128]{1,0:T(8,128)S(1)} %shard_map.110.own), channel_id=1, source_target_pairs={{0,48},{24,72},{48,0},{72,24},{96,144},{120,168},{144,96},{168,120... | collective-permute-start | bytes 86024 | tf_op jit(solution)/shard_map/ppermute | solution.py:364
  57.4 7.2 %collective-permute-start.9 = (f32[56,128]{1,0:T(8,128)S(1)}, f32[56,128]{1,0:T(8,128)S(1)}, u32[]{:S(2)}, u32[]{:S(2)}) collective-permute-start(f32[56,128]{1,0:T(8,128)S(1)} %shard_map.110.own), channel_id=1, source_target_pairs={{0,24},{24,0},{48,72},{72,48},{96,120},{120,96},{144,168},{168,144... | collective-permute-start | bytes 86024 | tf_op jit(solution)/shard_map/ppermute | solution.py:364
  65.5 7.2 %collective-permute-start.10 = (f32[48,256]{1,0:T(8,128)S(1)}, f32[48,256]{1,0:T(8,128)S(1)}, u32[]{:S(2)}, u32[]{:S(2)}) collective-permute-start(f32[48,256]{1,0:T(8,128)S(1)} %get-tuple-element.53), channel_id=1, source_target_pairs={{0,24},{24,0},{48,72},{72,48},{96,120},{120,96},{144,168},{168,144... | collective-permute-start | bytes 147464 | tf_op jit(solution)/shard_map/ppermute | solution.py:364
  69.4 6.0 %collective-permute-start.11 = (f32[48,256]{1,0:T(8,128)S(1)}, f32[48,256]{1,0:T(8,128)S(1)}, u32[]{:S(2)}, u32[]{:S(2)}) collective-permute-start(f32[48,256]{1,0:T(8,128)S(1)} %get-tuple-element.54), channel_id=1, source_target_pairs={{0,744},{24,48},{48,24},{72,96},{96,72},{120,144},{144,120},{168,1... | collective-permute-start | bytes 147464 | tf_op jit(solution)/shard_map/ppermute | solution.py:364
  75.6 15.7 %collective-permute-start.12 = (f32[56,128]{1,0:T(8,128)S(1)}, f32[56,128]{1,0:T(8,128)S(1)}, u32[]{:S(2)}, u32[]{:S(2)}) collective-permute-start(f32[56,128]{1,0:T(8,128)S(1)} %shard_map.114.own), channel_id=1, source_target_pairs={{0,720},{24,744},{48,96},{72,120},{96,48},{120,72},{144,192},{168,... | collective-permute-start | bytes 86024 | tf_op jit(solution)/shard_map/ppermute | solution.py:364
  80.6 10.7 %collective-permute-start.13 = (f32[56,128]{1,0:T(8,128)S(1)}, f32[56,128]{1,0:T(8,128)S(1)}, u32[]{:S(2)}, u32[]{:S(2)}) collective-permute-start(f32[56,128]{1,0:T(8,128)S(1)} %shard_map.114.own), channel_id=1, source_target_pairs={{0,744},{24,48},{48,24},{72,96},{96,72},{120,144},{144,120},{168,1... | collective-permute-start | bytes 86024 | tf_op jit(solution)/shard_map/ppermute | solution.py:364
  82.5 8.7 %collective-permute-start.14 = (f32[56,128]{1,0:T(8,128)S(1)}, f32[56,128]{1,0:T(8,128)S(1)}, u32[]{:S(2)}, u32[]{:S(2)}) collective-permute-start(f32[56,128]{1,0:T(8,128)S(1)} %shard_map.114.own), channel_id=1, source_target_pairs={{0,48},{24,72},{48,0},{72,24},{96,144},{120,168},{144,96},{168,120... | collective-permute-start | bytes 86024 | tf_op jit(solution)/shard_map/ppermute | solution.py:364
  85.5 6.4 %collective-permute-start.15 = (f32[56,128]{1,0:T(8,128)S(1)}, f32[56,128]{1,0:T(8,128)S(1)}, u32[]{:S(2)}, u32[]{:S(2)}) collective-permute-start(f32[56,128]{1,0:T(8,128)S(1)} %shard_map.114.own), channel_id=1, source_target_pairs={{0,24},{24,0},{48,72},{72,48},{96,120},{120,96},{144,168},{168,144... | collective-permute-start | bytes 86024 | tf_op jit(solution)/shard_map/ppermute | solution.py:364
  91.2 9.1 %copy-start.6 = (f32[1183]{0:T(1024)S(1)}, f32[1183]{0:T(1024)}, u32[]{:S(2)}) copy-start(f32[1183]{0:T(1024)} %param.17) | copy-start | bytes 14200
  92.8 8.8 %collective-permute-start.16 = (f32[48,256]{1,0:T(8,128)S(1)}, f32[48,256]{1,0:T(8,128)S(1)}, u32[]{:S(2)}, u32[]{:S(2)}) collective-permute-start(f32[48,256]{1,0:T(8,128)S(1)} %get-tuple-element.61), channel_id=1, source_target_pairs={{0,24},{24,0},{48,72},{72,48},{96,120},{120,96},{144,168},{168,144... | collective-permute-start | bytes 147464 | tf_op jit(solution)/shard_map/ppermute | solution.py:364
  96.7 6.0 %collective-permute-start.17 = (f32[48,256]{1,0:T(8,128)S(1)}, f32[48,256]{1,0:T(8,128)S(1)}, u32[]{:S(2)}, u32[]{:S(2)}) collective-permute-start(f32[48,256]{1,0:T(8,128)S(1)} %get-tuple-element.62), channel_id=1, source_target_pairs={{0,744},{24,48},{48,24},{72,96},{96,72},{120,144},{144,120},{168,1... | collective-permute-start | bytes 147464 | tf_op jit(solution)/shard_map/ppermute | solution.py:364
  103.9 29.3 %all-to-all-start = ((bf16[3,48,1183]{2,1,0:T(8,128)(2,1)}), bf16[3,48,1183]{2,1,0:T(8,128)(2,1)S(1)}, u32[]{:S(2)}, u32[]{:S(2)}) async-start(bf16[3,48,1183]{2,1,0:T(8,128)(2,1)} %bitcast.4), calls=%async_computation | async-start | bytes 737280 | tf_op jit(solution)/shard_map/all_to_all | solution.py:467
  166.9 15.7 %all-to-all-start.3 = ((f32[32,16,128]{2,1,0:T(8,128)}), f32[32,16,128]{2,1,0:T(8,128)S(1)}, u32[]{:S(2)}, u32[]{:S(2)}) async-start(f32[32,16,128]{2,1,0:T(8,128)} %tile.10), calls=%async_computation.3 | async-start | bytes 524288 | tf_op jit(solution)/shard_map/all_to_all | solution.py:477

commit v6 on v5

--- a/solution.py
+++ b/solution.py
@@ -100,7 +100,9 @@
     return face[0:1, :]
 
 
-def enter_kernel(waves, node_map, proj, contacts, scales, x_out, msg_out, parts_out, aux_out, wide, ids, pad):
+def enter_kernel(
+    waves, node_map, proj, contacts, scales, x_out, msg_out, parts_out, aux_out, wide, ids, pad
+):
     _, nodes = waves.shape
     ncell, cnodes = node_map.shape
     slots, flat = scales.shape[0], proj.shape[0]
@@ -143,40 +145,43 @@
     msg_out[...] = message(full(x, parts, nt), atoms)
 
 
-def table_kernel(
-    node_map, share, parity, matrix, bparts,
-    q_out, f_out, s_out, m_out, weight_out, sb_out,
-    ids, face, pad,
-):
+def table_kernel(node_map, share, parity, matrix, f_out, m_out, ids, face, pad):
     ncell, cnodes = node_map.shape
-    span = face.shape[1] // 2
-    id_row = node_row(node_map, ids)
-    total = ids.shape[1]
+    id_column = column(node_row(node_map, ids))
     faces_row = face_row(share, parity, face)
-    id_column = column(id_row)
-    face_column = column(faces_row)
-    for t in range(total // 128):
-        q_out[:, t * 128 : (t + 1) * 128] = hot(id_column == id_row[:, t * 128 : (t + 1) * 128])
-    for t in range(2 * span // 128):
+    for t in range(face.shape[1] // 128):
         f_out[:, t * 128 : (t + 1) * 128] = hot(
             id_column == faces_row[:, t * 128 : (t + 1) * 128]
         )
-    for t in range(total // 128):
-        s_out[:, t * 128 : (t + 1) * 128] = hot(
-            face_column == id_row[:, t * 128 : (t + 1) * 128]
-        )
-    count = nn(jnp.ones((16, total), BF16), q_out[...])
-    weight_out[...] = 1.0 / jnp.maximum(count[0:8], 1.0)
-    table = s_out[...]
-    parts = split(nt(table, bparts[0]) + nt(table, bparts[1]))
-    for k in range(2):
-        sb_out[k] = parts[k]
     pad[...] = jnp.zeros(pad.shape, F32)
     for c in range(ncell):
         pad[:cnodes, :cnodes] = matrix[c]
         parts = split(pad[...])
         for k in range(2):
             m_out[k, c] = parts[k]
+
+
+def inside_first_kernel(
+    lead, o, now, bparts, node_map, share, parity,
+    u_out, c_out, q_out, s_out, sb_out, weight_out,
+    ids, face,
+):
+    id_row = node_row(node_map, ids)
+    total = ids.shape[1]
+    id_column = column(id_row)
+    face_column = column(face_row(share, parity, face))
+    for t in range(total // 128):
+        q_out[:, t * 128 : (t + 1) * 128] = hot(id_column == id_row[:, t * 128 : (t + 1) * 128])
+        s_out[:, t * 128 : (t + 1) * 128] = hot(
+            face_column == id_row[:, t * 128 : (t + 1) * 128]
+        )
+    inside_kernel(lead, 0.0, o, q_out, now, now, bparts, u_out, c_out)
+    table = s_out[...]
+    parts = split(nt(table, bparts[0]) + nt(table, bparts[1]))
+    for k in range(2):
+        sb_out[k] = parts[k]
+    count = nn(jnp.ones((16, total), BF16), q_out[...])
+    weight_out[...] = 1.0 / jnp.maximum(count[0:8], 1.0)
 
 
 def cell_matrices(x, m, o_out):
@@ -346,9 +351,7 @@
             out_shape=[jax.ShapeDtypeStruct(shape, kind) for shape, kind in outs],
             in_specs=specs,
             out_specs=[pl.BlockSpec(memory_space=pltpu.VMEM) for _ in outs],
-            scratch_shapes=[
-                one if not isinstance(one, tuple) else pltpu.VMEM(*one) for one in scratch
-            ],
+            scratch_shapes=[pltpu.VMEM(shape, kind) for shape, kind in scratch],
             compiler_params=pltpu.CompilerParams(vmem_limit_bytes=grant << 20),
         )(*args)
 
@@ -391,22 +394,11 @@
         ],
         [((bands, whole), F32), ((8, total), F32), ((flat, width), F32)],
     )(waves, node_map, proj, contacts, scales)
-    q, f, s, m, weight, sb = call(
+    f, m = call(
         table_kernel,
-        [
-            ((total, total), BF16),
-            ((total, 2 * span), BF16),
-            ((2 * span, total), BF16),
-            ((2, ncell, width, width), BF16),
-            ((8, total), F32),
-            ((2, 2 * span, flat), BF16),
-        ],
-        [
-            ((8, total), F32),
-            ((8, 2 * span), F32),
-            ((width, width), F32),
-        ],
-    )(node_map, share_list, parity, cell_matrix, parts)
+        [((total, 2 * span), BF16), ((2, ncell, width, width), BF16)],
+        [((8, total), F32), ((8, 2 * span), F32), ((width, width), F32)],
+    )(node_map, share_list, parity, cell_matrix)
 
     first_scale, later_terms = filter_terms()
     terms = [(first_scale, 0.0)] + later_terms
@@ -428,10 +420,24 @@
         )
         from_b = swap(to_b, 1, False)
         from_a = swap(to_a, 1, True)
-        if turn < len(terms) - 1:
+        if turn == 0:
+            u, c, q, s, sb, weight = call(
+                functools.partial(inside_first_kernel, lead),
+                [
+                    block,
+                    ((bands, flat), F32),
+                    ((total, total), BF16),
+                    ((2 * span, total), BF16),
+                    ((2, 2 * span, flat), BF16),
+                    ((8, total), F32),
+                ],
+                [((8, total), F32), ((8, 2 * span), F32)],
+            )(o, now, parts, node_map, share_list, parity)
+        elif turn < len(terms) - 1:
             u, c = call(
                 functools.partial(inside_kernel, lead, back), [block, ((bands, flat), F32)]
             )(o, q, now, before, parts)
+        if turn < len(terms) - 1:
             (msg,) = call(functools.partial(send_kernel, lead), [((bands + 8, flat), F32)])(
                 from_a, from_b, sb, c, aux
             )

time: 185 us -> 182 us (0.984)
  starting transfers between devices: 89.5 us -> 87.3 us
  transfers between devices with their start and end apart: 20 -> 20, of which waited for: 6 -> 5; matrix products, arithmetic and copies ran while one was open for 1% -> 1% of each run, Pallas kernels for 6% -> 6%
where the time goes in v6:
time: 182 us; the launch traced here: 181 us
  starting transfers between devices  87.3 us (48%)
  blocking collectives  51.7 us (28%)
  Pallas kernels  17.3 us (10%)
  waiting for transfers between devices  17 us (9%)
  local copies, waits for them, and re-layouts  5.72 us (3%)
    ppermute x18, starting transfers between devices, swap(): return lax.ppermute(x, 'cell', pairs)  73.6 us
    all_gather x2, blocking collectives, gather(): lax.all_gather(x, 'band', axis=0, tiled=True, axis_index_groups=members)  21.8 us
    all_to_all x1, blocking collectives, inner_products(): pieces = lax.all_to_all(partial, 'cell', 0, 0, tiled=True)  20.5 us
    pallas_call x17, Pallas kernels, run(): pl.pallas_call(body, out_shape=[jax.ShapeDtypeStruct(shape, kind) for sha...  17.3 us
    all_to_all x1, waiting for transfers between devices, inner_products(): lax.all_to_all(jnp.tile(mine, (count, 1)), 'cell', 0, 0, tiled=True)  11.1 us
    all_to_all x1, blocking collectives, inner_products(): lax.all_to_all(summed, 'band', 0, 0, tiled=True, axis_index_groups=quads)  9.33 us
    all_to_all x1, starting transfers between devices, inner_products(): lax.all_to_all(copies, 'band', 0, 0, tiled=True, axis_index_groups=across)  9.16 us
    ppermute x18, waiting for transfers between devices, swap(): return lax.ppermute(x, 'cell', pairs)  5.93 us
  transfers between devices with their start and end apart: 20, of which 5 were waited for; matrix products, arithmetic and copies ran while one was open for 1% of the time, Pallas kernels for 6%

profile of v6, /device:TPU:8, one launch (start us, length us, event | category | flops | bytes accessed | tf_op | source)
XLA Modules:
  0.0 180.8 jit_solution(1578816617334836507)
XLA Ops:
  0.6 0.7 select_bitcast_fusion.scales
  1.3 0.9 copy-done
  2.3 0.9 copy-done.1
  3.2 0.7 copy-done.2
  3.9 0.7 copy-done.5
  4.6 1.3 shard_map.104
  5.9 7.5 %collective-permute-start = (f32[56,128]{1,0:T(8,128)S(1)}, f32[56,128]{1,0:T(8,128)S(1)}, u32[]{:S(2)}, u32[]{:S(2)}) collective-permute-start(f32[56,128]{1,0:T(8,128)S(1)} %get-tuple-element.37.own), channel_id=1, source_target_pairs={{0,720},{24,744},{48,96},{72,120},{96,48},{120,72},{144,192},{168,... | collective-permute-start | bytes 86024 | tf_op jit(solution)/shard_map/ppermute | solution.py:367
  13.4 1.9 %collective-permute-start.1 = (f32[56,128]{1,0:T(8,128)S(1)}, f32[56,128]{1,0:T(8,128)S(1)}, u32[]{:S(2)}, u32[]{:S(2)}) collective-permute-start(f32[56,128]{1,0:T(8,128)S(1)} %get-tuple-element.37.own), channel_id=1, source_target_pairs={{0,744},{24,48},{48,24},{72,96},{96,72},{120,144},{144,120},{168,1... | collective-permute-start | bytes 86024 | tf_op jit(solution)/shard_map/ppermute | solution.py:367
  15.3 2.1 %collective-permute-start.2 = (f32[56,128]{1,0:T(8,128)S(1)}, f32[56,128]{1,0:T(8,128)S(1)}, u32[]{:S(2)}, u32[]{:S(2)}) collective-permute-start(f32[56,128]{1,0:T(8,128)S(1)} %get-tuple-element.37.own), channel_id=1, source_target_pairs={{0,48},{24,72},{48,0},{72,24},{96,144},{120,168},{144,96},{168,120... | collective-permute-start | bytes 86024 | tf_op jit(solution)/shard_map/ppermute | solution.py:367
  17.4 5.7 %collective-permute-start.3 = (f32[56,128]{1,0:T(8,128)S(1)}, f32[56,128]{1,0:T(8,128)S(1)}, u32[]{:S(2)}, u32[]{:S(2)}) collective-permute-start(f32[56,128]{1,0:T(8,128)S(1)} %get-tuple-element.37.own), channel_id=1, source_target_pairs={{0,24},{24,0},{48,72},{72,48},{96,120},{120,96},{144,168},{168,144... | collective-permute-start | bytes 86024 | tf_op jit(solution)/shard_map/ppermute | solution.py:367
  23.1 0.0 copy-start.3
  23.1 0.0 copy-start.4
  23.1 1.7 copy.11.matrix
  24.8 1.1 shard_map.105
  25.9 0.9 shard_map.106.o
  26.8 0.0 collective-permute-done.1.m2
  26.8 0.0 collective-permute-done.2.m3
  26.9 0.9 shard_map.107
  27.7 1.9 %collective-permute-start.4 = (f32[48,256]{1,0:T(8,128)S(1)}, f32[48,256]{1,0:T(8,128)S(1)}, u32[]{:S(2)}, u32[]{:S(2)}) collective-permute-start(f32[48,256]{1,0:T(8,128)S(1)} %get-tuple-element.43), channel_id=1, source_target_pairs={{0,24},{24,0},{48,72},{72,48},{96,120},{120,96},{144,168},{168,144... | collective-permute-start | bytes 147464 | tf_op jit(solution)/shard_map/ppermute | solution.py:367
  29.7 5.4 %collective-permute-start.5 = (f32[48,256]{1,0:T(8,128)S(1)}, f32[48,256]{1,0:T(8,128)S(1)}, u32[]{:S(2)}, u32[]{:S(2)}) collective-permute-start(f32[48,256]{1,0:T(8,128)S(1)} %get-tuple-element.44), channel_id=1, source_target_pairs={{0,744},{24,48},{48,24},{72,96},{96,72},{120,144},{144,120},{168,1... | collective-permute-start | bytes 147464 | tf_op jit(solution)/shard_map/ppermute | solution.py:367
  35.1 3.5 %shard_map.108 = (f32[48,1536]{1,0:T(8,128)S(1)}, f32[48,128]{1,0:T(8,128)S(1)}, bf16[1536,1536]{1,0:T(8,128)(2,1)S(1)}, bf16[512,1536]{1,0:T(8,128)(2,1)S(1)}, ...) custom-call(f32[48,1536]{1,0:T(8,128)S(1)} %get-tuple-element.41.o, ...), custom_call_target="tpu_custom_call" | custom-call | tf_op jit(solution)/shard_map/pallas_call | solution.py:349
  38.5 0.0 collective-permute-done.4.from_a
  38.5 0.2 shard_map.110.own
  38.7 12.3 %collective-permute-start.6 = (f32[56,128]{1,0:T(8,128)S(1)}, f32[56,128]{1,0:T(8,128)S(1)}, u32[]{:S(2)}, u32[]{:S(2)}) collective-permute-start(f32[56,128]{1,0:T(8,128)S(1)} %shard_map.110.own), channel_id=1, source_target_pairs={{0,720},{24,744},{48,96},{72,120},{96,48},{120,72},{144,192},{168,... | collective-permute-start | bytes 86024 | tf_op jit(solution)/shard_map/ppermute | solution.py:367
  51.1 1.9 %collective-permute-start.7 = (f32[56,128]{1,0:T(8,128)S(1)}, f32[56,128]{1,0:T(8,128)S(1)}, u32[]{:S(2)}, u32[]{:S(2)}) collective-permute-start(f32[56,128]{1,0:T(8,128)S(1)} %shard_map.110.own), channel_id=1, source_target_pairs={{0,744},{24,48},{48,24},{72,96},{96,72},{120,144},{144,120},{168,1... | collective-permute-start | bytes 86024 | tf_op jit(solution)/shard_map/ppermute | solution.py:367
  53.0 1.9 %collective-permute-start.8 = (f32[56,128]{1,0:T(8,128)S(1)}, f32[56,128]{1,0:T(8,128)S(1)}, u32[]{:S(2)}, u32[]{:S(2)}) collective-permute-start(f32[56,128]{1,0:T(8,128)S(1)} %shard_map.110.own), channel_id=1, source_target_pairs={{0,48},{24,72},{48,0},{72,24},{96,144},{120,168},{144,96},{168,120... | collective-permute-start | bytes 86024 | tf_op jit(solution)/shard_map/ppermute | solution.py:367
  54.9 5.4 %collective-permute-start.9 = (f32[56,128]{1,0:T(8,128)S(1)}, f32[56,128]{1,0:T(8,128)S(1)}, u32[]{:S(2)}, u32[]{:S(2)}) collective-permute-start(f32[56,128]{1,0:T(8,128)S(1)} %shard_map.110.own), channel_id=1, source_target_pairs={{0,24},{24,0},{48,72},{72,48},{96,120},{120,96},{144,168},{168,144... | collective-permute-start | bytes 86024 | tf_op jit(solution)/shard_map/ppermute | solution.py:367
  60.3 1.1 shard_map.109
  61.5 0.0 collective-permute-done.6.m1
  61.5 0.0 collective-permute-done.7.m2
  61.5 0.6 collective-permute-done.9.m4
  62.1 0.9 shard_map.111
  63.0 3.9 %collective-permute-start.10 = (f32[48,256]{1,0:T(8,128)S(1)}, f32[48,256]{1,0:T(8,128)S(1)}, u32[]{:S(2)}, u32[]{:S(2)}) collective-permute-start(f32[48,256]{1,0:T(8,128)S(1)} %get-tuple-element.53), channel_id=1, source_target_pairs={{0,24},{24,0},{48,72},{72,48},{96,120},{120,96},{144,168},{168,144... | collective-permute-start | bytes 147464 | tf_op jit(solution)/shard_map/ppermute | solution.py:367
  67.0 1.9 %collective-permute-start.11 = (f32[48,256]{1,0:T(8,128)S(1)}, f32[48,256]{1,0:T(8,128)S(1)}, u32[]{:S(2)}, u32[]{:S(2)}) collective-permute-start(f32[48,256]{1,0:T(8,128)S(1)} %get-tuple-element.54), channel_id=1, source_target_pairs={{0,744},{24,48},{48,24},{72,96},{96,72},{120,144},{144,120},{168,1... | collective-permute-start | bytes 147464 | tf_op jit(solution)/shard_map/ppermute | solution.py:367
  68.9 1.3 shard_map.112
  70.2 0.0 collective-permute-done.10.from_a
  70.3 2.7 %collective-permute-done.11.from_b = f32[48,256]{1,0:T(8,128)S(1)} collective-permute-done((f32[48,256]{1,0:T(8,128)S(1)}, f32[48,256]{1,0:T(8,128)S(1)}, u32[]{:S(2)}, u32[]{:S(2)}) %collective-permute-start.11) | collective-permute-done | bytes 49184 | tf_op jit(solution)/shard_map/ppermute | solution.py:367
  72.9 0.2 shard_map.114.own
  73.1 5.8 %collective-permute-start.12 = (f32[56,128]{1,0:T(8,128)S(1)}, f32[56,128]{1,0:T(8,128)S(1)}, u32[]{:S(2)}, u32[]{:S(2)}) collective-permute-start(f32[56,128]{1,0:T(8,128)S(1)} %shard_map.114.own), channel_id=1, source_target_pairs={{0,720},{24,744},{48,96},{72,120},{96,48},{120,72},{144,192},{168,... | collective-permute-start | bytes 86024 | tf_op jit(solution)/shard_map/ppermute | solution.py:367
  79.0 1.9 %collective-permute-start.13 = (f32[56,128]{1,0:T(8,128)S(1)}, f32[56,128]{1,0:T(8,128)S(1)}, u32[]{:S(2)}, u32[]{:S(2)}) collective-permute-start(f32[56,128]{1,0:T(8,128)S(1)} %shard_map.114.own), channel_id=1, source_target_pairs={{0,744},{24,48},{48,24},{72,96},{96,72},{120,144},{144,120},{168,1... | collective-permute-start | bytes 86024 | tf_op jit(solution)/shard_map/ppermute | solution.py:367
  80.9 2.1 %collective-permute-start.14 = (f32[56,128]{1,0:T(8,128)S(1)}, f32[56,128]{1,0:T(8,128)S(1)}, u32[]{:S(2)}, u32[]{:S(2)}) collective-permute-start(f32[56,128]{1,0:T(8,128)S(1)} %shard_map.114.own), channel_id=1, source_target_pairs={{0,48},{24,72},{48,0},{72,24},{96,144},{120,168},{144,96},{168,120... | collective-permute-start | bytes 86024 | tf_op jit(solution)/shard_map/ppermute | solution.py:367
  83.0 5.2 %collective-permute-start.15 = (f32[56,128]{1,0:T(8,128)S(1)}, f32[56,128]{1,0:T(8,128)S(1)}, u32[]{:S(2)}, u32[]{:S(2)}) collective-permute-start(f32[56,128]{1,0:T(8,128)S(1)} %shard_map.114.own), channel_id=1, source_target_pairs={{0,24},{24,0},{48,72},{72,48},{96,120},{120,96},{144,168},{168,144... | collective-permute-start | bytes 86024 | tf_op jit(solution)/shard_map/ppermute | solution.py:367
  88.2 1.1 shard_map.113
  89.4 0.0 copy-start.6
  89.4 0.0 collective-permute-done.12.m1
  89.4 0.0 collective-permute-done.13.m2
  89.4 0.6 collective-permute-done.15.m4
  90.0 0.9 shard_map.115
  90.9 3.9 %collective-permute-start.16 = (f32[48,256]{1,0:T(8,128)S(1)}, f32[48,256]{1,0:T(8,128)S(1)}, u32[]{:S(2)}, u32[]{:S(2)}) collective-permute-start(f32[48,256]{1,0:T(8,128)S(1)} %get-tuple-element.61), channel_id=1, source_target_pairs={{0,24},{24,0},{48,72},{72,48},{96,120},{120,96},{144,168},{168,144... | collective-permute-start | bytes 147464 | tf_op jit(solution)/shard_map/ppermute | solution.py:367
  94.9 2.8 %collective-permute-start.17 = (f32[48,256]{1,0:T(8,128)S(1)}, f32[48,256]{1,0:T(8,128)S(1)}, u32[]{:S(2)}, u32[]{:S(2)}) collective-permute-start(f32[48,256]{1,0:T(8,128)S(1)} %get-tuple-element.62), channel_id=1, source_target_pairs={{0,744},{24,48},{48,24},{72,96},{96,72},{120,144},{144,120},{168,1... | collective-permute-start | bytes 147464 | tf_op jit(solution)/shard_map/ppermute | solution.py:367
  97.7 1.2 shard_map.116
  98.9 0.0 collective-permute-done.16.from_a
  98.9 1.9 %collective-permute-done.17.from_b = f32[48,256]{1,0:T(8,128)S(1)} collective-permute-done((f32[48,256]{1,0:T(8,128)S(1)}, f32[48,256]{1,0:T(8,128)S(1)}, u32[]{:S(2)}, u32[]{:S(2)}) %collective-permute-start.17) | collective-permute-done | bytes 49184 | tf_op jit(solution)/shard_map/ppermute | solution.py:367
  100.9 1.2 shard_map.117
  102.0 9.2 %all-to-all-start = ((bf16[3,48,1183]{2,1,0:T(8,128)(2,1)}), bf16[3,48,1183]{2,1,0:T(8,128)(2,1)S(1)}, u32[]{:S(2)}, u32[]{:S(2)}) async-start(bf16[3,48,1183]{2,1,0:T(8,128)(2,1)} %bitcast.4), calls=%async_computation | async-start | bytes 737280 | tf_op jit(solution)/shard_map/all_to_all | solution.py:473
  111.2 19.5 %all_gather.6.left = bf16[192,1183]{1,0:T(8,128)(2,1)S(1)} all-gather(bf16[48,1183]{1,0:T(8,128)(2,1)S(1)} %get-tuple-element.66), channel_id=1, replica_groups={{0,2,4,6},{1,3,5,7},{8,10,12,14},{9,11,13,15},{16,18,20,22},{17,19,21,2..., dimensions={0}, use_global_device_ids=true | all-gather | bytes 567840 | tf_op jit(solution)/shard_map/all_gather | solution.py:470
  130.7 2.3 %all_gather.7.right = bf16[288,1183]{1,0:T(8,128)(2,1)S(1)} all-gather(bf16[144,1183]{1,0:T(8,128)(2,1)S(1)} %bitcast.17), channel_id=1, replica_groups={{0,1},{2,3},{4,5},{6,7},{8,9},{10,11},{12,13},{14,15},{16,17},{18,19},{..., dimensions={0}, use_global_device_ids=true | all-gather | bytes 1022112 | tf_op jit(solution)/shard_map/all_gather | solution.py:470
  133.0 0.6 shard_map.118
  133.6 20.5 %all_to_all.40 = f32[32,16,128]{2,1,0:T(8,128)S(1)} all-to-all(f32[32,16,128]{2,1,0:T(8,128)S(1)} %bitcast.14), channel_id=1, replica_groups=mesh['cell'=32,'band'=24] {'cell'}, dimensions={0} | all-to-all | bytes 524288 | tf_op jit(solution)/shard_map/all_to_all | solution.py:480
  154.2 9.3 %all_to_all.41 = f32[4,4,128]{2,1,0:T(4,128)S(1)} all-to-all(f32[4,4,128]{2,1,0:T(4,128)S(1)} %bitcast.16), channel_id=1, replica_groups={{0,2,4,6},{1,3,5,7},{8,10,12,14},{9,11,13,15},{16,18,20,22},{17,19,21,2..., dimensions={0} | all-to-all | bytes 16384 | tf_op jit(solution)/shard_map/all_to_all | solution.py:482
  163.5 0.7 tile.10
  164.2 4.6 %all-to-all-start.3 = ((f32[32,16,128]{2,1,0:T(8,128)}), f32[32,16,128]{2,1,0:T(8,128)S(1)}, u32[]{:S(2)}, u32[]{:S(2)}) async-start(f32[32,16,128]{2,1,0:T(8,128)} %tile.10), calls=%async_computation.3 | async-start | bytes 524288 | tf_op jit(solution)/shard_map/all_to_all | solution.py:483
  168.8 11.1 %all-to-all-done.3 = f32[32,16,128]{2,1,0:T(8,128)S(1)} async-done(((f32[32,16,128]{2,1,0:T(8,128)}), f32[32,16,128]{2,1,0:T(8,128)S(1)}, u32[]{:S(2)}, u32[]{:S(2)}) %all-to-all-start.3) | async-done | bytes 262176 | tf_op jit(solution)/shard_map/all_to_all | solution.py:483
  179.9 1.0 shard_map.120
  (15 shorter events, 0.1 us)
Async XLA Ops:
  1.3 0.9 copy-start
  2.3 0.9 copy-start.1
  3.2 0.7 copy-start.2
  3.9 0.7 copy-start.5
  5.9 20.9 %collective-permute-start = (f32[56,128]{1,0:T(8,128)S(1)}, f32[56,128]{1,0:T(8,128)S(1)}, u32[]{:S(2)}, u32[]{:S(2)}) collective-permute-start(f32[56,128]{1,0:T(8,128)S(1)} %get-tuple-element.37.own), channel_id=1, source_target_pairs={{0,720},{24,744},{48,96},{72,120},{96,48},{120,72},{144,192},{168,... | collective-permute-start | bytes 86024 | tf_op jit(solution)/shard_map/ppermute | solution.py:367
  13.4 13.5 %collective-permute-start.1 = (f32[56,128]{1,0:T(8,128)S(1)}, f32[56,128]{1,0:T(8,128)S(1)}, u32[]{:S(2)}, u32[]{:S(2)}) collective-permute-start(f32[56,128]{1,0:T(8,128)S(1)} %get-tuple-element.37.own), channel_id=1, source_target_pairs={{0,744},{24,48},{48,24},{72,96},{96,72},{120,144},{144,120},{168,1... | collective-permute-start | bytes 86024 | tf_op jit(solution)/shard_map/ppermute | solution.py:367
  15.3 11.5 %collective-permute-start.2 = (f32[56,128]{1,0:T(8,128)S(1)}, f32[56,128]{1,0:T(8,128)S(1)}, u32[]{:S(2)}, u32[]{:S(2)}) collective-permute-start(f32[56,128]{1,0:T(8,128)S(1)} %get-tuple-element.37.own), channel_id=1, source_target_pairs={{0,48},{24,72},{48,0},{72,24},{96,144},{120,168},{144,96},{168,120... | collective-permute-start | bytes 86024 | tf_op jit(solution)/shard_map/ppermute | solution.py:367
  17.4 9.5 %collective-permute-start.3 = (f32[56,128]{1,0:T(8,128)S(1)}, f32[56,128]{1,0:T(8,128)S(1)}, u32[]{:S(2)}, u32[]{:S(2)}) collective-permute-start(f32[56,128]{1,0:T(8,128)S(1)} %get-tuple-element.37.own), channel_id=1, source_target_pairs={{0,24},{24,0},{48,72},{72,48},{96,120},{120,96},{144,168},{168,144... | collective-permute-start | bytes 86024 | tf_op jit(solution)/shard_map/ppermute | solution.py:367
  23.1 1.8 copy-start.3
  23.1 1.8 copy-start.4
  27.7 10.8 %collective-permute-start.4 = (f32[48,256]{1,0:T(8,128)S(1)}, f32[48,256]{1,0:T(8,128)S(1)}, u32[]{:S(2)}, u32[]{:S(2)}) collective-permute-start(f32[48,256]{1,0:T(8,128)S(1)} %get-tuple-element.43), channel_id=1, source_target_pairs={{0,24},{24,0},{48,72},{72,48},{96,120},{120,96},{144,168},{168,144... | collective-permute-start | bytes 147464 | tf_op jit(solution)/shard_map/ppermute | solution.py:367
  29.7 8.8 %collective-permute-start.5 = (f32[48,256]{1,0:T(8,128)S(1)}, f32[48,256]{1,0:T(8,128)S(1)}, u32[]{:S(2)}, u32[]{:S(2)}) collective-permute-start(f32[48,256]{1,0:T(8,128)S(1)} %get-tuple-element.44), channel_id=1, source_target_pairs={{0,744},{24,48},{48,24},{72,96},{96,72},{120,144},{144,120},{168,1... | collective-permute-start | bytes 147464 | tf_op jit(solution)/shard_map/ppermute | solution.py:367
  38.7 22.7 %collective-permute-start.6 = (f32[56,128]{1,0:T(8,128)S(1)}, f32[56,128]{1,0:T(8,128)S(1)}, u32[]{:S(2)}, u32[]{:S(2)}) collective-permute-start(f32[56,128]{1,0:T(8,128)S(1)} %shard_map.110.own), channel_id=1, source_target_pairs={{0,720},{24,744},{48,96},{72,120},{96,48},{120,72},{144,192},{168,... | collective-permute-start | bytes 86024 | tf_op jit(solution)/shard_map/ppermute | solution.py:367
  51.1 10.4 %collective-permute-start.7 = (f32[56,128]{1,0:T(8,128)S(1)}, f32[56,128]{1,0:T(8,128)S(1)}, u32[]{:S(2)}, u32[]{:S(2)}) collective-permute-start(f32[56,128]{1,0:T(8,128)S(1)} %shard_map.110.own), channel_id=1, source_target_pairs={{0,744},{24,48},{48,24},{72,96},{96,72},{120,144},{144,120},{168,1... | collective-permute-start | bytes 86024 | tf_op jit(solution)/shard_map/ppermute | solution.py:367
  53.0 8.5 %collective-permute-start.8 = (f32[56,128]{1,0:T(8,128)S(1)}, f32[56,128]{1,0:T(8,128)S(1)}, u32[]{:S(2)}, u32[]{:S(2)}) collective-permute-start(f32[56,128]{1,0:T(8,128)S(1)} %shard_map.110.own), channel_id=1, source_target_pairs={{0,48},{24,72},{48,0},{72,24},{96,144},{120,168},{144,96},{168,120... | collective-permute-start | bytes 86024 | tf_op jit(solution)/shard_map/ppermute | solution.py:367
  54.9 7.2 %collective-permute-start.9 = (f32[56,128]{1,0:T(8,128)S(1)}, f32[56,128]{1,0:T(8,128)S(1)}, u32[]{:S(2)}, u32[]{:S(2)}) collective-permute-start(f32[56,128]{1,0:T(8,128)S(1)} %shard_map.110.own), channel_id=1, source_target_pairs={{0,24},{24,0},{48,72},{72,48},{96,120},{120,96},{144,168},{168,144... | collective-permute-start | bytes 86024 | tf_op jit(solution)/shard_map/ppermute | solution.py:367
  63.0 7.2 %collective-permute-start.10 = (f32[48,256]{1,0:T(8,128)S(1)}, f32[48,256]{1,0:T(8,128)S(1)}, u32[]{:S(2)}, u32[]{:S(2)}) collective-permute-start(f32[48,256]{1,0:T(8,128)S(1)} %get-tuple-element.53), channel_id=1, source_target_pairs={{0,24},{24,0},{48,72},{72,48},{96,120},{120,96},{144,168},{168,144... | collective-permute-start | bytes 147464 | tf_op jit(solution)/shard_map/ppermute | solution.py:367
  67.0 6.0 %collective-permute-start.11 = (f32[48,256]{1,0:T(8,128)S(1)}, f32[48,256]{1,0:T(8,128)S(1)}, u32[]{:S(2)}, u32[]{:S(2)}) collective-permute-start(f32[48,256]{1,0:T(8,128)S(1)} %get-tuple-element.54), channel_id=1, source_target_pairs={{0,744},{24,48},{48,24},{72,96},{96,72},{120,144},{144,120},{168,1... | collective-permute-start | bytes 147464 | tf_op jit(solution)/shard_map/ppermute | solution.py:367
  73.1 16.3 %collective-permute-start.12 = (f32[56,128]{1,0:T(8,128)S(1)}, f32[56,128]{1,0:T(8,128)S(1)}, u32[]{:S(2)}, u32[]{:S(2)}) collective-permute-start(f32[56,128]{1,0:T(8,128)S(1)} %shard_map.114.own), channel_id=1, source_target_pairs={{0,720},{24,744},{48,96},{72,120},{96,48},{120,72},{144,192},{168,... | collective-permute-start | bytes 86024 | tf_op jit(solution)/shard_map/ppermute | solution.py:367
  79.0 10.4 %collective-permute-start.13 = (f32[56,128]{1,0:T(8,128)S(1)}, f32[56,128]{1,0:T(8,128)S(1)}, u32[]{:S(2)}, u32[]{:S(2)}) collective-permute-start(f32[56,128]{1,0:T(8,128)S(1)} %shard_map.114.own), channel_id=1, source_target_pairs={{0,744},{24,48},{48,24},{72,96},{96,72},{120,144},{144,120},{168,1... | collective-permute-start | bytes 86024 | tf_op jit(solution)/shard_map/ppermute | solution.py:367
  80.9 8.5 %collective-permute-start.14 = (f32[56,128]{1,0:T(8,128)S(1)}, f32[56,128]{1,0:T(8,128)S(1)}, u32[]{:S(2)}, u32[]{:S(2)}) collective-permute-start(f32[56,128]{1,0:T(8,128)S(1)} %shard_map.114.own), channel_id=1, source_target_pairs={{0,48},{24,72},{48,0},{72,24},{96,144},{120,168},{144,96},{168,120... | collective-permute-start | bytes 86024 | tf_op jit(solution)/shard_map/ppermute | solution.py:367
  83.0 7.0 %collective-permute-start.15 = (f32[56,128]{1,0:T(8,128)S(1)}, f32[56,128]{1,0:T(8,128)S(1)}, u32[]{:S(2)}, u32[]{:S(2)}) collective-permute-start(f32[56,128]{1,0:T(8,128)S(1)} %shard_map.114.own), channel_id=1, source_target_pairs={{0,24},{24,0},{48,72},{72,48},{96,120},{120,96},{144,168},{168,144... | collective-permute-start | bytes 86024 | tf_op jit(solution)/shard_map/ppermute | solution.py:367
  89.4 8.3 %copy-start.6 = (f32[1183]{0:T(1024)S(1)}, f32[1183]{0:T(1024)}, u32[]{:S(2)}) copy-start(f32[1183]{0:T(1024)} %param.17) | copy-start | bytes 14200
  90.9 8.0 %collective-permute-start.16 = (f32[48,256]{1,0:T(8,128)S(1)}, f32[48,256]{1,0:T(8,128)S(1)}, u32[]{:S(2)}, u32[]{:S(2)}) collective-permute-start(f32[48,256]{1,0:T(8,128)S(1)} %get-tuple-element.61), channel_id=1, source_target_pairs={{0,24},{24,0},{48,72},{72,48},{96,120},{120,96},{144,168},{168,144... | collective-permute-start | bytes 147464 | tf_op jit(solution)/shard_map/ppermute | solution.py:367
  94.9 6.0 %collective-permute-start.17 = (f32[48,256]{1,0:T(8,128)S(1)}, f32[48,256]{1,0:T(8,128)S(1)}, u32[]{:S(2)}, u32[]{:S(2)}) collective-permute-start(f32[48,256]{1,0:T(8,128)S(1)} %get-tuple-element.62), channel_id=1, source_target_pairs={{0,744},{24,48},{48,24},{72,96},{96,72},{120,144},{144,120},{168,1... | collective-permute-start | bytes 147464 | tf_op jit(solution)/shard_map/ppermute | solution.py:367
  102.0 28.7 %all-to-all-start = ((bf16[3,48,1183]{2,1,0:T(8,128)(2,1)}), bf16[3,48,1183]{2,1,0:T(8,128)(2,1)S(1)}, u32[]{:S(2)}, u32[]{:S(2)}) async-start(bf16[3,48,1183]{2,1,0:T(8,128)(2,1)} %bitcast.4), calls=%async_computation | async-start | bytes 737280 | tf_op jit(solution)/shard_map/all_to_all | solution.py:473
  164.2 15.7 %all-to-all-start.3 = ((f32[32,16,128]{2,1,0:T(8,128)}), f32[32,16,128]{2,1,0:T(8,128)S(1)}, u32[]{:S(2)}, u32[]{:S(2)}) async-start(f32[32,16,128]{2,1,0:T(8,128)} %tile.10), calls=%async_computation.3 | async-start | bytes 524288 | tf_op jit(solution)/shard_map/all_to_all | solution.py:483
